TPU v7x, 256 devices: a whole 4x4x8 slice. The times are simulated.
256 devices in a mesh: comp: 16 (over z, core), blk: 16 (over x, y).
Axes of the slice: x: 4, y: 4, z: 8, core: 2. Of those that a mesh axis runs over, the one named last changes fastest.
Arguments:
- state_now: float32 [16, 6, 128, 32, 256], P('comp', None, 'blk'), may hold values from -5 to 5
- state_prev: float32 [16, 6, 128, 32, 256], P('comp', None, 'blk'), may hold values from -5 to 5
- viscosity: float32 [16, 128, 32, 256], P('comp', 'blk'), may hold values from 0.05 to 0.5
- jacobian: float32 [16, 3, 6, 6], P('comp'), may hold values from -0.4 to 0.4
- donor_cell: int32 [16, 16, 16, 2, 8, 128], P('comp', 'blk'), may hold values from 0 to 57343, as said below
- interp_weight: float32 [16, 16, 16, 2, 8, 128], P('comp', 'blk'), may hold values from 0 to 1
- recv_cell: int32 [16, 16, 16, 2, 128], P('comp', 'blk'), may hold values from 0 to 57343, as said below
- pair_tiles: int32 [16, 16, 16], P('blk'), may hold values from 0 to 2, as said below
Outputs:
- state_next: float32 [16, 6, 128, 32, 256], P('comp', None, 'blk')
Inputs may be any that keep to these rules, and one draw needn't show every extreme that they name: `donor_cell`: the cells of one donor tile point are the eight corners of a cube of adjacent cells, corner k = 4 i + 2 j + l offset by (i, j, l). `recv_cell`: the receiving cells of one device are all different. `pair_tiles`: for each block index some destination component takes 2 tiles from every source component.
All inputs are finite; a program needn't handle non-finite values.
Results may differ from a plain program's by a relative error of at most 0.0003.
Values sent between devices are 32-bit elements; how exact they have to be, the bound alone decides.
No kernel may reach another device: no remote copies, remote signals or barrier semaphores. Data moves between devices by JAX's collectives and lax.ppermute only.
A program may use at most 128 MiB of HBM per device.

v0:
```python
import jax
import jax.numpy as jnp
from jax import lax
from jax.sharding import PartitionSpec as P

SUBITERS = 2


time_scale = 0.5
pseudo_diag = 2.5


def padded_2(block, sides, width):
    for axis, dim in sides:
        count = lax.axis_size(axis)
        forward = [(i, i + 1) for i in range(count - 1)]
        backward = [(target, source) for source, target in forward]
        low = lax.ppermute(
            lax.slice_in_dim(block, block.shape[dim] - width, None, axis=dim), axis, forward
        )
        high = lax.ppermute(lax.slice_in_dim(block, 0, width, axis=dim), axis, backward)
        block = jnp.concatenate([low, block, high], axis=dim)
    return block


def mix(jac_dim, field):
    return jnp.einsum("vw,wxyz->vxyz", jac_dim, field, precision=lax.Precision.HIGHEST)


def flux(padded, kappa, jac):
    centre = padded[:, 1:-1]
    along_x = (padded[:, 2:] - padded[:, :-2]) * 0.5
    spread = jnp.pad(centre, ((0, 0), (0, 0), (1, 1), (1, 1)))
    along_y = (spread[:, :, 2:, 1:-1] - spread[:, :, :-2, 1:-1]) * 0.5
    along_z = (spread[:, :, 1:-1, 2:] - spread[:, :, 1:-1, :-2]) * 0.5
    beside = padded[:, 2:] + padded[:, :-2] + spread[:, :, 2:, 1:-1] + spread[:, :, :-2, 1:-1]
    beside = beside + spread[:, :, 1:-1, 2:] + spread[:, :, 1:-1, :-2]
    convect = mix(jac[0], along_x) + mix(jac[1], along_y) + mix(jac[2], along_z)
    return convect + kappa * (6.0 * centre - beside)


def relax(rstar, padded_step, kappa, diag, jac):
    centre = padded_step[:, 1:-1]
    return -(rstar + flux(padded_step, kappa, jac) - 6.0 * kappa * centre) / diag


def shards(
    state_now, state_prev, viscosity, jacobian, donor_cell, interp_weight, recv_cell, pair_tiles
):
    now = state_now[0]
    prev = state_prev[0]
    kappa = viscosity[0]
    jac = jacobian[0]
    nvar, rows, width_y, width_z = now.shape
    total_cells = rows * width_y * width_z
    comps = lax.axis_size("comp")
    mine = lax.axis_index("comp")
    slots = donor_cell.shape[3]
    tile = donor_cell.shape[5]
    diag = pseudo_diag + 6.0 * kappa
    live = lax.dynamic_index_in_dim(pair_tiles[0], mine, 1, keepdims=False)
    keep = jnp.arange(slots, dtype=jnp.int32)[None, :] < live[:, None]
    keep = jnp.broadcast_to(keep[:, :, None], (comps, slots, tile)).reshape(-1)
    cells = recv_cell[0, 0].reshape(-1)
    target_cell = jnp.where(keep, cells, total_cells)
    corner_cell = donor_cell[0, 0].reshape(-1)
    weights = interp_weight[0, 0]
    held = lax.all_to_all(weights, "comp", split_axis=0, concat_axis=0, tiled=True)
    state = now
    for sub in range(SUBITERS):
        padded = padded_2(state, (("blk", 1),), 1)
        rstar = time_scale * (3.0 * state - 4.0 * now + prev) + flux(padded, kappa, jac)
        step = -rstar / diag
        for sweep in range(2):
            padded_step = padded_2(step, (("blk", 1),), 1)
            step = relax(rstar, padded_step, kappa, diag, jac)
        state = state + step
        flat = state.reshape(nvar, total_cells)
        values = flat[:, corner_cell].reshape(nvar, comps, slots, 8, tile)
        packed = jnp.einsum("vcskp,cskp->vcsp", values, held, precision=lax.Precision.HIGHEST)
        arrived = lax.all_to_all(packed, "comp", split_axis=1, concat_axis=1, tiled=True)
        incoming = arrived.reshape(nvar, -1)
        flat = flat.at[:, target_cell].set(incoming, mode="drop")
        state = flat.reshape(nvar, rows, width_y, width_z)
    return state[None]


def solution(mesh):
    in_specs = (
        P("comp", None, "blk", None, None),
        P("comp", None, "blk", None, None),
        P("comp", "blk", None, None),
        P("comp", None, None, None),
        P("comp", "blk", None, None, None, None),
        P("comp", "blk", None, None, None, None),
        P("comp", "blk", None, None, None),
        P("blk", None, None),
    )
    out_specs = P("comp", None, "blk", None, None)
    return jax.shard_map(shards, mesh=mesh, in_specs=in_specs, out_specs=out_specs, check_vma=False)
```

profile of v0, /device:TPU:27, one launch (start us, length us, event | category | flops | bytes accessed | tf_op | source)
XLA Modules:
  0.0 560.0 jit_solution(3538027819280823225)
XLA Ops:
  0.0 9.3 %all-to-all-start = ((f32[16,2,8,128]{3,2,1,0:T(8,128)}), f32[16,2,8,128]{3,2,1,0:T(8,128)S(1)}, u32[]{:S(2)}, u32[]{:S(2)}) async-start(f32[16,2,8,128]{3,2,1,0:T(8,128)} %bitcast.167), calls=%async_computation | async-start | bytes 262144 | tf_op jit(solution)/shard_map/all_to_all | solution.py:68
  26.8 7.2 %negate_divide_fusion.1 = (f32[6,8,32,256]{3,0,2,1:T(8,128)S(1)}, f32[6,8,32,256]{3,0,2,1:T(8,128)S(1)}) fusion(f32[8,32,256]{2,1,0:T(8,128)S(1)} %get-tuple-element.18, f32[6,8,32,256]{3,0,2,1:T(8,128)S(1)} %bitcast.147, f32[6,1,32,256]{3,0,2,1:T(8,128)} %collective-permute-done.1, f32[6,1,32,256]{3,0,2,1:T(8,128)} %collective-permute-done, ...), kind=kOutput, calls=%fused_computation.119 | convolution fusion | flops 38141952 | bytes 14683136 | tf_op jit(solution)/shard_map/vw,wxyz->vxyz/dot_general | solution.py:27
  45.2 4.0 collective-permute-done.2
  57.7 3.9 collective-permute-start.4
  67.6 4.9 fusion.14
  72.5 16.8 %copy.60 = f32[6,65536]{0,1:T(8,128)} copy(f32[6,65536]{1,0:T(8,128)S(1)} %bitcast.151) | data formatting | bytes 3145728 | tf_op jit(solution)/shard_map/reshape | solution.py:78
  89.3 118.8 %gather_fusion = f32[32768,6]{1,0:T(8,128)} fusion(f32[6,65536]{0,1:T(8,128)} %copy.60, s32[32768]{0:T(1024)S(1)} %broadcast_clamp_fusion), kind=kCustom, calls=%fused_computation | custom fusion | bytes 1703936 | tf_op jit(solution)/shard_map/gather | solution.py:79
  208.1 7.7 %multiply_reduce_fusion.1 = f32[16,2,128,6]{3,2,1,0:T(8,128)S(1)} fusion(f32[16,2,128,8,6]{4,2,3,1,0:T(8,128)} %bitcast.148, f32[16,2,128,8]{2,3,1,0:T(8,128)S(1)} %bitcast.152), kind=kLoop, calls=%fused_computation.5 | loop fusion | flops 368640 | bytes 1015808
  217.1 9.3 %all-to-all-start.1 = ((f32[6,16,2,128]{3,2,0,1:T(2,128)}), f32[6,16,2,128]{3,2,0,1:T(2,128)S(1)}, u32[]{:S(2)}, u32[]{:S(2)}) async-start(f32[6,16,2,128]{3,2,0,1:T(2,128)} %bitcast.37), calls=%async_computation.1 | async-start | bytes 196608 | tf_op jit(solution)/shard_map/all_to_all | solution.py:81
  226.5 8.4 %all-to-all-done.1 = f32[6,16,2,128]{3,2,0,1:T(2,128)S(1)} async-done(((f32[6,16,2,128]{3,2,0,1:T(2,128)}), f32[6,16,2,128]{3,2,0,1:T(2,128)S(1)}, u32[]{:S(2)}, u32[]{:S(2)}) %all-to-all-start.1) | async-done | bytes 98336 | tf_op jit(solution)/shard_map/all_to_all | solution.py:81
  235.7 32.3 %scatter_fusion = f32[6,65536]{0,1:T(8,128)} fusion(f32[6,65536]{0,1:T(8,128)} %copy.60, s32[4096]{0:T(1024)S(1)} %bitcast.164, f32[4096,6]{1,0:T(8,128)S(1)} %copy.61), kind=kCustom, calls=%fused_computation.2 | custom fusion | bytes 311296 | tf_op jit(solution)/shard_map/scatter | solution.py:83
  268.0 17.8 %copy.70 = f32[6,8,32,256]{3,0,2,1:T(8,128)S(1)} copy(f32[6,8,32,256]{0,3,2,1:T(8,128)} %bitcast.142) | data formatting | bytes 3145728 | tf_op jit(solution)/shard_map/reshape | solution.py:84
  298.4 4.3 collective-permute-done.6
  302.8 5.8 %negate_divide_fusion = (f32[6,8,32,256]{3,0,2,1:T(8,128)S(1)}, f32[6,8,32,256]{3,0,2,1:T(8,128)S(1)}) fusion(f32[8,32,256]{2,1,0:T(8,128)S(1)} %get-tuple-element.18, f32[6,8,32,256]{3,0,2,1:T(8,128)S(1)} %copy.70, f32[6,1,32,256]{3,0,2,1:T(8,128)S(1)} %collective-permute-done.7, f32[6,1,32,256]{3,0,2,1:T(8,128)S(1)} %collective-permute-done.6, ...), kind=kOutput, calls=%fused_computation.91 | convolution fusion | flops 38141952 | bytes 16256000 | tf_op jit(solution)/shard_map/vw,wxyz->vxyz/dot_general | solution.py:27
  320.3 4.0 collective-permute-done.8
  324.3 4.2 fusion.8
  339.3 4.0 collective-permute-done.10
  343.4 5.8 %fusion.4 = f32[6,8,32,256]{3,0,2,1:T(8,128)} fusion(f32[6,8,32,256]{3,0,2,1:T(8,128)S(1)} %copy.70, f32[6,8,32,256]{3,0,2,1:T(8,128)S(1)} %get-tuple-element.25, f32[6,8,32,256]{3,0,2,1:T(8,128)S(1)} %fusion.8, f32[8,32,256,6]{2,3,1,0:T(8,128)S(1)} %fusion.22, f32[8,32,256,6]{2,3,1,0:T(8,128)S(1)} %fusion.25, ...), kind=kOutput, calls=%fused_computation.47 | convolution fusion | flops 37355520 | bytes 15993856 | tf_op jit(solution)/shard_map/vw,wxyz->vxyz/dot_general | solution.py:27
  349.2 16.4 %copy.73 = f32[6,65536]{0,1:T(8,128)} copy(f32[6,65536]{1,0:T(8,128)} %bitcast.150) | data formatting | bytes 3145728 | tf_op jit(solution)/shard_map/reshape | solution.py:78
  365.6 118.8 %gather_fusion.1 = f32[32768,6]{1,0:T(8,128)} fusion(f32[6,65536]{0,1:T(8,128)} %copy.73, s32[32768]{0:T(1024)S(1)} %broadcast_clamp_fusion), kind=kCustom, calls=%fused_computation.1 | custom fusion | bytes 1703936 | tf_op jit(solution)/shard_map/gather | solution.py:79
  484.4 7.7 %multiply_reduce_fusion = f32[16,2,128,6]{3,2,1,0:T(8,128)S(1)} fusion(f32[16,2,128,8,6]{4,2,3,1,0:T(8,128)} %bitcast.149, f32[16,2,128,8]{2,3,1,0:T(8,128)S(1)} %bitcast.153), kind=kLoop, calls=%fused_computation.4 | loop fusion | flops 368640 | bytes 1015808
  492.7 13.4 %all_to_all.15 = f32[6,16,2,128]{3,2,0,1:T(2,128)S(1)} all-to-all(f32[6,16,2,128]{3,2,0,1:T(2,128)S(1)} %bitcast.157), channel_id=1, replica_groups=mesh['comp'=16,'blk'=16] {'comp'}, dimensions={1} | all-to-all | bytes 196608 | tf_op jit(solution)/shard_map/all_to_all | solution.py:81
  506.9 32.2 %scatter_fusion.1 = f32[6,65536]{0,1:T(8,128)} fusion(f32[6,65536]{0,1:T(8,128)} %copy.73, s32[4096]{0:T(1024)S(1)} %bitcast.165, f32[4096,6]{1,0:T(8,128)S(1)} %copy.74), kind=kCustom, calls=%fused_computation.3 | custom fusion | bytes 311296 | tf_op jit(solution)/shard_map/scatter | solution.py:83
  539.1 20.5 %copy.75 = f32[1,6,8,32,256]{4,3,2,1,0:T(8,128)} copy(f32[1,6,8,32,256]{1,4,3,2,0:T(8,128)} %bitcast.143) | data formatting | bytes 3145728 | tf_op jit(solution)/shard_map/broadcast_in_dim;reshape | solution.py:85
  (77 shorter events, 81.4 us)
Async XLA Ops:
  0.0 17.7 %copy-start = (s32[1,16,16]{2,1,0:T(8,128)S(1)}, s32[1,16,16]{2,1,0:T(8,128)}, u32[]{:S(2)}) copy-start(s32[1,16,16]{2,1,0:T(8,128)} %param.15) | copy-start | bytes 3076
  0.0 208.1 %all-to-all-start = ((f32[16,2,8,128]{3,2,1,0:T(8,128)}), f32[16,2,8,128]{3,2,1,0:T(8,128)S(1)}, u32[]{:S(2)}, u32[]{:S(2)}) async-start(f32[16,2,8,128]{3,2,1,0:T(8,128)} %bitcast.167), calls=%async_computation | async-start | bytes 262144 | tf_op jit(solution)/shard_map/all_to_all | solution.py:68
  9.3 8.8 %copy-start.7 = (f32[1,3,6,6]{3,0,2,1:T(1,128)S(1)}, f32[1,3,6,6]{3,0,2,1:T(1,128)}, u32[]{:S(2)}) copy-start(f32[1,3,6,6]{3,0,2,1:T(1,128)} %param.11) | copy-start | bytes 1300
  9.3 8.8 %copy-start.5 = (s32[1,1,16,2,8,128]{5,4,3,2,1,0:T(8,128)S(1)}, s32[1,1,16,2,8,128]{5,4,3,2,1,0:T(8,128)}, u32[]{:S(2)}) copy-start(s32[1,1,16,2,8,128]{5,4,3,2,1,0:T(8,128)} %param.12) | copy-start | bytes 393220
  12.4 10.7 %collective-permute-start.1 = (f32[6,1,32,256]{3,0,2,1:T(8,128)}, f32[6,1,32,256]{3,0,2,1:T(8,128)}, u32[]{:S(2)}, u32[]{:S(2)}) collective-permute-start(f32[6,1,32,256]{3,0,2,1:T(8,128)} %get-tuple-element.15), channel_id=1, source_target_pairs={{0,1},{1,2},{2,3},{3,4},{4,5},{5,6},{6,7},{7,8},{8,9},{9,10},{10,1... | collective-permute-start | bytes 589832 | tf_op jit(solution)/shard_map/ppermute | solution.py:18
  15.2 11.6 %collective-permute-start = (f32[6,1,32,256]{3,0,2,1:T(8,128)S(1)}, f32[6,1,32,256]{3,0,2,1:T(8,128)}, u32[]{:S(2)}, u32[]{:S(2)}) collective-permute-start(f32[6,1,32,256]{3,0,2,1:T(8,128)S(1)} %get-tuple-element.16), channel_id=1, source_target_pairs={{1,0},{2,1},{3,2},{4,3},{5,4},{6,5},{7,6},{8,7},{9,8},{10,9},{11,1... | collective-permute-start | bytes 589832 | tf_op jit(solution)/shard_map/ppermute | solution.py:21
  21.0 2.1 copy-start.4
  21.0 5.9 %copy-start.8 = (f32[1,6,8,32,256]{4,3,2,1,0:T(8,128)S(1)}, f32[1,6,8,32,256]{4,3,2,1,0:T(8,128)}, u32[]{:S(2)}) copy-start(f32[1,6,8,32,256]{4,3,2,1,0:T(8,128)} %param.9) | copy-start | bytes 4718596
  36.7 8.5 %collective-permute-start.3 = (f32[6,1,32,256]{3,0,2,1:T(8,128)S(1)}, f32[6,1,32,256]{3,0,2,1:T(8,128)S(1)}, u32[]{:S(2)}, u32[]{:S(2)}) collective-permute-start(f32[6,1,32,256]{3,0,2,1:T(8,128)S(1)} %get-tuple-element.13), channel_id=1, source_target_pairs={{0,1},{1,2},{2,3},{3,4},{4,5},{5,6},{6,7},{7,8},{8,9},{9,10},{10,1... | collective-permute-start | bytes 589832 | tf_op jit(solution)/shard_map/ppermute | solution.py:18
  38.6 10.6 %collective-permute-start.2 = (f32[6,1,32,256]{3,0,2,1:T(8,128)S(1)}, f32[6,1,32,256]{3,0,2,1:T(8,128)S(1)}, u32[]{:S(2)}, u32[]{:S(2)}) collective-permute-start(f32[6,1,32,256]{3,0,2,1:T(8,128)S(1)} %get-tuple-element.14), channel_id=1, source_target_pairs={{1,0},{2,1},{3,2},{4,3},{5,4},{6,5},{7,6},{8,7},{9,8},{10,9},{11,1... | collective-permute-start | bytes 589832 | tf_op jit(solution)/shard_map/ppermute | solution.py:21
  55.8 7.9 %collective-permute-start.5 = (f32[6,1,32,256]{3,0,2,1:T(8,128)S(1)}, f32[6,1,32,256]{3,0,2,1:T(8,128)S(1)}, u32[]{:S(2)}, u32[]{:S(2)}) collective-permute-start(f32[6,1,32,256]{3,0,2,1:T(8,128)S(1)} %get-tuple-element.11), channel_id=1, source_target_pairs={{0,1},{1,2},{2,3},{3,4},{4,5},{5,6},{6,7},{7,8},{8,9},{9,10},{10,1... | collective-permute-start | bytes 589832 | tf_op jit(solution)/shard_map/ppermute | solution.py:18
  57.7 9.8 %copy-start.2 = (f32[1,6,8,32,256]{4,3,2,1,0:T(8,128)S(1)}, f32[1,6,8,32,256]{4,3,2,1,0:T(8,128)}, u32[]{:S(2)}) copy-start(f32[1,6,8,32,256]{4,3,2,1,0:T(8,128)} %param.8) | copy-start | bytes 4718596
  57.7 9.8 %collective-permute-start.4 = (f32[6,1,32,256]{3,0,2,1:T(8,128)S(1)}, f32[6,1,32,256]{3,0,2,1:T(8,128)S(1)}, u32[]{:S(2)}, u32[]{:S(2)}) collective-permute-start(f32[6,1,32,256]{3,0,2,1:T(8,128)S(1)} %get-tuple-element.12), channel_id=1, source_target_pairs={{1,0},{2,1},{3,2},{4,3},{5,4},{6,5},{7,6},{8,7},{9,8},{10,9},{11,1... | collective-permute-start | bytes 589832 | tf_op jit(solution)/shard_map/ppermute | solution.py:21
  215.8 10.6 %copy-start.6 = (s32[1,1,16,2,128]{4,3,2,1,0:T(2,128)S(1)}, s32[1,1,16,2,128]{4,3,2,1,0:T(2,128)}, u32[]{:S(2)}) copy-start(s32[1,1,16,2,128]{4,3,2,1,0:T(2,128)} %param.14) | copy-start | bytes 49156
  217.1 17.8 %all-to-all-start.1 = ((f32[6,16,2,128]{3,2,0,1:T(2,128)}), f32[6,16,2,128]{3,2,0,1:T(2,128)S(1)}, u32[]{:S(2)}, u32[]{:S(2)}) async-start(f32[6,16,2,128]{3,2,0,1:T(2,128)} %bitcast.37), calls=%async_computation.1 | async-start | bytes 196608 | tf_op jit(solution)/shard_map/all_to_all | solution.py:81
  288.5 9.9 %collective-permute-start.7 = (f32[6,1,32,256]{3,0,2,1:T(8,128)S(1)}, f32[6,1,32,256]{3,0,2,1:T(8,128)S(1)}, u32[]{:S(2)}, u32[]{:S(2)}) collective-permute-start(f32[6,1,32,256]{3,0,2,1:T(8,128)S(1)} %get-tuple-element.9), channel_id=1, source_target_pairs={{0,1},{1,2},{2,3},{3,4},{4,5},{5,6},{6,7},{7,8},{8,9},{9,10},{10,1... | collective-permute-start | bytes 589832 | tf_op jit(solution)/shard_map/ppermute | solution.py:18
  290.4 12.3 %copy-start.3 = (f32[1,6,8,32,256]{4,3,2,1,0:T(8,128)S(1)}, f32[1,6,8,32,256]{4,3,2,1,0:T(8,128)}, u32[]{:S(2)}) copy-start(f32[1,6,8,32,256]{4,3,2,1,0:T(8,128)} %param.8) | copy-start | bytes 4718596
  290.4 12.3 %copy-start.9 = (f32[1,6,8,32,256]{4,3,2,1,0:T(8,128)S(1)}, f32[1,6,8,32,256]{4,3,2,1,0:T(8,128)}, u32[]{:S(2)}) copy-start(f32[1,6,8,32,256]{4,3,2,1,0:T(8,128)} %param.9) | copy-start | bytes 4718596
  290.5 12.3 %collective-permute-start.6 = (f32[6,1,32,256]{3,0,2,1:T(8,128)S(1)}, f32[6,1,32,256]{3,0,2,1:T(8,128)S(1)}, u32[]{:S(2)}, u32[]{:S(2)}) collective-permute-start(f32[6,1,32,256]{3,0,2,1:T(8,128)S(1)} %get-tuple-element.10), channel_id=1, source_target_pairs={{1,0},{2,1},{3,2},{4,3},{5,4},{6,5},{7,6},{8,7},{9,8},{10,9},{11,1... | collective-permute-start | bytes 589832 | tf_op jit(solution)/shard_map/ppermute | solution.py:21
  311.2 9.0 %collective-permute-start.9 = (f32[6,1,32,256]{3,0,2,1:T(8,128)S(1)}, f32[6,1,32,256]{3,0,2,1:T(8,128)S(1)}, u32[]{:S(2)}, u32[]{:S(2)}) collective-permute-start(f32[6,1,32,256]{3,0,2,1:T(8,128)S(1)} %get-tuple-element.7), channel_id=1, source_target_pairs={{0,1},{1,2},{2,3},{3,4},{4,5},{5,6},{6,7},{7,8},{8,9},{9,10},{10,1... | collective-permute-start | bytes 589832 | tf_op jit(solution)/shard_map/ppermute | solution.py:18
  313.1 11.2 %collective-permute-start.8 = (f32[6,1,32,256]{3,0,2,1:T(8,128)S(1)}, f32[6,1,32,256]{3,0,2,1:T(8,128)S(1)}, u32[]{:S(2)}, u32[]{:S(2)}) collective-permute-start(f32[6,1,32,256]{3,0,2,1:T(8,128)S(1)} %get-tuple-element.8), channel_id=1, source_target_pairs={{1,0},{2,1},{3,2},{4,3},{5,4},{6,5},{7,6},{8,7},{9,8},{10,9},{11,1... | collective-permute-start | bytes 589832 | tf_op jit(solution)/shard_map/ppermute | solution.py:21
  331.2 8.1 %collective-permute-start.11 = (f32[6,1,32,256]{3,0,2,1:T(8,128)S(1)}, f32[6,1,32,256]{3,0,2,1:T(8,128)S(1)}, u32[]{:S(2)}, u32[]{:S(2)}) collective-permute-start(f32[6,1,32,256]{3,0,2,1:T(8,128)S(1)} %get-tuple-element.5), channel_id=1, source_target_pairs={{0,1},{1,2},{2,3},{3,4},{4,5},{5,6},{6,7},{7,8},{8,9},{9,10},{10,1... | collective-permute-start | bytes 589832 | tf_op jit(solution)/shard_map/ppermute | solution.py:18
  333.2 10.2 %collective-permute-start.10 = (f32[6,1,32,256]{3,0,2,1:T(8,128)S(1)}, f32[6,1,32,256]{3,0,2,1:T(8,128)S(1)}, u32[]{:S(2)}, u32[]{:S(2)}) collective-permute-start(f32[6,1,32,256]{3,0,2,1:T(8,128)S(1)} %get-tuple-element.6), channel_id=1, source_target_pairs={{1,0},{2,1},{3,2},{4,3},{5,4},{6,5},{7,6},{8,7},{9,8},{10,9},{11,1... | collective-permute-start | bytes 589832 | tf_op jit(solution)/shard_map/ppermute | solution.py:21
  539.1 20.5 %copy-start.1 = (s32[1,16,16]{2,1,0:T(8,128)S(1)}, s32[1,16,16]{2,1,0:T(8,128)}, u32[]{:S(2)}) copy-start(s32[1,16,16]{2,1,0:T(8,128)} %param.15) | copy-start | bytes 3076
where the time goes:
time: 570 us; the launch traced here: 560 us
  local copies, waits for them, and re-layouts  381 us (67%)
  matrix products  59.9 us (11%)
  starting transfers between devices  51.8 us (9%)
  waiting for transfers between devices  37.6 us (7%)
  other arithmetic  15.7 us (3%)
  blocking collectives  13.4 us (2%)
    gather x2, local copies, waits for them, and re-layouts, shards(): values = flat[:, corner_cell].reshape(nvar, comps, slots, 8, tile)  238 us
    scatter x2, local copies, waits for them, and re-layouts, shards(): flat = flat.at[:, target_cell].set(incoming, mode='drop')  64.5 us
    dot_general x18, matrix products, mix(): jnp.einsum('vw,wxyz->vxyz', jac_dim, field, precision=lax.Precision.HIGHEST)  59.9 us
    reshape x2, local copies, waits for them, and re-layouts, shards(): flat = state.reshape(nvar, total_cells)  33.2 us
    ppermute x6, waiting for transfers between devices, padded_2(): lax.ppermute(lax.slice_in_dim(block, 0, width, axis=dim), axis, backward)  24 us
    ppermute x6, starting transfers between devices, padded_2(): lax.ppermute(lax.slice_in_dim(block, 0, width, axis=dim), axis, backward)  20.8 us
    another operation x1, local copies, waits for them, and re-layouts, shards(): return state[None]  20.5 us
    reshape x1, local copies, waits for them, and re-layouts, shards(): state = flat.reshape(nvar, rows, width_y, width_z)  17.8 us
  transfers between devices with their start and end apart: 14, of which 11 were waited for; matrix products, arithmetic and copies ran while one was open for 31% of the time, Pallas kernels for 0%

commit v1 on v0

v1 whole, which is shorter than its diff:
```python
import functools

import jax
import jax.numpy as jnp
from jax import lax
from jax.experimental import pallas as pl
from jax.experimental.pallas import tpu as pltpu
from jax.sharding import PartitionSpec as P

F32 = jnp.float32
I32 = jnp.int32
NV, CX, CY, CZ = 6, 8, 32, 256
LANES = 128
TILES = 32
POINTS = TILES * LANES
NT = CY // 8
YGROUPS = 11
DONOR_ROWS = 2 * YGROUPS * CZ
RECV_GROUPS = 2 * (CX - 1)
RECV_ROWS = RECV_GROUPS * CZ
PSEUDO_DIAG = 2.5
VMEM = pl.BlockSpec(memory_space=pltpu.VMEM)
SMEM = pl.BlockSpec(memory_space=pltpu.SMEM)
HBM = pl.BlockSpec(memory_space=pltpu.HBM)
ANY = pl.BlockSpec(memory_space=pl.ANY)
PADY = CY + 16
HALF = CZ // 2


def sds(shape, dtype=F32):
    return jax.ShapeDtypeStruct(shape, dtype)


def field(rows, pad=PADY):
    return pltpu.VMEM((NV, rows, 2, pad, LANES), F32)


def call(body, name, outs, ins, out_specs, scratch=(), vmem_mb=12, cost_us=1.0):
    outs = jax.tree.map(
        lambda o, spec: pltpu.HBM(o.shape, o.dtype) if spec is HBM else o, outs, out_specs
    )
    kernel = pl.pallas_call(
        body,
        out_shape=outs,
        in_specs=ins,
        out_specs=out_specs,
        scratch_shapes=list(scratch),
        compiler_params=pltpu.CompilerParams(vmem_limit_bytes=vmem_mb << 20),
        cost_estimate=pl.CostEstimate(
            flops=0, transcendentals=0, bytes_accessed=int(cost_us * 3.0e6)
        ),
        name=name,
    )

    def run(*args):
        return kernel(*[
            pltpu.with_memory_space_constraint(a, pltpu.HBM) if spec is HBM else a
            for a, spec in zip(args, ins, strict=True)
        ])

    return run


class Copies:
    def __init__(self, sem):
        self.sem, self.list = sem, []

    def add(self, src, dst):
        c = pltpu.make_async_copy(src, dst, self.sem)
        c.start()
        self.list.append(c)

    def halves(self, src, dst, y0=8):
        n = len(src.shape) - 2
        for h in range(2):
            full = (slice(None),) * n
            self.add(
                src.at[full + (slice(None), pl.ds(LANES * h, LANES))],
                dst.at[full + (h, pl.ds(y0, CY), slice(None))],
            )

    def halves_out(self, src, dst, y0=8):
        n = len(dst.shape) - 2
        for h in range(2):
            full = (slice(None),) * n
            self.add(
                src.at[full + (h, pl.ds(y0, CY), slice(None))],
                dst.at[full + (slice(None), pl.ds(LANES * h, LANES))],
            )

    def wait(self):
        for c in self.list:
            c.wait()
        self.list = []


def clear_pads(f, first, last):
    zero = jnp.zeros((8, LANES), F32)

    @pl.loop(first, last)
    def _(x):
        for v in range(NV):
            for h in range(2):
                f[v, x, h, 0:8, :] = zero
                f[v, x, h, PADY - 8 : PADY, :] = zero


def tile_terms(f, x, t, jh, kap):
    lane = lax.broadcasted_iota(I32, (8, LANES), 1)
    y0 = pl.multiple_of(8 * t + 8, 8)
    acc = [[None, None] for _ in range(NV)]
    centres = []
    for w in range(NV):
        c = [f[w, x, h, pl.ds(y0, 8), :] for h in range(2)]
        down = [pltpu.roll(c[h], 1, 1) for h in range(2)]
        up = [pltpu.roll(c[h], LANES - 1, 1) for h in range(2)]
        zm = [jnp.where(lane == 0, 0.0, down[0]), jnp.where(lane == 0, down[0], down[1])]
        zp = [
            jnp.where(lane == LANES - 1, up[1], up[0]),
            jnp.where(lane == LANES - 1, 0.0, up[1]),
        ]
        for h in range(2):
            xm, xp = f[w, x - 1, h, pl.ds(y0, 8), :], f[w, x + 1, h, pl.ds(y0, 8), :]
            ym, yp = f[w, x, h, pl.ds(y0 - 1, 8), :], f[w, x, h, pl.ds(y0 + 1, 8), :]
            dx, dy, dz = xp - xm, yp - ym, zp[h] - zm[h]
            beside = (xp + xm) + (yp + ym) + (zp[h] + zm[h])
            for v in range(NV):
                term = jh[v * 6 + w] * dx + jh[36 + v * 6 + w] * dy + jh[72 + v * 6 + w] * dz
                if v == w:
                    term = term - kap[h] * beside
                acc[v][h] = term if acc[v][h] is None else acc[v][h] + term
        centres.append(c)
    return acc, centres


def kap_tile(kap, k, t):
    y0 = pl.multiple_of(8 * t, 8)
    both = [kap[k, h, pl.ds(y0, 8), :] for h in range(2)]
    return both, [-1.0 / (PSEUDO_DIAG + 6.0 * b) for b in both]


def each_tile(count, row_of, body):
    @pl.loop(0, count * (NT // 2))
    def _(n):
        i = n // (NT // 2)
        row = row_of(i)
        for u in range(2):
            body(i, row, 2 * (n % (NT // 2)) + u)


def start_row(f, at, kap, k, now, prev, n, t, jh, emit):
    kp, ninv = kap_tile(kap, k, t)
    acc, centres = tile_terms(f, at, t, jh, kp)
    y0 = pl.multiple_of(8 * t, 8)
    for v in range(NV):
        for h in range(2):
            past = prev[v, n, h, pl.ds(y0, 8), :] - 4.0 * now[v, n, h, pl.ds(y0, 8), :]
            c = centres[v][h]
            r = 0.5 * (3.0 * c + past) + acc[v][h] + (6.0 * kp[h]) * c
            emit(v, h, r, r * ninv[h])


def relax_row(f, at, rs, ra, kap, k, t, jh, emit):
    kp, ninv = kap_tile(kap, k, t)
    acc, _ = tile_terms(f, at, t, jh, kp)
    y0 = pl.multiple_of(8 * t, 8)
    for v in range(NV):
        for h in range(2):
            emit(v, h, (rs[v, ra, h, pl.ds(y0, 8), :] + acc[v][h]) * ninv[h])


def edge_rows(f, kap, now, prev, jh, ers, es1):
    def body(i, row, t):
        y0 = pl.multiple_of(8 * t, 8)

        def emit(v, h, r, s):
            ers[v, i, h, pl.ds(y0, 8), :] = r
            es1[v, i, h, pl.ds(y0, 8), :] = s

        start_row(f, row + 1, kap, i, now, prev, i, t, jh, emit)

    each_tile(4, lambda i: i + 4 * (i // 2), body)


def edge_load(c, now, prev, kap, nowb, prevb, kapb):
    for i, x in ((0, 0), (2, 6)):
        c.halves(now.at[:, pl.ds(x, 2)], nowb.at[:, pl.ds(i, 2)], 0)
        c.halves(prev.at[:, pl.ds(x, 2)], prevb.at[:, pl.ds(i, 2)], 0)
        c.halves(kap.at[pl.ds(x, 2)], kapb.at[pl.ds(i, 2)], 0)


def edge_send(c, f, kap, ers, es1, lo, hi, er):
    for i, msg, row in ((0, lo, 0), (3, hi, CX - 1)):
        c.halves_out(f.at[:, row + 1], msg.at[pl.ds(0, NV)])
        c.halves_out(ers.at[:, i], msg.at[pl.ds(NV, NV)], 0)
        c.halves_out(es1.at[:, 1 + i // 3], msg.at[pl.ds(2 * NV, NV)], 0)
        c.halves_out(kap.at[i], msg.at[3 * NV], 0)
    c.halves_out(ers.at[:, pl.ds(1, 2)], er, 0)


def edge_zero(f):
    @pl.loop(0, CY // 8)
    def _(t):
        for v in range(NV):
            for h in range(2):
                for x in (0, CX + 1):
                    f[v, x, h, pl.ds(pl.multiple_of(8 * t + 8, 8), 8), :] = jnp.zeros((8, LANES), F32)


EDGE_SCRATCH = (
    field(4, CY), field(4, CY), pltpu.VMEM((4, 2, CY, LANES), F32),
    field(4, CY), field(4, CY),
)


def edge_body(now, prev, kap, jh, lo, hi, er, f, nowb, prevb, kapb, ers, es1, sem):
    c = Copies(sem.at[0])
    for x in (0, 5):
        c.halves(now.at[:, pl.ds(x, 3)], f.at[:, pl.ds(x + 1, 3)])
    edge_load(c, now, prev, kap, nowb, prevb, kapb)
    clear_pads(f, 1, 4)
    clear_pads(f, 6, 9)
    edge_zero(f)
    c.wait()
    edge_rows(f, kapb, nowb, prevb, jh, ers, es1)
    edge_send(c, f, kapb, ers, es1, lo, hi, er)
    c.wait()


def inner_body(
    q, now, prev, kap, jh, lo, hi, rs_out, s1_out, s2_out, s3_out,
    f, nowb, prevb, kapb, rs, s1, s2, s3, sem,
):
    c = Copies(sem.at[0])
    c.halves(q.at[:, pl.ds(1, 6)], f)
    c.halves(now.at[:, pl.ds(2, 4)], nowb, 0)
    c.halves(prev.at[:, pl.ds(2, 4)], prevb, 0)
    c.halves(kap.at[pl.ds(2, 4)], kapb, 0)
    c.halves(lo.at[pl.ds(2 * NV, NV)], s1.at[:, 0])
    c.halves(hi.at[pl.ds(2 * NV, NV)], s1.at[:, 5])
    clear_pads(f, 1, 5)
    clear_pads(s1, 1, 5)
    clear_pads(s2, 1, 3)
    c.wait()

    def first(i, row, t):
        def emit(v, h, r, s):
            rs[v, i, h, pl.ds(pl.multiple_of(8 * t, 8), 8), :] = r
            s1[v, i + 1, h, pl.ds(pl.multiple_of(8 * t + 8, 8), 8), :] = s

        start_row(f, i + 1, kapb, i, nowb, prevb, i, t, jh, emit)

    each_tile(4, lambda i: i, first)
    for i in range(2):
        c.halves_out(rs.at[:, 3 * i], rs_out.at[:, i], 0)
        c.halves_out(s1.at[:, 3 * i + 1], s1_out.at[:, i])

    def second(i, row, t):
        def emit(v, h, val):
            s2[v, i, h, pl.ds(pl.multiple_of(8 * t + 8, 8), 8), :] = val

        relax_row(s1, i + 1, rs, i, kapb, i, t, jh, emit)

    each_tile(4, lambda i: i, second)
    c.halves_out(s2, s2_out)

    def third(i, row, t):
        def emit(v, h, val):
            s3[v, i, h, pl.ds(pl.multiple_of(8 * t, 8), 8), :] = val

        relax_row(s2, i + 1, rs, i + 1, kapb, i + 1, t, jh, emit)

    each_tile(2, lambda i: i, third)
    c.halves_out(s3, s3_out, 0)
    c.wait()


INNER_SCRATCH = (
    field(6), field(4, CY), field(4, CY), pltpu.VMEM((4, 2, CY, LANES), F32),
    field(4, CY), field(6), field(4), field(2, CY), pltpu.SemaphoreType.DMA((1,)),
)


def fix_rows(rse, s1e, far, kape, jh, lo_ok, hi_ok):
    def body(i, row, t):
        y0 = pl.multiple_of(8 * t, 8)
        sign = jnp.where(i % 2 == 0, 1.0, -1.0).astype(F32)
        scale = jnp.where(i == 0, lo_ok, jnp.where(i == 3, hi_ok, 1.0))
        kp, ninv = kap_tile(kape, row + 1, t)
        for h in range(2):
            side = [far[w, i, h, pl.ds(y0, 8), :] for w in range(NV)]
            turned = [side[w] * sign for w in range(NV)]
            for v in range(NV):
                r = rse[v, row + 1, h, pl.ds(y0, 8), :] - kp[h] * side[v]
                for w in range(NV):
                    r = r + jh[v * 6 + w] * turned[w]
                rse[v, row + 1, h, pl.ds(y0, 8), :] = r
                s1e[v, row + 2, h, pl.ds(pl.multiple_of(y0 + 8, 8), 8), :] = r * (ninv[h] * scale)

    each_tile(4, lambda i: i - 1 + 6 * (i // 2), body)


def finish_body(
    q, kap, jh, who, idx_in, pairs_in, own_lo, own_hi, got_lo, got_hi, w_in,
    er, rs_in, s1_in, s2_in, s3_in, qn, send,
    rse, s1e, s2e, kape, far, qb, s3, q8, tab, g, wb, idx, pairs, sem,
):
    lo_ok = jnp.where(who[1] > 0, 1.0, 0.0).astype(F32)
    hi_ok = jnp.where(who[1] < who[2] - 1, 1.0, 0.0).astype(F32)
    c = Copies(sem.at[0])
    c.halves(kap, kape.at[pl.ds(1, CX)], 0)
    c.halves(got_lo.at[3 * NV], kape.at[0], 0)
    c.halves(got_hi.at[3 * NV], kape.at[CX + 1], 0)
    for i, msg in ((0, own_lo), (1, got_lo), (2, got_hi), (3, own_hi)):
        c.halves(msg.at[pl.ds(0, NV)], far.at[:, i], 0)
    for x, msg in ((0, got_lo), (1, own_lo), (8, own_hi), (9, got_hi)):
        c.halves(msg.at[pl.ds(NV, NV)], rse.at[:, x], 0)
    for x, msg in ((0, got_lo), (3, own_lo), (8, own_hi), (11, got_hi)):
        c.halves(msg.at[pl.ds(2 * NV, NV)], s1e.at[:, x])
    for i, (r, s) in enumerate(((2, 4), (7, 7))):
        c.halves(er.at[:, i], rse.at[:, r], 0)
        c.halves(rs_in.at[:, i], rse.at[:, (3, 6)[i]], 0)
        c.halves(s1_in.at[:, i], s1e.at[:, s])
    c.halves(s2_in, s2e.at[:, pl.ds(3, 4)])
    d = Copies(sem.at[1])
    d.halves(q, qb, 0)
    d.halves(s3_in, s3, 0)
    e = Copies(sem.at[2])
    e.add(w_in, wb)
    e.add(idx_in, idx)
    e.add(pairs_in, pairs)
    clear_pads(s1e, 1, 4)
    clear_pads(s1e, 8, 11)
    clear_pads(s2e, 1, 4)
    clear_pads(s2e, 6, 9)
    c.wait()

    fix_rows(rse, s1e, far, kape, jh, lo_ok, hi_ok)

    def second(i, row, t):
        scale = jnp.where(i == 0, lo_ok, jnp.where(i == 5, hi_ok, 1.0))

        def emit(v, h, val):
            s2e[v, row + 1, h, pl.ds(pl.multiple_of(8 * t + 8, 8), 8), :] = val * scale

        relax_row(s1e, row + 2, rse, row + 1, kape, row + 1, t, jh, emit)

    each_tile(6, lambda i: i - 1 + 4 * (i // 3), second)
    d.wait()

    def put(row, v, h, t, val):
        qb[v, row, h, pl.ds(pl.multiple_of(8 * t, 8), 8), :] = val
        q8[row, h, pl.ds(64 * t + v, 8, stride=8), :] = val

    def third(i, row, t):
        def emit(v, h, val):
            put(row, v, h, t, qb[v, row, h, pl.ds(pl.multiple_of(8 * t, 8), 8), :] + val)

        relax_row(s2e, row + 1, rse, row + 1, kape, row + 1, t, jh, emit)

    each_tile(6, lambda i: i + 2 * (i // 3), third)

    def rest(i, row, t):
        y0 = pl.multiple_of(8 * t, 8)
        for v in range(NV):
            for h in range(2):
                put(row, v, h, t, qb[v, row, h, pl.ds(y0, 8), :] + s3[v, i, h, pl.ds(y0, 8), :])

    each_tile(2, lambda i: i + 3, rest)
    d.halves_out(qb, qn, 0)
    gather_points(idx, pairs, who[0], wb, e, send, q8, tab, g)
    d.wait()


FINISH_SCRATCH = (
    field(CX + 2, CY), field(CX + 4), field(CX + 2), pltpu.VMEM((CX + 2, 2, CY, LANES), F32),
    field(4, CY), field(CX, CY), field(2, CY),
    pltpu.VMEM((CX, 2, 8 * CY, LANES), F32),
    pltpu.VMEM((DONOR_ROWS + 8, LANES), F32),
    pltpu.VMEM((2 * POINTS, LANES), F32),
    pltpu.VMEM((2, POINTS, LANES), F32),
    pltpu.SMEM((TILES, LANES), I32),
    pltpu.SMEM((16, 16), I32),
    pltpu.SemaphoreType.DMA((3,)),
)


def gather_points(idx, pairs, me, wb, loads, send, q8, tab, g):
    @pl.loop(0, YGROUPS)
    def _(yg):
        first = pl.multiple_of(jnp.minimum(yg * 3, CY - 4) * 8, 8)
        for xg in range(2):
            for h in range(2):
                block = [q8[xg * 3 + xx, h, pl.ds(first, 32), :] for xx in range(4)]
                row = pl.multiple_of((xg * YGROUPS + yg) * CZ + h * LANES, LANES)
                tab[pl.ds(row, LANES), :] = jnp.concatenate(block, axis=0).T

    loads.wait()

    @pl.loop(0, TILES)
    def _(tile):
        @pl.when(tile % 2 < pairs[me, tile // 2])
        def _():
            @pl.loop(0, LANES // 16)
            def _(b):
                for u in range(16):
                    row = idx[tile, b * 16 + u]
                    at = pl.multiple_of(tile * 256 + b * 32, 32) + 2 * u
                    g[pl.ds(at, 2), :] = tab[pl.ds(row, 2), :]

    @pl.loop(0, TILES // 4)
    def _(n):
        for u in range(4):
            o = pl.multiple_of(n * 4 * LANES + u * LANES, LANES)
            here = g[pl.ds(o * 2, LANES, stride=2), :] * wb[0, pl.ds(o, LANES), :]
            here = here + g[pl.ds(o * 2 + 1, LANES, stride=2), :] * wb[1, pl.ds(o, LANES), :]
            turned = here.T
            parts = [turned[8 * k : 8 * k + 8] for k in range(16)]
            while len(parts) > 1:
                parts = [a + b for a, b in zip(parts[::2], parts[1::2])]
            send[2 * n + u // 2, u % 2] = parts[0]


def setup_body(
    donor_in, recv_in, pairs_in, who, held_in, didx_out, ridx_out, rlane_out, w_out,
    donor, recv, pairs, held, didx, dpos, ridx, rlane, w, sem,
):
    c = Copies(sem.at[0])
    c.add(donor_in, donor)
    c.add(recv_in, recv)
    c.add(pairs_in, pairs)
    d = Copies(sem.at[1])
    d.add(held_in, held)
    c.wait()
    me = who[0]
    for s in range(16):
        live = pairs[s, me]
        for t in range(2):
            i = 2 * s + t
            cell = donor[s, t, 0:1, :]
            x, y, z = cell >> 13, (cell >> 8) & (CY - 1), cell & (CZ - 1)
            xg = jnp.where(x >= 3, 1, 0)
            yg = (y * 11) >> 5
            didx[i : i + 1, :] = (xg * YGROUPS + yg) * CZ + z
            dpos[i : i + 1, :] = (x - 3 * xg) * 4 + (y - jnp.minimum(yg * 3, CY - 4))
            cell = recv[s, t : t + 1, :]
            x, y, z = cell >> 13, (cell >> 8) & (CY - 1), cell & (CZ - 1)
            row = (2 * x + (y >> 4)) * CZ + z
            ridx[i : i + 1, :] = jnp.where(t < live, row, RECV_ROWS)
            rlane[i : i + 1, :] = y & 15
    c.add(didx, didx_out)
    c.add(ridx, ridx_out)
    c.add(rlane, rlane_out)
    d.wait()

    @pl.loop(0, TILES // 2)
    def _(n):
        for u in range(2):
            kpos = lax.broadcasted_iota(I32, (16, LANES), 0)
            base = jnp.broadcast_to(dpos[pl.ds(2 * n + u, 1), :], (16, LANES))
            o = pl.multiple_of(n * 2 * LANES + u * LANES, LANES)
            for l in range(2):
                grid = jnp.zeros((16, LANES), F32)
                for i in range(2):
                    for j in range(2):
                        k = 4 * i + 2 * j + l
                        row = jnp.broadcast_to(held[n, u, k : k + 1, :], (16, LANES))
                        grid = jnp.where(kpos == base + (4 * i + j), row, grid)
                wide = [jnp.broadcast_to(grid[k : k + 1], (8, LANES)) for k in range(16)]
                w[l, pl.ds(o, LANES), :] = jnp.concatenate(wide, axis=0).T

    d.add(w, w_out)
    c.wait()
    d.wait()


SETUP_SCRATCH = (
    pltpu.VMEM((16, 2, 8, LANES), I32),
    pltpu.VMEM((16, 2, LANES), I32),
    pltpu.SMEM((16, 16), I32),
    pltpu.VMEM((16, 2, 8, LANES), F32),
    pltpu.VMEM((TILES, LANES), I32),
    pltpu.VMEM((TILES, LANES), I32),
    pltpu.VMEM((TILES, LANES), I32),
    pltpu.VMEM((TILES, LANES), I32),
    pltpu.VMEM((2, POINTS, LANES), F32),
    pltpu.SemaphoreType.DMA((2,)),
)


def scatter_points(vals, ridx, rlane, qb, arrive, loads, f, y0, x0, vrep, u, ut):
    mark = lax.broadcasted_iota(I32, (8, LANES), 0) == NV
    lane = lax.broadcasted_iota(I32, (1, LANES), 1) >> 3

    @pl.loop(0, RECV_ROWS // LANES)
    def _(i):
        u[pl.ds(pl.multiple_of(i * LANES, LANES), LANES), :] = jnp.zeros((LANES, LANES), F32)

    @pl.loop(0, TILES // 4)
    def _(n):
        for k in range(4):
            v = jnp.where(mark, 1.0, vals[2 * n + k // 2, k % 2])
            rows = pl.ds(pl.multiple_of(n * 4 * LANES + k * LANES, LANES), LANES)
            vrep[rows, :] = jnp.concatenate([v] * 16, axis=0).T

    loads.wait()

    @pl.loop(0, TILES)
    def _(tile):
        @pl.loop(0, LANES // 16)
        def _(b):
            for j in range(16):
                row = ridx[tile, b * 16 + j]
                k = rlane[tile, b * 16 + j]
                at = pl.multiple_of(tile * LANES + b * 16, 16) + j
                pltpu.store(u.at[pl.ds(row, 1), :], vrep[pl.ds(at, 1), :], mask=lane == k)

    @pl.loop(0, CX - 1)
    def _(x):
        for yh in range(2):
            for h in range(2):
                row = pl.multiple_of((2 * x + yh) * CZ + h * LANES, LANES)
                ut[2 * x + yh, h] = u[pl.ds(row, LANES), :].T

    arrive.wait()

    @pl.loop(0, CX - 1)
    def _(x):
        for yh in range(2):
            for h in range(2):
                for t in range(2):
                    part = ut.at[2 * x + yh, h]
                    hit = part[pl.ds(64 * t + NV, 8, stride=8), :] != 0.0
                    y = 16 * yh + 8 * t
                    for v in range(NV):
                        new = part[pl.ds(64 * t + v, 8, stride=8), :]
                        f[v, x + x0, h, y0 + y : y0 + y + 8, :] = jnp.where(
                            hit, new, qb[v, x, h, y : y + 8, :]
                        )


def scatter_body(q, vals, ridx_in, rlane_in, out, qb, vrep, u, ut, ridx, rlane, sem):
    c, e = Copies(sem.at[0]), Copies(sem.at[2])
    e.add(ridx_in, ridx)
    e.add(rlane_in, rlane)
    c.halves(q, qb, 0)
    scatter_points(vals, ridx, rlane, qb, c, e, qb, 0, 0, vrep, u, ut)
    c.halves_out(qb, out, 0)
    c.wait()


def scatter_edge_body(
    q, vals, ridx_in, rlane_in, now, prev, kap, jh, out, lo, hi, er,
    qb, vrep, u, ut, ridx, rlane, f, nowb, prevb, kapb, ers, es1, sem,
):
    c, e = Copies(sem.at[0]), Copies(sem.at[2])
    e.add(ridx_in, ridx)
    e.add(rlane_in, rlane)
    c.halves(q, qb, 0)
    d = Copies(sem.at[1])
    edge_load(d, now, prev, kap, nowb, prevb, kapb)
    clear_pads(f, 1, 4)
    clear_pads(f, 6, 9)
    edge_zero(f)
    scatter_points(vals, ridx, rlane, qb, c, e, f, 8, 1, vrep, u, ut)
    for v in range(NV):
        for h in range(2):
            f[v, CX, h, 8 : 8 + CY, :] = qb[v, CX - 1, h]
    c.halves_out(f.at[:, pl.ds(1, CX)], out)
    d.wait()
    edge_rows(f, kapb, nowb, prevb, jh, ers, es1)
    edge_send(d, f, kapb, ers, es1, lo, hi, er)
    d.wait()
    c.wait()


STATE = (NV, CX, CY, CZ)
SCATTER_SCRATCH = (
    field(CX, CY),
    pltpu.VMEM((POINTS, LANES), F32),
    pltpu.VMEM((RECV_ROWS + 8, LANES), F32),
    pltpu.VMEM((RECV_GROUPS, 2, LANES, LANES), F32),
    pltpu.SMEM((TILES, LANES), I32),
    pltpu.SMEM((TILES, LANES), I32),
)


def rows_of(n):
    return sds((NV, n, CY, CZ))


def shards(
    state_now, state_prev, viscosity, jacobian, donor_cell, interp_weight, recv_cell, pair_tiles
):
    now = state_now[0]
    prev = state_prev[0]
    kap = viscosity[0]
    jh = (jacobian[0] * 0.5).reshape(-1)
    count = lax.axis_size("blk")
    at = lax.axis_index("blk")
    me = lax.axis_index("comp")
    who = jnp.stack([me, at, jnp.int32(count)]).astype(I32)
    pairs = pair_tiles[0]
    forward = [(i, i + 1) for i in range(count - 1)]
    backward = [(b, a) for a, b in forward]

    messages = [sds((3 * NV + 1, CY, CZ))] * 2 + [rows_of(2)]

    idx_shape = sds((TILES, LANES), I32)
    sems = pltpu.SemaphoreType.DMA((3,))

    lo, hi, er = call(
        edge_body, "edge", messages, [HBM] * 3 + [SMEM], [HBM] * 3,
        scratch=(field(CX + 2),) + EDGE_SCRATCH + (sems,), cost_us=3.0,
    )(now, prev, kap, jh)
    state = now
    for sub in range(2):
        got_lo = lax.ppermute(hi, "blk", forward)
        got_hi = lax.ppermute(lo, "blk", backward)
        inner = call(
            inner_body, "inner", [rows_of(n) for n in (2, 2, 4, 2)],
            [HBM] * 4 + [SMEM] + [HBM] * 2, [HBM] * 4,
            scratch=INNER_SCRATCH, vmem_mb=14, cost_us=4.0,
        )(state, now, prev, kap, jh, lo, hi)
        if sub == 0:
            weights, _ = lax.optimization_barrier((interp_weight[0, 0], lo))
            held = lax.all_to_all(weights, "comp", split_axis=0, concat_axis=0, tiled=True)
            didx, ridx, rlane, wide = call(
                setup_body, "setup", [idx_shape] * 3 + [sds((2, POINTS, LANES))],
                [HBM] * 3 + [SMEM, ANY], [HBM] * 4, scratch=SETUP_SCRATCH, cost_us=4.0,
            )(donor_cell[0, 0], recv_cell[0, 0], pairs, who, held)
        relaxed, send = call(
            finish_body, "finish", [sds(STATE), sds((16, 2, 8, LANES))],
            [HBM, HBM, SMEM, SMEM] + [HBM] * 4 + [ANY] * 2 + [HBM] * 6, [HBM, VMEM],
            scratch=FINISH_SCRATCH, vmem_mb=30, cost_us=14.0,
        )(
            state, kap, jh, who, didx, pairs, lo, hi, got_lo, got_hi, wide,
            er, *inner,
        )
        arrived = lax.all_to_all(send, "comp", split_axis=0, concat_axis=0, tiled=True)
        if sub == 0:
            state, lo, hi, er = call(
                scatter_edge_body, "scatter_edge", [sds(STATE)] + messages,
                [HBM, VMEM, HBM, HBM, HBM, HBM, HBM, SMEM], [HBM] * 4,
                scratch=SCATTER_SCRATCH + (field(CX + 2),) + EDGE_SCRATCH + (sems,),
                vmem_mb=20, cost_us=12.0,
            )(relaxed, arrived, ridx, rlane, now, prev, kap, jh)
        else:
            state = call(
                scatter_body, "scatter", sds(STATE), [HBM, VMEM, HBM, HBM], HBM,
                scratch=SCATTER_SCRATCH + (sems,), vmem_mb=12, cost_us=10.0,
            )(relaxed, arrived, ridx, rlane)
    return state[None]


def solution(mesh):
    in_specs = (
        P("comp", None, "blk", None, None),
        P("comp", None, "blk", None, None),
        P("comp", "blk", None, None),
        P("comp", None, None, None),
        P("comp", "blk", None, None, None, None),
        P("comp", "blk", None, None, None, None),
        P("comp", "blk", None, None, None),
        P("blk", None, None),
    )
    out_specs = P("comp", None, "blk", None, None)
    return jax.shard_map(shards, mesh=mesh, in_specs=in_specs, out_specs=out_specs, check_vma=False)
```

time: 570 us -> 158 us (0.28)
  the two profiles are of different devices: /device:TPU:27 before, /device:TPU:7 now
where the time goes in v1:
time: 158 us
  Pallas kernels  93.9 us (59%)
  blocking collectives  29.7 us (19%)
  starting transfers between devices  22.9 us (14%)
  waiting for transfers between devices  10.7 us (7%)
    pallas_call x8, Pallas kernels, run(): kernel(*[pltpu.with_memory_space_constraint(a, pltpu.HBM) if spec is HBM...  93.9 us
    all_to_all x2, blocking collectives, shards(): lax.all_to_all(send, 'comp', split_axis=0, concat_axis=0, tiled=True)  29.7 us
    all_to_all x1, starting transfers between devices, shards(): lax.all_to_all(weights, 'comp', split_axis=0, concat_axis=0, tiled=True)  9.72 us
    ppermute x2, starting transfers between devices, shards(): got_hi = lax.ppermute(lo, 'blk', backward)  6.68 us
    ppermute x2, starting transfers between devices, shards(): got_lo = lax.ppermute(hi, 'blk', forward)  6.51 us
    ppermute x2, waiting for transfers between devices, shards(): got_hi = lax.ppermute(lo, 'blk', backward)  5.21 us
    ppermute x2, waiting for transfers between devices, shards(): got_lo = lax.ppermute(hi, 'blk', forward)  3.91 us
  transfers between devices with their start and end apart: 5, of which 3 were waited for; matrix products, arithmetic and copies ran while one was open for 0% of the time, Pallas kernels for 13%

profile of v1, /device:TPU:7, one launch (start us, length us, event | category | flops | bytes accessed | tf_op | source)
XLA Modules:
  0.0 158.3 jit_solution(9559062331449711962)
XLA Ops:
  0.0 0.7 multiply_reduce_fusion
  0.7 0.1 mul.12.jh
  0.8 5.4 %edge.1 = (f32[19,32,256]{2,1,0:T(8,128)}, f32[19,32,256]{2,1,0:T(8,128)}, f32[6,2,32,256]{3,2,1,0:T(8,128)}) custom-call(f32[6,8,32,256]{3,2,1,0:T(8,128)} %bitcast.10, f32[6,8,32,256]{3,2,1,0:T(8,128)} %bitcast.16, f32[8,32,256]{2,1,0:T(8,128)} %bitcast.20, f32[108]{0:T(128)S(1)} %mul.12.jh), custom_call_target="tpu_custom_call" | custom-call | bytes 9000000 | tf_op jit(solution)/shard_map/edge/pallas_call | solution.py:56
  6.3 3.2 %collective-permute-start = (f32[19,32,256]{2,1,0:T(8,128)}, f32[19,32,256]{2,1,0:T(8,128)S(1)}, u32[]{:S(2)}, u32[]{:S(2)}) collective-permute-start(f32[19,32,256]{2,1,0:T(8,128)} %get-tuple-element.32.hi.own_hi), channel_id=1, source_target_pairs={{0,1},{1,2},{2,3},{3,4},{4,5},{5,6},{6,7},{7,8},{8,9},{9,10},{10,1... | collective-permute-start | bytes 1867784 | tf_op jit(solution)/shard_map/ppermute | solution.py:618
  9.5 4.2 %collective-permute-start.1 = (f32[19,32,256]{2,1,0:T(8,128)}, f32[19,32,256]{2,1,0:T(8,128)S(1)}, u32[]{:S(2)}, u32[]{:S(2)}) collective-permute-start(f32[19,32,256]{2,1,0:T(8,128)} %get-tuple-element.29.lo.own_lo), channel_id=1, source_target_pairs={{1,0},{2,1},{3,2},{4,3},{5,4},{6,5},{7,6},{8,7},{9,8},{10,9},{11,1... | collective-permute-start | bytes 1867784 | tf_op jit(solution)/shard_map/ppermute | solution.py:619
  13.7 9.7 %all-to-all-start = ((f32[16,2,8,128]{3,2,1,0:T(8,128)}), f32[16,2,8,128]{3,2,1,0:T(8,128)S(1)}, u32[]{:S(2)}, u32[]{:S(2)}) async-start(f32[16,2,8,128]{3,2,1,0:T(8,128)} %bitcast.7), calls=%async_computation | async-start | bytes 262144 | tf_op jit(solution)/shard_map/all_to_all | solution.py:627
  23.4 7.5 %inner.2 = (f32[6,2,32,256]{3,2,1,0:T(8,128)}, f32[6,2,32,256]{3,2,1,0:T(8,128)}, f32[6,4,32,256]{3,2,1,0:T(8,128)}, f32[6,2,32,256]{3,2,1,0:T(8,128)}) custom-call(f32[6,8,32,256]{3,2,1,0:T(8,128)} %bitcast.11, f32[6,8,32,256]{3,2,1,0:T(8,128)} %bitcast.12, f32[6,8,32,256]{3,2,1,0:T(8,128)} %bitcast.17, f32[8,32,256]{2,1,0:T(8,128)} %bitcast.21, ...), custom_call_target="tpu_custom_call" | custom-call | bytes 12000000 | tf_op jit(solution)/shard_map/inner/pallas_call | solution.py:56
  30.9 0.1 pad_add_fusion.who
  31.0 1.6 all-to-all-done.held_in
  32.6 5.8 %setup.1 = (s32[32,128]{1,0:T(8,128)}, s32[32,128]{1,0:T(8,128)}, s32[32,128]{1,0:T(8,128)}, f32[2,4096,128]{2,1,0:T(8,128)}) custom-call(s32[16,2,8,128]{3,2,1,0:T(8,128)} %bitcast.26, s32[16,2,128]{2,1,0:T(2,128)} %bitcast.30, s32[16,16]{1,0:T(8,128)} %bitcast.27, s32[3]{0:T(128)S(1)} %pad_add_fusion.who, f32[16,2,8,128]{3,2,1,0:T(8,128)S(1)} %all-to-all-done.held_in), custom_call_target="tpu_custom_call" | custom-call | bytes 12000000 | tf_op jit(solution)/shard_map/setup/pallas_call | solution.py:56
  38.4 0.0 collective-permute-done.got_lo
  38.4 0.0 collective-permute-done.1.got_hi
  38.4 17.4 %finish.2 = (f32[6,8,32,256]{3,2,1,0:T(8,128)}, f32[16,2,8,128]{3,2,1,0:T(8,128)S(1)}) custom-call(f32[6,8,32,256]{3,2,1,0:T(8,128)} %bitcast.13, f32[8,32,256]{2,1,0:T(8,128)} %bitcast.22, f32[108]{0:T(128)S(1)} %mul.12.jh, s32[3]{0:T(128)S(1)} %pad_add_fusion.who, s32[32,128]{1,0:T(8,128)} %get-tuple-element.31.idx_in, s32[16,16]{1,0:T(8,128)} %bitcast.28, ...), custom_call_target="tpu_custom_call" | custom-call | bytes 42000000 | tf_op jit(solution)/shard_map/finish/pallas_call | solution.py:56
  55.9 15.2 %all_to_all.15.vals = f32[16,2,8,128]{3,2,1,0:T(8,128)S(1)} all-to-all(f32[16,2,8,128]{3,2,1,0:T(8,128)S(1)} %get-tuple-element.40), channel_id=1, replica_groups=mesh['comp'=16,'blk'=16] {'comp'}, dimensions={0} | all-to-all | bytes 262144 | tf_op jit(solution)/shard_map/all_to_all | solution.py:640
  71.1 17.8 %scatter_edge.1 = (f32[6,8,32,256]{3,2,1,0:T(8,128)}, f32[19,32,256]{2,1,0:T(8,128)}, f32[19,32,256]{2,1,0:T(8,128)}, f32[6,2,32,256]{3,2,1,0:T(8,128)}) custom-call(f32[6,8,32,256]{3,2,1,0:T(8,128)} %get-tuple-element.39.q, f32[16,2,8,128]{3,2,1,0:T(8,128)S(1)} %all_to_all.15.vals, s32[32,128]{1,0:T(8,128)} %get-tuple-element.41.ridx_in, ...), custom_call_target="tpu_custom_call" | custom-call | bytes 36000000 | tf_op jit(solution)/shard_map/scatter_edge/pallas_call | solution.py:56
  88.9 2.5 %collective-permute-start.3 = (f32[19,32,256]{2,1,0:T(8,128)}, f32[19,32,256]{2,1,0:T(8,128)S(1)}, u32[]{:S(2)}, u32[]{:S(2)}) collective-permute-start(f32[19,32,256]{2,1,0:T(8,128)} %get-tuple-element.44.lo.own_lo), channel_id=1, source_target_pairs={{1,0},{2,1},{3,2},{4,3},{5,4},{6,5},{7,6},{8,7},{9,8},{10,9},{11,1... | collective-permute-start | bytes 1867784 | tf_op jit(solution)/shard_map/ppermute | solution.py:619
  91.4 3.3 %collective-permute-start.2 = (f32[19,32,256]{2,1,0:T(8,128)}, f32[19,32,256]{2,1,0:T(8,128)S(1)}, u32[]{:S(2)}, u32[]{:S(2)}) collective-permute-start(f32[19,32,256]{2,1,0:T(8,128)} %get-tuple-element.45.hi.own_hi), channel_id=1, source_target_pairs={{0,1},{1,2},{2,3},{3,4},{4,5},{5,6},{6,7},{7,8},{8,9},{9,10},{10,1... | collective-permute-start | bytes 1867784 | tf_op jit(solution)/shard_map/ppermute | solution.py:618
  94.7 7.5 %inner.3 = (f32[6,2,32,256]{3,2,1,0:T(8,128)}, f32[6,2,32,256]{3,2,1,0:T(8,128)}, f32[6,4,32,256]{3,2,1,0:T(8,128)}, f32[6,2,32,256]{3,2,1,0:T(8,128)}) custom-call(f32[6,8,32,256]{3,2,1,0:T(8,128)} %get-tuple-element.43.q, f32[6,8,32,256]{3,2,1,0:T(8,128)} %bitcast.15, f32[6,8,32,256]{3,2,1,0:T(8,128)} %bitcast.19, f32[8,32,256]{2,1,0:T(8,128)} %bitcast.24, ...), custom_call_target="tpu_custom_call" | custom-call | bytes 12000000 | tf_op jit(solution)/shard_map/inner/pallas_call | solution.py:56
  102.2 5.2 %collective-permute-done.3.got_hi = f32[19,32,256]{2,1,0:T(8,128)S(1)} collective-permute-done((f32[19,32,256]{2,1,0:T(8,128)}, f32[19,32,256]{2,1,0:T(8,128)S(1)}, u32[]{:S(2)}, u32[]{:S(2)}) %collective-permute-start.3) | collective-permute-done | bytes 622624 | tf_op jit(solution)/shard_map/ppermute | solution.py:619
  107.4 3.9 %collective-permute-done.2.got_lo = f32[19,32,256]{2,1,0:T(8,128)S(1)} collective-permute-done((f32[19,32,256]{2,1,0:T(8,128)}, f32[19,32,256]{2,1,0:T(8,128)S(1)}, u32[]{:S(2)}, u32[]{:S(2)}) %collective-permute-start.2) | collective-permute-done | bytes 622624 | tf_op jit(solution)/shard_map/ppermute | solution.py:618
  111.3 17.4 %finish.3 = (f32[6,8,32,256]{3,2,1,0:T(8,128)}, f32[16,2,8,128]{3,2,1,0:T(8,128)S(1)}) custom-call(f32[6,8,32,256]{3,2,1,0:T(8,128)} %get-tuple-element.43.q, f32[8,32,256]{2,1,0:T(8,128)} %bitcast.25, f32[108]{0:T(128)S(1)} %mul.12.jh, s32[3]{0:T(128)S(1)} %pad_add_fusion.who, s32[32,128]{1,0:T(8,128)} %get-tuple-element.31.idx_in, s32[16,16]{1,0:T(8,128)} %bitcast.29, ...), custom_call_target="tpu_custom_call" | custom-call | bytes 42000000 | tf_op jit(solution)/shard_map/finish/pallas_call | solution.py:56
  128.7 14.5 %all_to_all.16.vals = f32[16,2,8,128]{3,2,1,0:T(8,128)S(1)} all-to-all(f32[16,2,8,128]{3,2,1,0:T(8,128)S(1)} %get-tuple-element.52), channel_id=1, replica_groups=mesh['comp'=16,'blk'=16] {'comp'}, dimensions={0} | all-to-all | bytes 262144 | tf_op jit(solution)/shard_map/all_to_all | solution.py:640
  143.2 15.0 %scatter.1 = f32[6,8,32,256]{3,2,1,0:T(8,128)} custom-call(f32[6,8,32,256]{3,2,1,0:T(8,128)} %get-tuple-element.51.q, f32[16,2,8,128]{3,2,1,0:T(8,128)S(1)} %all_to_all.16.vals, s32[32,128]{1,0:T(8,128)} %get-tuple-element.41.ridx_in, s32[32,128]{1,0:T(8,128)} %get-tuple-element.42.rlane_in), custom_call_target="tpu_custom_call" | custom-call | bytes 30000000 | tf_op jit(solution)/shard_map/scatter/pallas_call | solution.py:56
Async XLA Ops:
  6.3 32.1 %collective-permute-start = (f32[19,32,256]{2,1,0:T(8,128)}, f32[19,32,256]{2,1,0:T(8,128)S(1)}, u32[]{:S(2)}, u32[]{:S(2)}) collective-permute-start(f32[19,32,256]{2,1,0:T(8,128)} %get-tuple-element.32.hi.own_hi), channel_id=1, source_target_pairs={{0,1},{1,2},{2,3},{3,4},{4,5},{5,6},{6,7},{7,8},{8,9},{9,10},{10,1... | collective-permute-start | bytes 1867784 | tf_op jit(solution)/shard_map/ppermute | solution.py:618
  9.5 28.9 %collective-permute-start.1 = (f32[19,32,256]{2,1,0:T(8,128)}, f32[19,32,256]{2,1,0:T(8,128)S(1)}, u32[]{:S(2)}, u32[]{:S(2)}) collective-permute-start(f32[19,32,256]{2,1,0:T(8,128)} %get-tuple-element.29.lo.own_lo), channel_id=1, source_target_pairs={{1,0},{2,1},{3,2},{4,3},{5,4},{6,5},{7,6},{8,7},{9,8},{10,9},{11,1... | collective-permute-start | bytes 1867784 | tf_op jit(solution)/shard_map/ppermute | solution.py:619
  13.7 18.9 %all-to-all-start = ((f32[16,2,8,128]{3,2,1,0:T(8,128)}), f32[16,2,8,128]{3,2,1,0:T(8,128)S(1)}, u32[]{:S(2)}, u32[]{:S(2)}) async-start(f32[16,2,8,128]{3,2,1,0:T(8,128)} %bitcast.7), calls=%async_computation | async-start | bytes 262144 | tf_op jit(solution)/shard_map/all_to_all | solution.py:627
  88.9 18.5 %collective-permute-start.3 = (f32[19,32,256]{2,1,0:T(8,128)}, f32[19,32,256]{2,1,0:T(8,128)S(1)}, u32[]{:S(2)}, u32[]{:S(2)}) collective-permute-start(f32[19,32,256]{2,1,0:T(8,128)} %get-tuple-element.44.lo.own_lo), channel_id=1, source_target_pairs={{1,0},{2,1},{3,2},{4,3},{5,4},{6,5},{7,6},{8,7},{9,8},{10,9},{11,1... | collective-permute-start | bytes 1867784 | tf_op jit(solution)/shard_map/ppermute | solution.py:619
  91.4 19.9 %collective-permute-start.2 = (f32[19,32,256]{2,1,0:T(8,128)}, f32[19,32,256]{2,1,0:T(8,128)S(1)}, u32[]{:S(2)}, u32[]{:S(2)}) collective-permute-start(f32[19,32,256]{2,1,0:T(8,128)} %get-tuple-element.45.hi.own_hi), channel_id=1, source_target_pairs={{0,1},{1,2},{2,3},{3,4},{4,5},{5,6},{6,7},{7,8},{8,9},{9,10},{10,1... | collective-permute-start | bytes 1867784 | tf_op jit(solution)/shard_map/ppermute | solution.py:618

commit v2 on v1

--- a/solution.py
+++ b/solution.py
@@ -379,7 +379,7 @@
     pltpu.VMEM((DONOR_ROWS + 8, LANES), F32),
     pltpu.VMEM((2 * POINTS, LANES), F32),
     pltpu.VMEM((2, POINTS, LANES), F32),
-    pltpu.SMEM((TILES, LANES), I32),
+    pltpu.SMEM((POINTS,), I32),
     pltpu.SMEM((16, 16), I32),
     pltpu.SemaphoreType.DMA((3,)),
 )
@@ -401,29 +401,29 @@
     def _(tile):
         @pl.when(tile % 2 < pairs[me, tile // 2])
         def _():
-            @pl.loop(0, LANES // 16)
+            @pl.loop(0, LANES // 64)
             def _(b):
-                for u in range(16):
-                    row = idx[tile, b * 16 + u]
-                    at = pl.multiple_of(tile * 256 + b * 32, 32) + 2 * u
+                for u in range(64):
+                    row = idx[pl.multiple_of(tile * LANES + b * 64, 64) + u]
+                    at = pl.multiple_of(tile * 256 + b * 128, 128) + 2 * u
                     g[pl.ds(at, 2), :] = tab[pl.ds(row, 2), :]
 
-    @pl.loop(0, TILES // 4)
+    @pl.loop(0, TILES // 8)
     def _(n):
-        for u in range(4):
-            o = pl.multiple_of(n * 4 * LANES + u * LANES, LANES)
+        for u in range(8):
+            o = pl.multiple_of(n * 8 * LANES + u * LANES, LANES)
             here = g[pl.ds(o * 2, LANES, stride=2), :] * wb[0, pl.ds(o, LANES), :]
             here = here + g[pl.ds(o * 2 + 1, LANES, stride=2), :] * wb[1, pl.ds(o, LANES), :]
             turned = here.T
             parts = [turned[8 * k : 8 * k + 8] for k in range(16)]
             while len(parts) > 1:
                 parts = [a + b for a, b in zip(parts[::2], parts[1::2])]
-            send[2 * n + u // 2, u % 2] = parts[0]
+            send[4 * n + u // 2, u % 2] = parts[0]
 
 
 def setup_body(
-    donor_in, recv_in, pairs_in, who, held_in, didx_out, ridx_out, rlane_out, w_out,
-    donor, recv, pairs, held, didx, dpos, ridx, rlane, w, sem,
+    donor_in, recv_in, pairs_in, who, held_in, didx_out, ridx_out, w_out,
+    donor, recv, pairs, held, didx, dpos, ridx, w, sem,
 ):
     c = Copies(sem.at[0])
     c.add(donor_in, donor)
@@ -446,16 +446,15 @@
             cell = recv[s, t : t + 1, :]
             x, y, z = cell >> 13, (cell >> 8) & (CY - 1), cell & (CZ - 1)
             row = (2 * x + (y >> 4)) * CZ + z
-            ridx[i : i + 1, :] = jnp.where(t < live, row, RECV_ROWS)
-            rlane[i : i + 1, :] = y & 15
+            row = jnp.where(t < live, row, RECV_ROWS)
+            ridx[i : i + 1, :] = row * 16 + (y & 15)
     c.add(didx, didx_out)
     c.add(ridx, ridx_out)
-    c.add(rlane, rlane_out)
     d.wait()
 
-    @pl.loop(0, TILES // 2)
-    def _(n):
-        for u in range(2):
+    @pl.loop(0, TILES // 4)
+    def _(m):
+        for n, u in ((2 * m, 0), (2 * m, 1), (2 * m + 1, 0), (2 * m + 1, 1)):
             kpos = lax.broadcasted_iota(I32, (16, LANES), 0)
             base = jnp.broadcast_to(dpos[pl.ds(2 * n + u, 1), :], (16, LANES))
             o = pl.multiple_of(n * 2 * LANES + u * LANES, LANES)
@@ -482,13 +481,12 @@
     pltpu.VMEM((TILES, LANES), I32),
     pltpu.VMEM((TILES, LANES), I32),
     pltpu.VMEM((TILES, LANES), I32),
-    pltpu.VMEM((TILES, LANES), I32),
     pltpu.VMEM((2, POINTS, LANES), F32),
     pltpu.SemaphoreType.DMA((2,)),
 )
 
 
-def scatter_points(vals, ridx, rlane, qb, arrive, loads, f, y0, x0, vrep, u, ut):
+def scatter_points(vals, ridx, qb, arrive, loads, f, y0, x0, vrep, u, ut):
     mark = lax.broadcasted_iota(I32, (8, LANES), 0) == NV
     lane = lax.broadcasted_iota(I32, (1, LANES), 1) >> 3
 
@@ -496,24 +494,22 @@
     def _(i):
         u[pl.ds(pl.multiple_of(i * LANES, LANES), LANES), :] = jnp.zeros((LANES, LANES), F32)
 
-    @pl.loop(0, TILES // 4)
+    @pl.loop(0, TILES // 8)
     def _(n):
-        for k in range(4):
-            v = jnp.where(mark, 1.0, vals[2 * n + k // 2, k % 2])
-            rows = pl.ds(pl.multiple_of(n * 4 * LANES + k * LANES, LANES), LANES)
+        for k in range(8):
+            v = jnp.where(mark, 1.0, vals[4 * n + k // 2, k % 2])
+            rows = pl.ds(pl.multiple_of(n * 8 * LANES + k * LANES, LANES), LANES)
             vrep[rows, :] = jnp.concatenate([v] * 16, axis=0).T
 
     loads.wait()
 
-    @pl.loop(0, TILES)
-    def _(tile):
-        @pl.loop(0, LANES // 16)
-        def _(b):
-            for j in range(16):
-                row = ridx[tile, b * 16 + j]
-                k = rlane[tile, b * 16 + j]
-                at = pl.multiple_of(tile * LANES + b * 16, 16) + j
-                pltpu.store(u.at[pl.ds(row, 1), :], vrep[pl.ds(at, 1), :], mask=lane == k)
+    @pl.loop(0, POINTS // 64)
+    def _(b):
+        for j in range(64):
+            at = pl.multiple_of(b * 64, 64) + j
+            word = ridx[at]
+            mask = (jnp.full((1, LANES), word, I32) & 15) == lane
+            pltpu.store(u.at[pl.ds(word >> 4, 1), :], vrep[pl.ds(at, 1), :], mask=mask)
 
     @pl.loop(0, CX - 1)
     def _(x):
@@ -539,30 +535,28 @@
                         )
 
 
-def scatter_body(q, vals, ridx_in, rlane_in, out, qb, vrep, u, ut, ridx, rlane, sem):
+def scatter_body(q, vals, ridx_in, out, qb, vrep, u, ut, ridx, sem):
     c, e = Copies(sem.at[0]), Copies(sem.at[2])
     e.add(ridx_in, ridx)
-    e.add(rlane_in, rlane)
     c.halves(q, qb, 0)
-    scatter_points(vals, ridx, rlane, qb, c, e, qb, 0, 0, vrep, u, ut)
+    scatter_points(vals, ridx, qb, c, e, qb, 0, 0, vrep, u, ut)
     c.halves_out(qb, out, 0)
     c.wait()
 
 
 def scatter_edge_body(
-    q, vals, ridx_in, rlane_in, now, prev, kap, jh, out, lo, hi, er,
-    qb, vrep, u, ut, ridx, rlane, f, nowb, prevb, kapb, ers, es1, sem,
+    q, vals, ridx_in, now, prev, kap, jh, out, lo, hi, er,
+    qb, vrep, u, ut, ridx, f, nowb, prevb, kapb, ers, es1, sem,
 ):
     c, e = Copies(sem.at[0]), Copies(sem.at[2])
     e.add(ridx_in, ridx)
-    e.add(rlane_in, rlane)
     c.halves(q, qb, 0)
     d = Copies(sem.at[1])
     edge_load(d, now, prev, kap, nowb, prevb, kapb)
     clear_pads(f, 1, 4)
     clear_pads(f, 6, 9)
     edge_zero(f)
-    scatter_points(vals, ridx, rlane, qb, c, e, f, 8, 1, vrep, u, ut)
+    scatter_points(vals, ridx, qb, c, e, f, 8, 1, vrep, u, ut)
     for v in range(NV):
         for h in range(2):
             f[v, CX, h, 8 : 8 + CY, :] = qb[v, CX - 1, h]
@@ -580,8 +574,7 @@
     pltpu.VMEM((POINTS, LANES), F32),
     pltpu.VMEM((RECV_ROWS + 8, LANES), F32),
     pltpu.VMEM((RECV_GROUPS, 2, LANES, LANES), F32),
-    pltpu.SMEM((TILES, LANES), I32),
-    pltpu.SMEM((TILES, LANES), I32),
+    pltpu.SMEM((POINTS,), I32),
 )
 
 
@@ -615,24 +608,26 @@
     )(now, prev, kap, jh)
     state = now
     for sub in range(2):
+        kept = HBM if sub == 0 else ANY
         got_lo = lax.ppermute(hi, "blk", forward)
         got_hi = lax.ppermute(lo, "blk", backward)
         inner = call(
             inner_body, "inner", [rows_of(n) for n in (2, 2, 4, 2)],
-            [HBM] * 4 + [SMEM] + [HBM] * 2, [HBM] * 4,
+            [kept, HBM, HBM, HBM, SMEM, kept, kept], [kept] * 4,
             scratch=INNER_SCRATCH, vmem_mb=14, cost_us=4.0,
         )(state, now, prev, kap, jh, lo, hi)
         if sub == 0:
             weights, _ = lax.optimization_barrier((interp_weight[0, 0], lo))
             held = lax.all_to_all(weights, "comp", split_axis=0, concat_axis=0, tiled=True)
-            didx, ridx, rlane, wide = call(
-                setup_body, "setup", [idx_shape] * 3 + [sds((2, POINTS, LANES))],
-                [HBM] * 3 + [SMEM, ANY], [HBM] * 4, scratch=SETUP_SCRATCH, cost_us=4.0,
+            didx, ridx, wide = call(
+                setup_body, "setup", [idx_shape] * 2 + [sds((2, POINTS, LANES))],
+                [HBM] * 3 + [SMEM, ANY], [HBM] * 3, scratch=SETUP_SCRATCH, cost_us=4.0,
             )(donor_cell[0, 0], recv_cell[0, 0], pairs, who, held)
+            didx, ridx = didx.reshape(-1), ridx.reshape(-1)
         relaxed, send = call(
             finish_body, "finish", [sds(STATE), sds((16, 2, 8, LANES))],
-            [HBM, HBM, SMEM, SMEM] + [HBM] * 4 + [ANY] * 2 + [HBM] * 6, [HBM, VMEM],
-            scratch=FINISH_SCRATCH, vmem_mb=30, cost_us=14.0,
+            [kept, HBM, SMEM, SMEM, HBM, HBM, kept, kept, ANY, ANY, HBM] + [kept] * 5,
+            [ANY, VMEM], scratch=FINISH_SCRATCH, vmem_mb=30, cost_us=14.0,
         )(
             state, kap, jh, who, didx, pairs, lo, hi, got_lo, got_hi, wide,
             er, *inner,
@@ -641,15 +636,15 @@
         if sub == 0:
             state, lo, hi, er = call(
                 scatter_edge_body, "scatter_edge", [sds(STATE)] + messages,
-                [HBM, VMEM, HBM, HBM, HBM, HBM, HBM, SMEM], [HBM] * 4,
+                [ANY, VMEM, HBM, HBM, HBM, HBM, SMEM], [ANY] * 4,
                 scratch=SCATTER_SCRATCH + (field(CX + 2),) + EDGE_SCRATCH + (sems,),
                 vmem_mb=20, cost_us=12.0,
-            )(relaxed, arrived, ridx, rlane, now, prev, kap, jh)
+            )(relaxed, arrived, ridx, now, prev, kap, jh)
         else:
             state = call(
-                scatter_body, "scatter", sds(STATE), [HBM, VMEM, HBM, HBM], HBM,
+                scatter_body, "scatter", sds(STATE), [ANY, VMEM, HBM], HBM,
                 scratch=SCATTER_SCRATCH + (sems,), vmem_mb=12, cost_us=10.0,
-            )(relaxed, arrived, ridx, rlane)
+            )(relaxed, arrived, ridx)
     return state[None]
 
 

time: 158 us -> 133 us (0.84)
  Pallas kernels: 93.9 us -> 69.4 us
  blocking collectives: 29.7 us -> 27.5 us
    pallas_call x8, Pallas kernels: 93.9 us -> 69.4 us  [run(): kernel(*[pltpu.with_memory_space_constraint(a, pltpu.HBM) if spec is HBM...]
    all_to_all x2, blocking collectives: 29.7 us -> 27.5 us  [shards(): lax.all_to_all(send, 'comp', split_axis=0, concat_axis=0, tiled=True)]
  transfers between devices with their start and end apart: 5 -> 5, of which waited for: 3 -> 3; matrix products, arithmetic and copies ran while one was open for 0% -> 0% of each run, Pallas kernels for 13% -> 14%
where the time goes in v2:
time: 133 us; the launch traced here: 132 us
  Pallas kernels  69.4 us (52%)
  blocking collectives  27.5 us (21%)
  starting transfers between devices  22.4 us (17%)
  waiting for transfers between devices  12.2 us (9%)
    pallas_call x8, Pallas kernels, run(): kernel(*[pltpu.with_memory_space_constraint(a, pltpu.HBM) if spec is HBM...  69.4 us
    all_to_all x2, blocking collectives, shards(): lax.all_to_all(send, 'comp', split_axis=0, concat_axis=0, tiled=True)  27.5 us
    all_to_all x1, starting transfers between devices, shards(): lax.all_to_all(weights, 'comp', split_axis=0, concat_axis=0, tiled=True)  9.72 us
    ppermute x2, starting transfers between devices, shards(): got_hi = lax.ppermute(lo, 'blk', backward)  6.77 us
    ppermute x2, waiting for transfers between devices, shards(): got_hi = lax.ppermute(lo, 'blk', backward)  6.07 us
    ppermute x2, starting transfers between devices, shards(): got_lo = lax.ppermute(hi, 'blk', forward)  5.91 us
    ppermute x2, waiting for transfers between devices, shards(): got_lo = lax.ppermute(hi, 'blk', forward)  4.5 us
  transfers between devices with their start and end apart: 5, of which 3 were waited for; matrix products, arithmetic and copies ran while one was open for 0% of the time, Pallas kernels for 14%

profile of v2, /device:TPU:7, one launch (start us, length us, event | category | flops | bytes accessed | tf_op | source)
XLA Modules:
  0.0 132.5 jit_solution(13821511190601423299)
XLA Ops:
  0.0 0.7 multiply_reduce_fusion
  0.7 0.1 mul.12.jh
  0.8 5.5 %edge.1 = (f32[19,32,256]{2,1,0:T(8,128)}, f32[19,32,256]{2,1,0:T(8,128)}, f32[6,2,32,256]{3,2,1,0:T(8,128)}) custom-call(f32[6,8,32,256]{3,2,1,0:T(8,128)} %bitcast.12, f32[6,8,32,256]{3,2,1,0:T(8,128)} %bitcast.18, f32[8,32,256]{2,1,0:T(8,128)} %bitcast.22, f32[108]{0:T(128)S(1)} %mul.12.jh), custom_call_target="tpu_custom_call" | custom-call | bytes 9000000 | tf_op jit(solution)/shard_map/edge/pallas_call | solution.py:56
  6.3 3.2 %collective-permute-start = (f32[19,32,256]{2,1,0:T(8,128)}, f32[19,32,256]{2,1,0:T(8,128)S(1)}, u32[]{:S(2)}, u32[]{:S(2)}) collective-permute-start(f32[19,32,256]{2,1,0:T(8,128)} %get-tuple-element.31.hi.own_hi), channel_id=1, source_target_pairs={{0,1},{1,2},{2,3},{3,4},{4,5},{5,6},{6,7},{7,8},{8,9},{9,10},{10,1... | collective-permute-start | bytes 1867784 | tf_op jit(solution)/shard_map/ppermute | solution.py:612
  9.5 4.2 %collective-permute-start.1 = (f32[19,32,256]{2,1,0:T(8,128)}, f32[19,32,256]{2,1,0:T(8,128)S(1)}, u32[]{:S(2)}, u32[]{:S(2)}) collective-permute-start(f32[19,32,256]{2,1,0:T(8,128)} %get-tuple-element.28.lo.own_lo), channel_id=1, source_target_pairs={{1,0},{2,1},{3,2},{4,3},{5,4},{6,5},{7,6},{8,7},{9,8},{10,9},{11,1... | collective-permute-start | bytes 1867784 | tf_op jit(solution)/shard_map/ppermute | solution.py:613
  13.7 9.7 %all-to-all-start = ((f32[16,2,8,128]{3,2,1,0:T(8,128)}), f32[16,2,8,128]{3,2,1,0:T(8,128)S(1)}, u32[]{:S(2)}, u32[]{:S(2)}) async-start(f32[16,2,8,128]{3,2,1,0:T(8,128)} %bitcast.7), calls=%async_computation | async-start | bytes 262144 | tf_op jit(solution)/shard_map/all_to_all | solution.py:621
  23.4 7.5 %inner.2 = (f32[6,2,32,256]{3,2,1,0:T(8,128)}, f32[6,2,32,256]{3,2,1,0:T(8,128)}, f32[6,4,32,256]{3,2,1,0:T(8,128)}, f32[6,2,32,256]{3,2,1,0:T(8,128)}) custom-call(f32[6,8,32,256]{3,2,1,0:T(8,128)} %bitcast.13, f32[6,8,32,256]{3,2,1,0:T(8,128)} %bitcast.14, f32[6,8,32,256]{3,2,1,0:T(8,128)} %bitcast.19, f32[8,32,256]{2,1,0:T(8,128)} %bitcast.23, ...), custom_call_target="tpu_custom_call" | custom-call | bytes 12000000 | tf_op jit(solution)/shard_map/inner/pallas_call | solution.py:56
  30.9 0.1 pad_add_fusion.who
  31.0 1.6 %all-to-all-done.held_in = f32[16,2,8,128]{3,2,1,0:T(8,128)S(1)} async-done(((f32[16,2,8,128]{3,2,1,0:T(8,128)}), f32[16,2,8,128]{3,2,1,0:T(8,128)S(1)}, u32[]{:S(2)}, u32[]{:S(2)}) %all-to-all-start) | async-done | bytes 131104 | tf_op jit(solution)/shard_map/all_to_all | solution.py:621
  32.6 5.3 %setup.1 = (s32[32,128]{1,0:T(8,128)}, s32[32,128]{1,0:T(8,128)}, f32[2,4096,128]{2,1,0:T(8,128)}) custom-call(s32[16,2,8,128]{3,2,1,0:T(8,128)} %bitcast.28, s32[16,2,128]{2,1,0:T(2,128)} %bitcast.36, s32[16,16]{1,0:T(8,128)} %bitcast.29, s32[3]{0:T(128)S(1)} %pad_add_fusion.who, f32[16,2,8,128]{3,2,1,0:T(8,128)S(1)} %all-to-all-done.held_in), custom_call_target="tpu_custom_call" | custom-call | bytes 12000000 | tf_op jit(solution)/shard_map/setup/pallas_call | solution.py:56
  37.8 0.0 collective-permute-done.got_lo
  37.9 0.0 collective-permute-done.1.got_hi
  37.9 13.8 %finish.2 = (f32[6,8,32,256]{3,2,1,0:T(8,128)S(1)}, f32[16,2,8,128]{3,2,1,0:T(8,128)S(1)}) custom-call(f32[6,8,32,256]{3,2,1,0:T(8,128)} %bitcast.15, f32[8,32,256]{2,1,0:T(8,128)} %bitcast.24, f32[108]{0:T(128)S(1)} %mul.12.jh, s32[3]{0:T(128)S(1)} %pad_add_fusion.who, s32[4096]{0:T(1024)} %bitcast.34, s32[16,16]{1,0:T(8,128)} %bitcast.30, ...), custom_call_target="tpu_custom_call" | custom-call | bytes 42000000 | tf_op jit(solution)/shard_map/finish/pallas_call | solution.py:56
  51.7 14.8 %all_to_all.15.vals = f32[16,2,8,128]{3,2,1,0:T(8,128)S(1)} all-to-all(f32[16,2,8,128]{3,2,1,0:T(8,128)S(1)} %get-tuple-element.39), channel_id=1, replica_groups=mesh['comp'=16,'blk'=16] {'comp'}, dimensions={0} | all-to-all | bytes 262144 | tf_op jit(solution)/shard_map/all_to_all | solution.py:635
  66.5 10.0 %scatter_edge.1 = (f32[6,8,32,256]{3,2,1,0:T(8,128)S(1)}, f32[19,32,256]{2,1,0:T(8,128)S(1)}, f32[19,32,256]{2,1,0:T(8,128)S(1)}, f32[6,2,32,256]{3,2,1,0:T(8,128)S(1)}) custom-call(f32[6,8,32,256]{3,2,1,0:T(8,128)S(1)} %get-tuple-element.38.q, f32[16,2,8,128]{3,2,1,0:T(8,128)S(1)} %all_to_all.15.vals, s32[4096]{0:T(1024)} %bitcast.32, ...), custom_call_target="tpu_custom_call" | custom-call | bytes 36000000 | tf_op jit(solution)/shard_map/scatter_edge/pallas_call | solution.py:56
  76.5 2.6 %collective-permute-start.3 = (f32[19,32,256]{2,1,0:T(8,128)S(1)}, f32[19,32,256]{2,1,0:T(8,128)S(1)}, u32[]{:S(2)}, u32[]{:S(2)}) collective-permute-start(f32[19,32,256]{2,1,0:T(8,128)S(1)} %get-tuple-element.42.lo.own_lo), channel_id=1, source_target_pairs={{1,0},{2,1},{3,2},{4,3},{5,4},{6,5},{7,6},{8,7},{9,8},{10,9},{11,1... | collective-permute-start | bytes 1867784 | tf_op jit(solution)/shard_map/ppermute | solution.py:613
  79.1 2.7 %collective-permute-start.2 = (f32[19,32,256]{2,1,0:T(8,128)S(1)}, f32[19,32,256]{2,1,0:T(8,128)S(1)}, u32[]{:S(2)}, u32[]{:S(2)}) collective-permute-start(f32[19,32,256]{2,1,0:T(8,128)S(1)} %get-tuple-element.43.hi.own_hi), channel_id=1, source_target_pairs={{0,1},{1,2},{2,3},{3,4},{4,5},{5,6},{6,7},{7,8},{8,9},{9,10},{10,1... | collective-permute-start | bytes 1867784 | tf_op jit(solution)/shard_map/ppermute | solution.py:612
  81.8 6.4 %inner.3 = (f32[6,2,32,256]{3,2,1,0:T(8,128)S(1)}, f32[6,2,32,256]{3,2,1,0:T(8,128)S(1)}, f32[6,4,32,256]{3,2,1,0:T(8,128)S(1)}, f32[6,2,32,256]{3,2,1,0:T(8,128)S(1)}) custom-call(f32[6,8,32,256]{3,2,1,0:T(8,128)S(1)} %get-tuple-element.41.q, f32[6,8,32,256]{3,2,1,0:T(8,128)} %bitcast.17, f32[6,8,32,256]{3,2,1,0:T(8,128)} %bitcast.21, ...), custom_call_target="tpu_custom_call" | custom-call | bytes 12000000 | tf_op jit(solution)/shard_map/inner/pallas_call | solution.py:56
  88.3 6.1 %collective-permute-done.3.got_hi = f32[19,32,256]{2,1,0:T(8,128)S(1)} collective-permute-done((f32[19,32,256]{2,1,0:T(8,128)S(1)}, f32[19,32,256]{2,1,0:T(8,128)S(1)}, u32[]{:S(2)}, u32[]{:S(2)}) %collective-permute-start.3) | collective-permute-done | bytes 622624 | tf_op jit(solution)/shard_map/ppermute | solution.py:613
  94.3 4.5 %collective-permute-done.2.got_lo = f32[19,32,256]{2,1,0:T(8,128)S(1)} collective-permute-done((f32[19,32,256]{2,1,0:T(8,128)S(1)}, f32[19,32,256]{2,1,0:T(8,128)S(1)}, u32[]{:S(2)}, u32[]{:S(2)}) %collective-permute-start.2) | collective-permute-done | bytes 622624 | tf_op jit(solution)/shard_map/ppermute | solution.py:612
  98.8 12.7 %finish.3 = (f32[6,8,32,256]{3,2,1,0:T(8,128)S(1)}, f32[16,2,8,128]{3,2,1,0:T(8,128)S(1)}) custom-call(f32[6,8,32,256]{3,2,1,0:T(8,128)S(1)} %get-tuple-element.41.q, f32[8,32,256]{2,1,0:T(8,128)} %bitcast.27, f32[108]{0:T(128)S(1)} %mul.12.jh, s32[3]{0:T(128)S(1)} %pad_add_fusion.who, s32[4096]{0:T(1024)} %bitcast.35, s32[16,16]{1,0:T(8,128)} %bitcast.31, ...), custom_call_target="tpu_custom_call" | custom-call | bytes 42000000 | tf_op jit(solution)/shard_map/finish/pallas_call | solution.py:56
  111.5 12.7 %all_to_all.16.vals = f32[16,2,8,128]{3,2,1,0:T(8,128)S(1)} all-to-all(f32[16,2,8,128]{3,2,1,0:T(8,128)S(1)} %get-tuple-element.50), channel_id=1, replica_groups=mesh['comp'=16,'blk'=16] {'comp'}, dimensions={0} | all-to-all | bytes 262144 | tf_op jit(solution)/shard_map/all_to_all | solution.py:635
  124.2 8.2 %scatter.1 = f32[6,8,32,256]{3,2,1,0:T(8,128)} custom-call(f32[6,8,32,256]{3,2,1,0:T(8,128)S(1)} %get-tuple-element.49.q, f32[16,2,8,128]{3,2,1,0:T(8,128)S(1)} %all_to_all.16.vals, s32[4096]{0:T(1024)} %bitcast.33), custom_call_target="tpu_custom_call" | custom-call | bytes 30000000 | tf_op jit(solution)/shard_map/scatter/pallas_call | solution.py:56
Async XLA Ops:
  6.3 31.6 %collective-permute-start = (f32[19,32,256]{2,1,0:T(8,128)}, f32[19,32,256]{2,1,0:T(8,128)S(1)}, u32[]{:S(2)}, u32[]{:S(2)}) collective-permute-start(f32[19,32,256]{2,1,0:T(8,128)} %get-tuple-element.31.hi.own_hi), channel_id=1, source_target_pairs={{0,1},{1,2},{2,3},{3,4},{4,5},{5,6},{6,7},{7,8},{8,9},{9,10},{10,1... | collective-permute-start | bytes 1867784 | tf_op jit(solution)/shard_map/ppermute | solution.py:612
  9.5 28.4 %collective-permute-start.1 = (f32[19,32,256]{2,1,0:T(8,128)}, f32[19,32,256]{2,1,0:T(8,128)S(1)}, u32[]{:S(2)}, u32[]{:S(2)}) collective-permute-start(f32[19,32,256]{2,1,0:T(8,128)} %get-tuple-element.28.lo.own_lo), channel_id=1, source_target_pairs={{1,0},{2,1},{3,2},{4,3},{5,4},{6,5},{7,6},{8,7},{9,8},{10,9},{11,1... | collective-permute-start | bytes 1867784 | tf_op jit(solution)/shard_map/ppermute | solution.py:613
  13.7 18.9 %all-to-all-start = ((f32[16,2,8,128]{3,2,1,0:T(8,128)}), f32[16,2,8,128]{3,2,1,0:T(8,128)S(1)}, u32[]{:S(2)}, u32[]{:S(2)}) async-start(f32[16,2,8,128]{3,2,1,0:T(8,128)} %bitcast.7), calls=%async_computation | async-start | bytes 262144 | tf_op jit(solution)/shard_map/all_to_all | solution.py:621
  76.5 17.8 %collective-permute-start.3 = (f32[19,32,256]{2,1,0:T(8,128)S(1)}, f32[19,32,256]{2,1,0:T(8,128)S(1)}, u32[]{:S(2)}, u32[]{:S(2)}) collective-permute-start(f32[19,32,256]{2,1,0:T(8,128)S(1)} %get-tuple-element.42.lo.own_lo), channel_id=1, source_target_pairs={{1,0},{2,1},{3,2},{4,3},{5,4},{6,5},{7,6},{8,7},{9,8},{10,9},{11,1... | collective-permute-start | bytes 1867784 | tf_op jit(solution)/shard_map/ppermute | solution.py:613
  79.1 19.7 %collective-permute-start.2 = (f32[19,32,256]{2,1,0:T(8,128)S(1)}, f32[19,32,256]{2,1,0:T(8,128)S(1)}, u32[]{:S(2)}, u32[]{:S(2)}) collective-permute-start(f32[19,32,256]{2,1,0:T(8,128)S(1)} %get-tuple-element.43.hi.own_hi), channel_id=1, source_target_pairs={{0,1},{1,2},{2,3},{3,4},{4,5},{5,6},{6,7},{7,8},{8,9},{9,10},{10,1... | collective-permute-start | bytes 1867784 | tf_op jit(solution)/shard_map/ppermute | solution.py:612

commit v3 on v2

--- a/solution.py
+++ b/solution.py
@@ -31,8 +31,12 @@
     return jax.ShapeDtypeStruct(shape, dtype)
 
 
-def field(rows, pad=PADY):
-    return pltpu.VMEM((NV, rows, 2, pad, LANES), F32)
+def field(rows):
+    return pltpu.VMEM((NV, rows, 2, PADY, LANES), F32)
+
+
+def half_of(h):
+    return pl.ds(LANES * h, LANES)
 
 
 def call(body, name, outs, ins, out_specs, scratch=(), vmem_mb=12, cost_us=1.0):
@@ -70,21 +74,21 @@
         c.start()
         self.list.append(c)
 
-    def halves(self, src, dst, y0=8):
+    def halves(self, src, dst):
         n = len(src.shape) - 2
         for h in range(2):
             full = (slice(None),) * n
             self.add(
                 src.at[full + (slice(None), pl.ds(LANES * h, LANES))],
-                dst.at[full + (h, pl.ds(y0, CY), slice(None))],
+                dst.at[full + (h, pl.ds(8, CY), slice(None))],
             )
 
-    def halves_out(self, src, dst, y0=8):
+    def halves_out(self, src, dst):
         n = len(dst.shape) - 2
         for h in range(2):
             full = (slice(None),) * n
             self.add(
-                src.at[full + (h, pl.ds(y0, CY), slice(None))],
+                src.at[full + (h, pl.ds(8, CY), slice(None))],
                 dst.at[full + (slice(None), pl.ds(LANES * h, LANES))],
             )
 
@@ -135,7 +139,7 @@
 
 def kap_tile(kap, k, t):
     y0 = pl.multiple_of(8 * t, 8)
-    both = [kap[k, h, pl.ds(y0, 8), :] for h in range(2)]
+    both = [kap[k, pl.ds(y0, 8), half_of(h)] for h in range(2)]
     return both, [-1.0 / (PSEUDO_DIAG + 6.0 * b) for b in both]
 
 
@@ -154,9 +158,13 @@
     y0 = pl.multiple_of(8 * t, 8)
     for v in range(NV):
         for h in range(2):
-            past = prev[v, n, h, pl.ds(y0, 8), :] - 4.0 * now[v, n, h, pl.ds(y0, 8), :]
             c = centres[v][h]
-            r = 0.5 * (3.0 * c + past) + acc[v][h] + (6.0 * kp[h]) * c
+            past = prev[v, n, pl.ds(y0, 8), half_of(h)]
+            if now is None:
+                own = 0.5 * (past - c)
+            else:
+                own = 0.5 * (3.0 * c + (past - 4.0 * now[v, n, pl.ds(y0, 8), half_of(h)]))
+            r = own + acc[v][h] + (6.0 * kp[h]) * c
             emit(v, h, r, r * ninv[h])
 
 
@@ -166,36 +174,38 @@
     y0 = pl.multiple_of(8 * t, 8)
     for v in range(NV):
         for h in range(2):
-            emit(v, h, (rs[v, ra, h, pl.ds(y0, 8), :] + acc[v][h]) * ninv[h])
-
-
-def edge_rows(f, kap, now, prev, jh, ers, es1):
+            emit(v, h, (rs[v, ra, pl.ds(y0, 8), half_of(h)] + acc[v][h]) * ninv[h])
+
+
+def edge_rows(side, f, kap, now, prev, jh, ers, es1):
     def body(i, row, t):
         y0 = pl.multiple_of(8 * t, 8)
+        at = i + 2 * side
 
         def emit(v, h, r, s):
-            ers[v, i, h, pl.ds(y0, 8), :] = r
-            es1[v, i, h, pl.ds(y0, 8), :] = s
-
-        start_row(f, row + 1, kap, i, now, prev, i, t, jh, emit)
-
-    each_tile(4, lambda i: i + 4 * (i // 2), body)
-
-
-def edge_load(c, now, prev, kap, nowb, prevb, kapb):
-    for i, x in ((0, 0), (2, 6)):
-        c.halves(now.at[:, pl.ds(x, 2)], nowb.at[:, pl.ds(i, 2)], 0)
-        c.halves(prev.at[:, pl.ds(x, 2)], prevb.at[:, pl.ds(i, 2)], 0)
-        c.halves(kap.at[pl.ds(x, 2)], kapb.at[pl.ds(i, 2)], 0)
-
-
-def edge_send(c, f, kap, ers, es1, lo, hi, er):
-    for i, msg, row in ((0, lo, 0), (3, hi, CX - 1)):
-        c.halves_out(f.at[:, row + 1], msg.at[pl.ds(0, NV)])
-        c.halves_out(ers.at[:, i], msg.at[pl.ds(NV, NV)], 0)
-        c.halves_out(es1.at[:, 1 + i // 3], msg.at[pl.ds(2 * NV, NV)], 0)
-        c.halves_out(kap.at[i], msg.at[3 * NV], 0)
-    c.halves_out(ers.at[:, pl.ds(1, 2)], er, 0)
+            ers[v, at, pl.ds(y0, 8), half_of(h)] = r
+            es1[v, at, pl.ds(y0, 8), half_of(h)] = s
+
+        start_row(f, row + 1, kap, at, now, prev, at, t, jh, emit)
+
+    each_tile(2, lambda i: i + 6 * side, body)
+
+
+def edge_load(c, side, now, prev, kap, nowb, prevb, kapb):
+    x, i = 6 * side, 2 * side
+    if nowb is not None:
+        c.add(now.at[:, pl.ds(x, 2)], nowb.at[:, pl.ds(i, 2)])
+    c.add(prev.at[:, pl.ds(x, 2)], prevb.at[:, pl.ds(i, 2)])
+    c.add(kap.at[pl.ds(x, 2)], kapb.at[pl.ds(i, 2)])
+
+
+def edge_send(c, side, f, kap, ers, es1, msg, er):
+    outer, inner = 3 * side, 1 + side
+    c.halves_out(f.at[:, 1 + (CX - 1) * side], msg.at[pl.ds(0, NV)])
+    c.add(ers.at[:, outer], msg.at[pl.ds(NV, NV)])
+    c.add(es1.at[:, inner], msg.at[pl.ds(2 * NV, NV)])
+    c.add(kap.at[outer], msg.at[3 * NV])
+    c.add(ers.at[:, inner], er.at[:, side])
 
 
 def edge_zero(f):
@@ -208,51 +218,63 @@
 
 
 EDGE_SCRATCH = (
-    field(4, CY), field(4, CY), pltpu.VMEM((4, 2, CY, LANES), F32),
-    field(4, CY), field(4, CY),
+    pltpu.VMEM((NV, 4, CY, CZ), F32), pltpu.VMEM((NV, 4, CY, CZ), F32), pltpu.VMEM((4, CY, CZ), F32),
+    pltpu.VMEM((NV, 4, CY, CZ), F32), pltpu.VMEM((NV, 4, CY, CZ), F32),
 )
 
 
 def edge_body(now, prev, kap, jh, lo, hi, er, f, nowb, prevb, kapb, ers, es1, sem):
-    c = Copies(sem.at[0])
-    for x in (0, 5):
-        c.halves(now.at[:, pl.ds(x, 3)], f.at[:, pl.ds(x + 1, 3)])
-    edge_load(c, now, prev, kap, nowb, prevb, kapb)
+    groups = []
+    for side in range(2):
+        c = Copies(sem.at[side])
+        c.halves(now.at[:, pl.ds(5 * side, 3)], f.at[:, pl.ds(5 * side + 1, 3)])
+        edge_load(c, side, now, prev, kap, None, prevb, kapb)
+        groups.append(c)
     clear_pads(f, 1, 4)
     clear_pads(f, 6, 9)
     edge_zero(f)
-    c.wait()
-    edge_rows(f, kapb, nowb, prevb, jh, ers, es1)
-    edge_send(c, f, kapb, ers, es1, lo, hi, er)
-    c.wait()
+    for side, msg in ((0, lo), (1, hi)):
+        groups[side].wait()
+        edge_rows(side, f, kapb, None, prevb, jh, ers, es1)
+        edge_send(groups[side], side, f, kapb, ers, es1, msg, er)
+    for c in groups:
+        c.wait()
 
 
 def inner_body(
     q, now, prev, kap, jh, lo, hi, rs_out, s1_out, s2_out, s3_out,
-    f, nowb, prevb, kapb, rs, s1, s2, s3, sem,
+    f, nowb, prevb, kapb, rs, s1, s2, s3, sem, later=True,
 ):
-    c = Copies(sem.at[0])
-    c.halves(q.at[:, pl.ds(1, 6)], f)
-    c.halves(now.at[:, pl.ds(2, 4)], nowb, 0)
-    c.halves(prev.at[:, pl.ds(2, 4)], prevb, 0)
-    c.halves(kap.at[pl.ds(2, 4)], kapb, 0)
+    groups = []
+    for k, x, n in ((0, 1, 4), (1, 5, 2)):
+        c = Copies(sem.at[k])
+        c.halves(q.at[:, pl.ds(x, n)], f.at[:, pl.ds(x - 1, n)])
+        rows = pl.ds(2 + 2 * k, 2)
+        if later:
+            c.add(now.at[:, rows], nowb.at[:, pl.ds(2 * k, 2)])
+        c.add(prev.at[:, rows], prevb.at[:, pl.ds(2 * k, 2)])
+        c.add(kap.at[rows], kapb.at[pl.ds(2 * k, 2)])
+        groups.append(c)
+    c = groups[1]
     c.halves(lo.at[pl.ds(2 * NV, NV)], s1.at[:, 0])
     c.halves(hi.at[pl.ds(2 * NV, NV)], s1.at[:, 5])
     clear_pads(f, 1, 5)
     clear_pads(s1, 1, 5)
     clear_pads(s2, 1, 3)
-    c.wait()
 
     def first(i, row, t):
         def emit(v, h, r, s):
-            rs[v, i, h, pl.ds(pl.multiple_of(8 * t, 8), 8), :] = r
-            s1[v, i + 1, h, pl.ds(pl.multiple_of(8 * t + 8, 8), 8), :] = s
-
-        start_row(f, i + 1, kapb, i, nowb, prevb, i, t, jh, emit)
-
-    each_tile(4, lambda i: i, first)
+            rs[v, row, pl.ds(pl.multiple_of(8 * t, 8), 8), half_of(h)] = r
+            s1[v, row + 1, h, pl.ds(pl.multiple_of(8 * t + 8, 8), 8), :] = s
+
+        start_row(f, row + 1, kapb, row, nowb if later else None, prevb, row, t, jh, emit)
+
+    groups[0].wait()
+    each_tile(2, lambda i: i, first)
+    groups[1].wait()
+    each_tile(2, lambda i: i + 2, first)
     for i in range(2):
-        c.halves_out(rs.at[:, 3 * i], rs_out.at[:, i], 0)
+        c.add(rs.at[:, 3 * i], rs_out.at[:, i])
         c.halves_out(s1.at[:, 3 * i + 1], s1_out.at[:, i])
 
     def second(i, row, t):
@@ -266,18 +288,18 @@
 
     def third(i, row, t):
         def emit(v, h, val):
-            s3[v, i, h, pl.ds(pl.multiple_of(8 * t, 8), 8), :] = val
+            s3[v, i, pl.ds(pl.multiple_of(8 * t, 8), 8), half_of(h)] = val
 
         relax_row(s2, i + 1, rs, i + 1, kapb, i + 1, t, jh, emit)
 
     each_tile(2, lambda i: i, third)
-    c.halves_out(s3, s3_out, 0)
+    c.add(s3, s3_out)
     c.wait()
 
 
 INNER_SCRATCH = (
-    field(6), field(4, CY), field(4, CY), pltpu.VMEM((4, 2, CY, LANES), F32),
-    field(4, CY), field(6), field(4), field(2, CY), pltpu.SemaphoreType.DMA((1,)),
+    field(6), pltpu.VMEM((NV, 4, CY, CZ), F32), pltpu.VMEM((NV, 4, CY, CZ), F32), pltpu.VMEM((4, CY, CZ), F32),
+    pltpu.VMEM((NV, 4, CY, CZ), F32), field(6), field(4), pltpu.VMEM((NV, 2, CY, CZ), F32), pltpu.SemaphoreType.DMA((2,)),
 )
 
 
@@ -288,13 +310,13 @@
         scale = jnp.where(i == 0, lo_ok, jnp.where(i == 3, hi_ok, 1.0))
         kp, ninv = kap_tile(kape, row + 1, t)
         for h in range(2):
-            side = [far[w, i, h, pl.ds(y0, 8), :] for w in range(NV)]
+            side = [far[w, i, pl.ds(y0, 8), half_of(h)] for w in range(NV)]
             turned = [side[w] * sign for w in range(NV)]
             for v in range(NV):
-                r = rse[v, row + 1, h, pl.ds(y0, 8), :] - kp[h] * side[v]
+                r = rse[v, row + 1, pl.ds(y0, 8), half_of(h)] - kp[h] * side[v]
                 for w in range(NV):
                     r = r + jh[v * 6 + w] * turned[w]
-                rse[v, row + 1, h, pl.ds(y0, 8), :] = r
+                rse[v, row + 1, pl.ds(y0, 8), half_of(h)] = r
                 s1e[v, row + 2, h, pl.ds(pl.multiple_of(y0 + 8, 8), 8), :] = r * (ninv[h] * scale)
 
     each_tile(4, lambda i: i - 1 + 6 * (i // 2), body)
@@ -307,25 +329,23 @@
 ):
     lo_ok = jnp.where(who[1] > 0, 1.0, 0.0).astype(F32)
     hi_ok = jnp.where(who[1] < who[2] - 1, 1.0, 0.0).astype(F32)
-    c = Copies(sem.at[0])
-    c.halves(kap, kape.at[pl.ds(1, CX)], 0)
-    c.halves(got_lo.at[3 * NV], kape.at[0], 0)
-    c.halves(got_hi.at[3 * NV], kape.at[CX + 1], 0)
+    c, d, e, k = (Copies(sem.at[n]) for n in range(4))
     for i, msg in ((0, own_lo), (1, got_lo), (2, got_hi), (3, own_hi)):
-        c.halves(msg.at[pl.ds(0, NV)], far.at[:, i], 0)
+        c.add(msg.at[pl.ds(0, NV)], far.at[:, i])
     for x, msg in ((0, got_lo), (1, own_lo), (8, own_hi), (9, got_hi)):
-        c.halves(msg.at[pl.ds(NV, NV)], rse.at[:, x], 0)
+        c.add(msg.at[pl.ds(NV, NV)], rse.at[:, x])
+    c.add(kap, kape.at[pl.ds(1, CX)])
+    c.add(got_lo.at[3 * NV], kape.at[0])
+    c.add(got_hi.at[3 * NV], kape.at[CX + 1])
     for x, msg in ((0, got_lo), (3, own_lo), (8, own_hi), (11, got_hi)):
-        c.halves(msg.at[pl.ds(2 * NV, NV)], s1e.at[:, x])
+        k.halves(msg.at[pl.ds(2 * NV, NV)], s1e.at[:, x])
     for i, (r, s) in enumerate(((2, 4), (7, 7))):
-        c.halves(er.at[:, i], rse.at[:, r], 0)
-        c.halves(rs_in.at[:, i], rse.at[:, (3, 6)[i]], 0)
-        c.halves(s1_in.at[:, i], s1e.at[:, s])
-    c.halves(s2_in, s2e.at[:, pl.ds(3, 4)])
-    d = Copies(sem.at[1])
-    d.halves(q, qb, 0)
-    d.halves(s3_in, s3, 0)
-    e = Copies(sem.at[2])
+        k.add(er.at[:, i], rse.at[:, r])
+        k.add(rs_in.at[:, i], rse.at[:, (3, 6)[i]])
+        k.halves(s1_in.at[:, i], s1e.at[:, s])
+    d.halves(s2_in, s2e.at[:, pl.ds(3, 4)])
+    d.add(q, qb)
+    d.add(s3_in, s3)
     e.add(w_in, wb)
     e.add(idx_in, idx)
     e.add(pairs_in, pairs)
@@ -336,6 +356,7 @@
     c.wait()
 
     fix_rows(rse, s1e, far, kape, jh, lo_ok, hi_ok)
+    k.wait()
 
     def second(i, row, t):
         scale = jnp.where(i == 0, lo_ok, jnp.where(i == 5, hi_ok, 1.0))
@@ -349,12 +370,12 @@
     d.wait()
 
     def put(row, v, h, t, val):
-        qb[v, row, h, pl.ds(pl.multiple_of(8 * t, 8), 8), :] = val
+        qb[v, row, pl.ds(pl.multiple_of(8 * t, 8), 8), half_of(h)] = val
         q8[row, h, pl.ds(64 * t + v, 8, stride=8), :] = val
 
     def third(i, row, t):
         def emit(v, h, val):
-            put(row, v, h, t, qb[v, row, h, pl.ds(pl.multiple_of(8 * t, 8), 8), :] + val)
+            put(row, v, h, t, qb[v, row, pl.ds(pl.multiple_of(8 * t, 8), 8), half_of(h)] + val)
 
         relax_row(s2e, row + 1, rse, row + 1, kape, row + 1, t, jh, emit)
 
@@ -364,24 +385,24 @@
         y0 = pl.multiple_of(8 * t, 8)
         for v in range(NV):
             for h in range(2):
-                put(row, v, h, t, qb[v, row, h, pl.ds(y0, 8), :] + s3[v, i, h, pl.ds(y0, 8), :])
+                put(row, v, h, t, qb[v, row, pl.ds(y0, 8), half_of(h)] + s3[v, i, pl.ds(y0, 8), half_of(h)])
 
     each_tile(2, lambda i: i + 3, rest)
-    d.halves_out(qb, qn, 0)
+    d.add(qb, qn)
     gather_points(idx, pairs, who[0], wb, e, send, q8, tab, g)
     d.wait()
 
 
 FINISH_SCRATCH = (
-    field(CX + 2, CY), field(CX + 4), field(CX + 2), pltpu.VMEM((CX + 2, 2, CY, LANES), F32),
-    field(4, CY), field(CX, CY), field(2, CY),
+    pltpu.VMEM((NV, CX + 2, CY, CZ), F32), field(CX + 4), field(CX + 2), pltpu.VMEM((CX + 2, CY, CZ), F32),
+    pltpu.VMEM((NV, 4, CY, CZ), F32), pltpu.VMEM((NV, CX, CY, CZ), F32), pltpu.VMEM((NV, 2, CY, CZ), F32),
     pltpu.VMEM((CX, 2, 8 * CY, LANES), F32),
     pltpu.VMEM((DONOR_ROWS + 8, LANES), F32),
     pltpu.VMEM((2 * POINTS, LANES), F32),
     pltpu.VMEM((2, POINTS, LANES), F32),
     pltpu.SMEM((POINTS,), I32),
     pltpu.SMEM((16, 16), I32),
-    pltpu.SemaphoreType.DMA((3,)),
+    pltpu.SemaphoreType.DMA((4,)),
 )
 
 
@@ -452,23 +473,29 @@
     c.add(ridx, ridx_out)
     d.wait()
 
-    @pl.loop(0, TILES // 4)
-    def _(m):
-        for n, u in ((2 * m, 0), (2 * m, 1), (2 * m + 1, 0), (2 * m + 1, 1)):
-            kpos = lax.broadcasted_iota(I32, (16, LANES), 0)
-            base = jnp.broadcast_to(dpos[pl.ds(2 * n + u, 1), :], (16, LANES))
-            o = pl.multiple_of(n * 2 * LANES + u * LANES, LANES)
-            for l in range(2):
-                grid = jnp.zeros((16, LANES), F32)
-                for i in range(2):
-                    for j in range(2):
-                        k = 4 * i + 2 * j + l
-                        row = jnp.broadcast_to(held[n, u, k : k + 1, :], (16, LANES))
-                        grid = jnp.where(kpos == base + (4 * i + j), row, grid)
-                wide = [jnp.broadcast_to(grid[k : k + 1], (8, LANES)) for k in range(16)]
-                w[l, pl.ds(o, LANES), :] = jnp.concatenate(wide, axis=0).T
-
-    d.add(w, w_out)
+    def weigh(tile, u):
+        kpos = lax.broadcasted_iota(I32, (16, LANES), 0)
+        base = jnp.broadcast_to(dpos[pl.ds(tile, 1), :], (16, LANES))
+        o = pl.multiple_of(tile * LANES, LANES)
+        for l in range(2):
+            grid = jnp.zeros((16, LANES), F32)
+            for i in range(2):
+                for j in range(2):
+                    k = 4 * i + 2 * j + l
+                    row = jnp.broadcast_to(held[tile // 2, u, k : k + 1, :], (16, LANES))
+                    grid = jnp.where(kpos == base + (4 * i + j), row, grid)
+            wide = [jnp.broadcast_to(grid[k : k + 1], (8, LANES)) for k in range(16)]
+            w[l, pl.ds(o, LANES), :] = jnp.concatenate(wide, axis=0).T
+
+    for part in range(4):
+
+        @pl.loop(0, TILES // 16)
+        def _(m):
+            for u in range(4):
+                weigh(part * (TILES // 4) + 4 * m + u, u % 2)
+
+        rows = pl.ds(part * (POINTS // 4), POINTS // 4)
+        d.add(w.at[:, rows], w_out.at[:, rows])
     c.wait()
     d.wait()
 
@@ -486,7 +513,7 @@
 )
 
 
-def scatter_points(vals, ridx, qb, arrive, loads, f, y0, x0, vrep, u, ut):
+def scatter_points(vals, ridx, qb, arrive, loads, write, vrep, u, ut, half=None):
     mark = lax.broadcasted_iota(I32, (8, LANES), 0) == NV
     lane = lax.broadcasted_iota(I32, (1, LANES), 1) >> 3
 
@@ -520,8 +547,7 @@
 
     arrive.wait()
 
-    @pl.loop(0, CX - 1)
-    def _(x):
+    def merge(x):
         for yh in range(2):
             for h in range(2):
                 for t in range(2):
@@ -530,17 +556,28 @@
                     y = 16 * yh + 8 * t
                     for v in range(NV):
                         new = part[pl.ds(64 * t + v, 8, stride=8), :]
-                        f[v, x + x0, h, y0 + y : y0 + y + 8, :] = jnp.where(
-                            hit, new, qb[v, x, h, y : y + 8, :]
-                        )
+                        old = qb[v, x, y : y + 8, half_of(h)]
+                        write(v, x, h, y, jnp.where(hit, new, old))
+
+    pl.loop(0, 4)(merge)
+    if half is not None:
+        half()
+    pl.loop(4, CX - 1)(merge)
 
 
 def scatter_body(q, vals, ridx_in, out, qb, vrep, u, ut, ridx, sem):
     c, e = Copies(sem.at[0]), Copies(sem.at[2])
     e.add(ridx_in, ridx)
-    c.halves(q, qb, 0)
-    scatter_points(vals, ridx, qb, c, e, qb, 0, 0, vrep, u, ut)
-    c.halves_out(qb, out, 0)
+    c.add(q, qb)
+
+    def write(v, x, h, y, val):
+        qb[v, x, y : y + 8, half_of(h)] = val
+
+    def half():
+        c.add(qb.at[:, pl.ds(0, 4)], out.at[:, pl.ds(0, 4)])
+
+    scatter_points(vals, ridx, qb, c, e, write, vrep, u, ut, half)
+    c.add(qb.at[:, pl.ds(4, 4)], out.at[:, pl.ds(4, 4)])
     c.wait()
 
 
@@ -550,27 +587,33 @@
 ):
     c, e = Copies(sem.at[0]), Copies(sem.at[2])
     e.add(ridx_in, ridx)
-    c.halves(q, qb, 0)
+    c.add(q, qb)
     d = Copies(sem.at[1])
-    edge_load(d, now, prev, kap, nowb, prevb, kapb)
+    for side in range(2):
+        edge_load(d, side, now, prev, kap, nowb, prevb, kapb)
     clear_pads(f, 1, 4)
     clear_pads(f, 6, 9)
     edge_zero(f)
-    scatter_points(vals, ridx, qb, c, e, f, 8, 1, vrep, u, ut)
+
+    def write(v, x, h, y, val):
+        f[v, x + 1, h, 8 + y : 16 + y, :] = val
+
+    scatter_points(vals, ridx, qb, c, e, write, vrep, u, ut)
     for v in range(NV):
         for h in range(2):
-            f[v, CX, h, 8 : 8 + CY, :] = qb[v, CX - 1, h]
+            f[v, CX, h, 8 : 8 + CY, :] = qb[v, CX - 1, :, half_of(h)]
     c.halves_out(f.at[:, pl.ds(1, CX)], out)
     d.wait()
-    edge_rows(f, kapb, nowb, prevb, jh, ers, es1)
-    edge_send(d, f, kapb, ers, es1, lo, hi, er)
+    for side, msg in ((0, lo), (1, hi)):
+        edge_rows(side, f, kapb, nowb, prevb, jh, ers, es1)
+        edge_send(d, side, f, kapb, ers, es1, msg, er)
     d.wait()
     c.wait()
 
 
 STATE = (NV, CX, CY, CZ)
 SCATTER_SCRATCH = (
-    field(CX, CY),
+    pltpu.VMEM((NV, CX, CY, CZ), F32),
     pltpu.VMEM((POINTS, LANES), F32),
     pltpu.VMEM((RECV_ROWS + 8, LANES), F32),
     pltpu.VMEM((RECV_GROUPS, 2, LANES, LANES), F32),
@@ -602,23 +645,22 @@
     idx_shape = sds((TILES, LANES), I32)
     sems = pltpu.SemaphoreType.DMA((3,))
 
+    held = lax.all_to_all(interp_weight[0, 0], "comp", split_axis=0, concat_axis=0, tiled=True)
+    jh, held = lax.optimization_barrier((jh, held))
     lo, hi, er = call(
-        edge_body, "edge", messages, [HBM] * 3 + [SMEM], [HBM] * 3,
+        edge_body, "edge", messages, [HBM] * 3 + [SMEM], [ANY] * 3,
         scratch=(field(CX + 2),) + EDGE_SCRATCH + (sems,), cost_us=3.0,
     )(now, prev, kap, jh)
     state = now
     for sub in range(2):
-        kept = HBM if sub == 0 else ANY
         got_lo = lax.ppermute(hi, "blk", forward)
         got_hi = lax.ppermute(lo, "blk", backward)
         inner = call(
-            inner_body, "inner", [rows_of(n) for n in (2, 2, 4, 2)],
-            [kept, HBM, HBM, HBM, SMEM, kept, kept], [kept] * 4,
+            functools.partial(inner_body, later=sub > 0), "inner", [rows_of(n) for n in (2, 2, 4, 2)],
+            [HBM if sub == 0 else ANY, HBM, HBM, HBM, SMEM, ANY, ANY], [ANY] * 4,
             scratch=INNER_SCRATCH, vmem_mb=14, cost_us=4.0,
         )(state, now, prev, kap, jh, lo, hi)
         if sub == 0:
-            weights, _ = lax.optimization_barrier((interp_weight[0, 0], lo))
-            held = lax.all_to_all(weights, "comp", split_axis=0, concat_axis=0, tiled=True)
             didx, ridx, wide = call(
                 setup_body, "setup", [idx_shape] * 2 + [sds((2, POINTS, LANES))],
                 [HBM] * 3 + [SMEM, ANY], [HBM] * 3, scratch=SETUP_SCRATCH, cost_us=4.0,
@@ -626,7 +668,7 @@
             didx, ridx = didx.reshape(-1), ridx.reshape(-1)
         relaxed, send = call(
             finish_body, "finish", [sds(STATE), sds((16, 2, 8, LANES))],
-            [kept, HBM, SMEM, SMEM, HBM, HBM, kept, kept, ANY, ANY, HBM] + [kept] * 5,
+            [HBM if sub == 0 else ANY, HBM, SMEM, SMEM, HBM, HBM] + [ANY] * 4 + [HBM] + [ANY] * 5,
             [ANY, VMEM], scratch=FINISH_SCRATCH, vmem_mb=30, cost_us=14.0,
         )(
             state, kap, jh, who, didx, pairs, lo, hi, got_lo, got_hi, wide,

time: 133 us -> 139 us (1.045)
  waiting for transfers between devices: 12.2 us -> 25.5 us
  Pallas kernels: 69.4 us -> 65.8 us
  blocking collectives: 27.5 us -> 24.5 us
    all_to_all x1, waiting for transfers between devices: 1.59 us -> 8.35 us  [shards(): lax.all_to_all(interp_weight[0, 0], 'comp', split_axis=0, concat_axis=0,...]
    ppermute x2, waiting for transfers between devices: 4.5 us -> 10.1 us  [shards(): got_lo = lax.ppermute(hi, 'blk', forward)]
    pallas_call x8, Pallas kernels: 69.4 us -> 65.8 us  [run(): kernel(*[pltpu.with_memory_space_constraint(a, pltpu.HBM) if spec is HBM...]
    all_to_all x2, blocking collectives: 27.5 us -> 24.5 us  [shards(): lax.all_to_all(send, 'comp', split_axis=0, concat_axis=0, tiled=True)]
  transfers between devices with their start and end apart: 5 -> 5, of which waited for: 3 -> 5; matrix products, arithmetic and copies ran while one was open for 0% -> 1% of each run, Pallas kernels for 14% -> 12%
where the time goes in v3:
time: 139 us; the launch traced here: 138 us
  Pallas kernels  65.8 us (47%)
  waiting for transfers between devices  25.5 us (18%)
  blocking collectives  24.5 us (18%)
  starting transfers between devices  21.3 us (15%)
    pallas_call x8, Pallas kernels, run(): kernel(*[pltpu.with_memory_space_constraint(a, pltpu.HBM) if spec is HBM...  65.8 us
    all_to_all x2, blocking collectives, shards(): lax.all_to_all(send, 'comp', split_axis=0, concat_axis=0, tiled=True)  24.5 us
    ppermute x2, waiting for transfers between devices, shards(): got_lo = lax.ppermute(hi, 'blk', forward)  10.1 us
    all_to_all x1, starting transfers between devices, shards(): lax.all_to_all(interp_weight[0, 0], 'comp', split_axis=0, concat_axis=0,...  9.15 us
    all_to_all x1, waiting for transfers between devices, shards(): lax.all_to_all(interp_weight[0, 0], 'comp', split_axis=0, concat_axis=0,...  8.35 us
    ppermute x2, waiting for transfers between devices, shards(): got_hi = lax.ppermute(lo, 'blk', backward)  7.07 us
    ppermute x2, starting transfers between devices, shards(): got_hi = lax.ppermute(lo, 'blk', backward)  6.83 us
    ppermute x2, starting transfers between devices, shards(): got_lo = lax.ppermute(hi, 'blk', forward)  5.28 us
  transfers between devices with their start and end apart: 5, of which 5 were waited for; matrix products, arithmetic and copies ran while one was open for 1% of the time, Pallas kernels for 12%

profile of v3, /device:TPU:7, one launch (start us, length us, event | category | flops | bytes accessed | tf_op | source)
XLA Modules:
  0.0 138.1 jit_solution(18103764651492864759)
XLA Ops:
  0.0 9.2 %all-to-all-start = ((f32[16,2,8,128]{3,2,1,0:T(8,128)}), f32[16,2,8,128]{3,2,1,0:T(8,128)S(1)}, u32[]{:S(2)}, u32[]{:S(2)}) async-start(f32[16,2,8,128]{3,2,1,0:T(8,128)} %bitcast.28), calls=%async_computation | async-start | bytes 262144 | tf_op jit(solution)/shard_map/all_to_all | solution.py:648
  9.2 0.7 multiply_reduce_fusion
  9.9 0.1 mul.12.jh
  10.0 8.3 %all-to-all-done.held_in = f32[16,2,8,128]{3,2,1,0:T(8,128)S(1)} async-done(((f32[16,2,8,128]{3,2,1,0:T(8,128)}), f32[16,2,8,128]{3,2,1,0:T(8,128)S(1)}, u32[]{:S(2)}, u32[]{:S(2)}) %all-to-all-start) | async-done | bytes 131104 | tf_op jit(solution)/shard_map/all_to_all | solution.py:648
  18.3 4.0 %edge.1 = (f32[19,32,256]{2,1,0:T(8,128)S(1)}, f32[19,32,256]{2,1,0:T(8,128)S(1)}, f32[6,2,32,256]{3,2,1,0:T(8,128)S(1)}) custom-call(f32[6,8,32,256]{3,2,1,0:T(8,128)} %bitcast.12, f32[6,8,32,256]{3,2,1,0:T(8,128)} %bitcast.18, f32[8,32,256]{2,1,0:T(8,128)} %bitcast.22, f32[108]{0:T(128)S(1)} %mul.12.jh), custom_call_target="tpu_custom_call" | custom-call | bytes 9000000 | tf_op jit(solution)/shard_map/edge/pallas_call | solution.py:60
  22.3 4.9 %collective-permute-start.1 = (f32[19,32,256]{2,1,0:T(8,128)S(1)}, f32[19,32,256]{2,1,0:T(8,128)S(1)}, u32[]{:S(2)}, u32[]{:S(2)}) collective-permute-start(f32[19,32,256]{2,1,0:T(8,128)S(1)} %get-tuple-element.32.lo.own_lo), channel_id=1, source_target_pairs={{1,0},{2,1},{3,2},{4,3},{5,4},{6,5},{7,6},{8,7},{9,8},{10,9},{11,1... | collective-permute-start | bytes 1867784 | tf_op jit(solution)/shard_map/ppermute | solution.py:657
  27.2 1.9 %collective-permute-start = (f32[19,32,256]{2,1,0:T(8,128)S(1)}, f32[19,32,256]{2,1,0:T(8,128)S(1)}, u32[]{:S(2)}, u32[]{:S(2)}) collective-permute-start(f32[19,32,256]{2,1,0:T(8,128)S(1)} %get-tuple-element.33.hi.own_hi), channel_id=1, source_target_pairs={{0,1},{1,2},{2,3},{3,4},{4,5},{5,6},{6,7},{7,8},{8,9},{9,10},{10,1... | collective-permute-start | bytes 1867784 | tf_op jit(solution)/shard_map/ppermute | solution.py:656
  29.2 0.1 pad_add_fusion.who
  29.3 6.4 %inner.2 = (f32[6,2,32,256]{3,2,1,0:T(8,128)S(1)}, f32[6,2,32,256]{3,2,1,0:T(8,128)S(1)}, f32[6,4,32,256]{3,2,1,0:T(8,128)S(1)}, f32[6,2,32,256]{3,2,1,0:T(8,128)S(1)}) custom-call(f32[6,8,32,256]{3,2,1,0:T(8,128)} %bitcast.13, f32[6,8,32,256]{3,2,1,0:T(8,128)} %bitcast.14, f32[6,8,32,256]{3,2,1,0:T(8,128)} %bitcast.19, f32[8,32,256]{2,1,0:T(8,128)} %bitcast.23, ...), custom_call_target="tpu_custom_call" | custom-call | bytes 12000000 | tf_op jit(solution)/shard_map/inner/pallas_call | solution.py:60
  35.6 4.3 %setup.1 = (s32[32,128]{1,0:T(8,128)}, s32[32,128]{1,0:T(8,128)}, f32[2,4096,128]{2,1,0:T(8,128)}) custom-call(s32[16,2,8,128]{3,2,1,0:T(8,128)} %bitcast.29, s32[16,2,128]{2,1,0:T(2,128)} %bitcast.37, s32[16,16]{1,0:T(8,128)} %bitcast.30, s32[3]{0:T(128)S(1)} %pad_add_fusion.who, f32[16,2,8,128]{3,2,1,0:T(8,128)S(1)} %all-to-all-done.held_in), custom_call_target="tpu_custom_call" | custom-call | bytes 12000000 | tf_op jit(solution)/shard_map/setup/pallas_call | solution.py:60
  39.9 1.0 collective-permute-done.1.got_hi
  40.9 6.0 %collective-permute-done.got_lo = f32[19,32,256]{2,1,0:T(8,128)S(1)} collective-permute-done((f32[19,32,256]{2,1,0:T(8,128)S(1)}, f32[19,32,256]{2,1,0:T(8,128)S(1)}, u32[]{:S(2)}, u32[]{:S(2)}) %collective-permute-start) | collective-permute-done | bytes 622624 | tf_op jit(solution)/shard_map/ppermute | solution.py:656
  47.0 13.3 %finish.2 = (f32[6,8,32,256]{3,2,1,0:T(8,128)S(1)}, f32[16,2,8,128]{3,2,1,0:T(8,128)S(1)}) custom-call(f32[6,8,32,256]{3,2,1,0:T(8,128)} %bitcast.15, f32[8,32,256]{2,1,0:T(8,128)} %bitcast.24, f32[108]{0:T(128)S(1)} %mul.12.jh, s32[3]{0:T(128)S(1)} %pad_add_fusion.who, s32[4096]{0:T(1024)} %bitcast.35, s32[16,16]{1,0:T(8,128)} %bitcast.31, ...), custom_call_target="tpu_custom_call" | custom-call | bytes 42000000 | tf_op jit(solution)/shard_map/finish/pallas_call | solution.py:60
  60.2 12.3 %all_to_all.15.vals = f32[16,2,8,128]{3,2,1,0:T(8,128)S(1)} all-to-all(f32[16,2,8,128]{3,2,1,0:T(8,128)S(1)} %get-tuple-element.41), channel_id=1, replica_groups=mesh['comp'=16,'blk'=16] {'comp'}, dimensions={0} | all-to-all | bytes 262144 | tf_op jit(solution)/shard_map/all_to_all | solution.py:677
  72.6 10.1 %scatter_edge.1 = (f32[6,8,32,256]{3,2,1,0:T(8,128)S(1)}, f32[19,32,256]{2,1,0:T(8,128)S(1)}, f32[19,32,256]{2,1,0:T(8,128)S(1)}, f32[6,2,32,256]{3,2,1,0:T(8,128)S(1)}) custom-call(f32[6,8,32,256]{3,2,1,0:T(8,128)S(1)} %get-tuple-element.40.q, f32[16,2,8,128]{3,2,1,0:T(8,128)S(1)} %all_to_all.15.vals, s32[4096]{0:T(1024)} %bitcast.33, ...), custom_call_target="tpu_custom_call" | custom-call | bytes 36000000 | tf_op jit(solution)/shard_map/scatter_edge/pallas_call | solution.py:60
  82.7 1.9 %collective-permute-start.3 = (f32[19,32,256]{2,1,0:T(8,128)S(1)}, f32[19,32,256]{2,1,0:T(8,128)S(1)}, u32[]{:S(2)}, u32[]{:S(2)}) collective-permute-start(f32[19,32,256]{2,1,0:T(8,128)S(1)} %get-tuple-element.44.lo.own_lo), channel_id=1, source_target_pairs={{1,0},{2,1},{3,2},{4,3},{5,4},{6,5},{7,6},{8,7},{9,8},{10,9},{11,1... | collective-permute-start | bytes 1867784 | tf_op jit(solution)/shard_map/ppermute | solution.py:657
  84.7 3.4 %collective-permute-start.2 = (f32[19,32,256]{2,1,0:T(8,128)S(1)}, f32[19,32,256]{2,1,0:T(8,128)S(1)}, u32[]{:S(2)}, u32[]{:S(2)}) collective-permute-start(f32[19,32,256]{2,1,0:T(8,128)S(1)} %get-tuple-element.45.hi.own_hi), channel_id=1, source_target_pairs={{0,1},{1,2},{2,3},{3,4},{4,5},{5,6},{6,7},{7,8},{8,9},{9,10},{10,1... | collective-permute-start | bytes 1867784 | tf_op jit(solution)/shard_map/ppermute | solution.py:656
  88.0 6.4 %inner.3 = (f32[6,2,32,256]{3,2,1,0:T(8,128)S(1)}, f32[6,2,32,256]{3,2,1,0:T(8,128)S(1)}, f32[6,4,32,256]{3,2,1,0:T(8,128)S(1)}, f32[6,2,32,256]{3,2,1,0:T(8,128)S(1)}) custom-call(f32[6,8,32,256]{3,2,1,0:T(8,128)S(1)} %get-tuple-element.43.q, f32[6,8,32,256]{3,2,1,0:T(8,128)} %bitcast.17, f32[6,8,32,256]{3,2,1,0:T(8,128)} %bitcast.21, ...), custom_call_target="tpu_custom_call" | custom-call | bytes 12000000 | tf_op jit(solution)/shard_map/inner/pallas_call | solution.py:60
  94.4 6.1 %collective-permute-done.3.got_hi = f32[19,32,256]{2,1,0:T(8,128)S(1)} collective-permute-done((f32[19,32,256]{2,1,0:T(8,128)S(1)}, f32[19,32,256]{2,1,0:T(8,128)S(1)}, u32[]{:S(2)}, u32[]{:S(2)}) %collective-permute-start.3) | collective-permute-done | bytes 622624 | tf_op jit(solution)/shard_map/ppermute | solution.py:657
  100.5 4.0 %collective-permute-done.2.got_lo = f32[19,32,256]{2,1,0:T(8,128)S(1)} collective-permute-done((f32[19,32,256]{2,1,0:T(8,128)S(1)}, f32[19,32,256]{2,1,0:T(8,128)S(1)}, u32[]{:S(2)}, u32[]{:S(2)}) %collective-permute-start.2) | collective-permute-done | bytes 622624 | tf_op jit(solution)/shard_map/ppermute | solution.py:656
  104.5 13.3 %finish.3 = (f32[6,8,32,256]{3,2,1,0:T(8,128)S(1)}, f32[16,2,8,128]{3,2,1,0:T(8,128)S(1)}) custom-call(f32[6,8,32,256]{3,2,1,0:T(8,128)S(1)} %get-tuple-element.43.q, f32[8,32,256]{2,1,0:T(8,128)} %bitcast.27, f32[108]{0:T(128)S(1)} %mul.12.jh, s32[3]{0:T(128)S(1)} %pad_add_fusion.who, s32[4096]{0:T(1024)} %bitcast.36, s32[16,16]{1,0:T(8,128)} %bitcast.32, ...), custom_call_target="tpu_custom_call" | custom-call | bytes 42000000 | tf_op jit(solution)/shard_map/finish/pallas_call | solution.py:60
  117.8 12.2 %all_to_all.16.vals = f32[16,2,8,128]{3,2,1,0:T(8,128)S(1)} all-to-all(f32[16,2,8,128]{3,2,1,0:T(8,128)S(1)} %get-tuple-element.52), channel_id=1, replica_groups=mesh['comp'=16,'blk'=16] {'comp'}, dimensions={0} | all-to-all | bytes 262144 | tf_op jit(solution)/shard_map/all_to_all | solution.py:677
  130.0 8.1 %scatter.1 = f32[6,8,32,256]{3,2,1,0:T(8,128)} custom-call(f32[6,8,32,256]{3,2,1,0:T(8,128)S(1)} %get-tuple-element.51.q, f32[16,2,8,128]{3,2,1,0:T(8,128)S(1)} %all_to_all.16.vals, s32[4096]{0:T(1024)} %bitcast.34), custom_call_target="tpu_custom_call" | custom-call | bytes 30000000 | tf_op jit(solution)/shard_map/scatter/pallas_call | solution.py:60
Async XLA Ops:
  0.0 18.3 %all-to-all-start = ((f32[16,2,8,128]{3,2,1,0:T(8,128)}), f32[16,2,8,128]{3,2,1,0:T(8,128)S(1)}, u32[]{:S(2)}, u32[]{:S(2)}) async-start(f32[16,2,8,128]{3,2,1,0:T(8,128)} %bitcast.28), calls=%async_computation | async-start | bytes 262144 | tf_op jit(solution)/shard_map/all_to_all | solution.py:648
  22.3 18.6 %collective-permute-start.1 = (f32[19,32,256]{2,1,0:T(8,128)S(1)}, f32[19,32,256]{2,1,0:T(8,128)S(1)}, u32[]{:S(2)}, u32[]{:S(2)}) collective-permute-start(f32[19,32,256]{2,1,0:T(8,128)S(1)} %get-tuple-element.32.lo.own_lo), channel_id=1, source_target_pairs={{1,0},{2,1},{3,2},{4,3},{5,4},{6,5},{7,6},{8,7},{9,8},{10,9},{11,1... | collective-permute-start | bytes 1867784 | tf_op jit(solution)/shard_map/ppermute | solution.py:657
  27.2 19.7 %collective-permute-start = (f32[19,32,256]{2,1,0:T(8,128)S(1)}, f32[19,32,256]{2,1,0:T(8,128)S(1)}, u32[]{:S(2)}, u32[]{:S(2)}) collective-permute-start(f32[19,32,256]{2,1,0:T(8,128)S(1)} %get-tuple-element.33.hi.own_hi), channel_id=1, source_target_pairs={{0,1},{1,2},{2,3},{3,4},{4,5},{5,6},{6,7},{7,8},{8,9},{9,10},{10,1... | collective-permute-start | bytes 1867784 | tf_op jit(solution)/shard_map/ppermute | solution.py:656
  82.7 17.8 %collective-permute-start.3 = (f32[19,32,256]{2,1,0:T(8,128)S(1)}, f32[19,32,256]{2,1,0:T(8,128)S(1)}, u32[]{:S(2)}, u32[]{:S(2)}) collective-permute-start(f32[19,32,256]{2,1,0:T(8,128)S(1)} %get-tuple-element.44.lo.own_lo), channel_id=1, source_target_pairs={{1,0},{2,1},{3,2},{4,3},{5,4},{6,5},{7,6},{8,7},{9,8},{10,9},{11,1... | collective-permute-start | bytes 1867784 | tf_op jit(solution)/shard_map/ppermute | solution.py:657
  84.7 19.9 %collective-permute-start.2 = (f32[19,32,256]{2,1,0:T(8,128)S(1)}, f32[19,32,256]{2,1,0:T(8,128)S(1)}, u32[]{:S(2)}, u32[]{:S(2)}) collective-permute-start(f32[19,32,256]{2,1,0:T(8,128)S(1)} %get-tuple-element.45.hi.own_hi), channel_id=1, source_target_pairs={{0,1},{1,2},{2,3},{3,4},{4,5},{5,6},{6,7},{7,8},{8,9},{9,10},{10,1... | collective-permute-start | bytes 1867784 | tf_op jit(solution)/shard_map/ppermute | solution.py:656

commit v4 on v3

--- a/solution.py
+++ b/solution.py
@@ -204,7 +204,8 @@
     c.halves_out(f.at[:, 1 + (CX - 1) * side], msg.at[pl.ds(0, NV)])
     c.add(ers.at[:, outer], msg.at[pl.ds(NV, NV)])
     c.add(es1.at[:, inner], msg.at[pl.ds(2 * NV, NV)])
-    c.add(kap.at[outer], msg.at[3 * NV])
+    if msg.shape[0] > 3 * NV:
+        c.add(kap.at[outer], msg.at[3 * NV])
     c.add(ers.at[:, inner], er.at[:, side])
 
 
@@ -323,7 +324,7 @@
 
 
 def finish_body(
-    q, kap, jh, who, idx_in, pairs_in, own_lo, own_hi, got_lo, got_hi, w_in,
+    q, kap, jh, who, idx_in, pairs_in, own_lo, own_hi, got_lo, got_hi, klo, khi, w_in,
     er, rs_in, s1_in, s2_in, s3_in, qn, send,
     rse, s1e, s2e, kape, far, qb, s3, q8, tab, g, wb, idx, pairs, sem,
 ):
@@ -335,8 +336,8 @@
     for x, msg in ((0, got_lo), (1, own_lo), (8, own_hi), (9, got_hi)):
         c.add(msg.at[pl.ds(NV, NV)], rse.at[:, x])
     c.add(kap, kape.at[pl.ds(1, CX)])
-    c.add(got_lo.at[3 * NV], kape.at[0])
-    c.add(got_hi.at[3 * NV], kape.at[CX + 1])
+    c.add(klo.at[3 * NV], kape.at[0])
+    c.add(khi.at[3 * NV], kape.at[CX + 1])
     for x, msg in ((0, got_lo), (3, own_lo), (8, own_hi), (11, got_hi)):
         k.halves(msg.at[pl.ds(2 * NV, NV)], s1e.at[:, x])
     for i, (r, s) in enumerate(((2, 4), (7, 7))):
@@ -422,12 +423,10 @@
     def _(tile):
         @pl.when(tile % 2 < pairs[me, tile // 2])
         def _():
-            @pl.loop(0, LANES // 64)
-            def _(b):
-                for u in range(64):
-                    row = idx[pl.multiple_of(tile * LANES + b * 64, 64) + u]
-                    at = pl.multiple_of(tile * 256 + b * 128, 128) + 2 * u
-                    g[pl.ds(at, 2), :] = tab[pl.ds(row, 2), :]
+            for u in range(LANES):
+                row = idx[pl.multiple_of(tile * LANES, LANES) + u]
+                at = pl.multiple_of(tile * 2 * LANES, 2 * LANES) + 2 * u
+                g[pl.ds(at, 2), :] = tab[pl.ds(row, 2), :]
 
     @pl.loop(0, TILES // 8)
     def _(n):
@@ -640,21 +639,26 @@
     forward = [(i, i + 1) for i in range(count - 1)]
     backward = [(b, a) for a, b in forward]
 
-    messages = [sds((3 * NV + 1, CY, CZ))] * 2 + [rows_of(2)]
+    def messages(planes):
+        return [sds((planes, CY, CZ))] * 2 + [rows_of(2)]
+
 
     idx_shape = sds((TILES, LANES), I32)
     sems = pltpu.SemaphoreType.DMA((3,))
 
-    held = lax.all_to_all(interp_weight[0, 0], "comp", split_axis=0, concat_axis=0, tiled=True)
-    jh, held = lax.optimization_barrier((jh, held))
     lo, hi, er = call(
-        edge_body, "edge", messages, [HBM] * 3 + [SMEM], [ANY] * 3,
+        edge_body, "edge", messages(3 * NV + 1), [HBM] * 3 + [SMEM], [ANY] * 3,
         scratch=(field(CX + 2),) + EDGE_SCRATCH + (sems,), cost_us=3.0,
     )(now, prev, kap, jh)
     state = now
     for sub in range(2):
         got_lo = lax.ppermute(hi, "blk", forward)
         got_hi = lax.ppermute(lo, "blk", backward)
+        if sub == 0:
+            klo, khi = got_lo, got_hi
+            weights, lo, who = lax.optimization_barrier((interp_weight[0, 0], lo, who))
+            held = lax.all_to_all(weights, "comp", split_axis=0, concat_axis=0, tiled=True)
+            jh, held = lax.optimization_barrier((jh, held))
         inner = call(
             functools.partial(inner_body, later=sub > 0), "inner", [rows_of(n) for n in (2, 2, 4, 2)],
             [HBM if sub == 0 else ANY, HBM, HBM, HBM, SMEM, ANY, ANY], [ANY] * 4,
@@ -668,16 +672,16 @@
             didx, ridx = didx.reshape(-1), ridx.reshape(-1)
         relaxed, send = call(
             finish_body, "finish", [sds(STATE), sds((16, 2, 8, LANES))],
-            [HBM if sub == 0 else ANY, HBM, SMEM, SMEM, HBM, HBM] + [ANY] * 4 + [HBM] + [ANY] * 5,
+            [HBM if sub == 0 else ANY, HBM, SMEM, SMEM, HBM, HBM] + [ANY] * 6 + [HBM] + [ANY] * 5,
             [ANY, VMEM], scratch=FINISH_SCRATCH, vmem_mb=30, cost_us=14.0,
         )(
-            state, kap, jh, who, didx, pairs, lo, hi, got_lo, got_hi, wide,
+            state, kap, jh, who, didx, pairs, lo, hi, got_lo, got_hi, klo, khi, wide,
             er, *inner,
         )
         arrived = lax.all_to_all(send, "comp", split_axis=0, concat_axis=0, tiled=True)
         if sub == 0:
             state, lo, hi, er = call(
-                scatter_edge_body, "scatter_edge", [sds(STATE)] + messages,
+                scatter_edge_body, "scatter_edge", [sds(STATE)] + messages(3 * NV),
                 [ANY, VMEM, HBM, HBM, HBM, HBM, SMEM], [ANY] * 4,
                 scratch=SCATTER_SCRATCH + (field(CX + 2),) + EDGE_SCRATCH + (sems,),
                 vmem_mb=20, cost_us=12.0,

time: 139 us -> 135 us (0.971)
  blocking collectives: 24.5 us -> 42 us
  waiting for transfers between devices: 25.5 us -> 10.4 us
  starting transfers between devices: 21.3 us -> 14.8 us
    all_to_all x0 -> x1, blocking collectives: none -> 18.4 us  [shards(): lax.all_to_all(weights, 'comp', split_axis=0, concat_axis=0, tiled=True)]
    all_to_all x1 -> x0, starting transfers between devices: 9.15 us -> none  [shards(): lax.all_to_all(interp_weight[0, 0], 'comp', split_axis=0, concat_axis=0,...]
    all_to_all x1 -> x0, waiting for transfers between devices: 8.35 us -> none  [shards(): lax.all_to_all(interp_weight[0, 0], 'comp', split_axis=0, concat_axis=0,...]
    ppermute x2, starting transfers between devices: 6.83 us -> 11 us  [shards(): got_hi = lax.ppermute(lo, 'blk', backward)]
    ppermute x2, waiting for transfers between devices: 10.1 us -> 5.91 us  [shards(): got_lo = lax.ppermute(hi, 'blk', forward)]
    ppermute x2, waiting for transfers between devices: 7.07 us -> 4.45 us  [shards(): got_hi = lax.ppermute(lo, 'blk', backward)]
    ppermute x2, starting transfers between devices: 5.28 us -> 3.84 us  [shards(): got_lo = lax.ppermute(hi, 'blk', forward)]
  transfers between devices with their start and end apart: 5 -> 4, of which waited for: 5 -> 2; matrix products, arithmetic and copies ran while one was open for 1% -> 0% of each run, Pallas kernels for 12% -> 13%
where the time goes in v4:
time: 135 us; the launch traced here: 134 us
  Pallas kernels  65.8 us (49%)
  blocking collectives  42 us (31%)
  starting transfers between devices  14.8 us (11%)
  waiting for transfers between devices  10.4 us (8%)
    pallas_call x8, Pallas kernels, run(): kernel(*[pltpu.with_memory_space_constraint(a, pltpu.HBM) if spec is HBM...  65.8 us
    all_to_all x2, blocking collectives, shards(): lax.all_to_all(send, 'comp', split_axis=0, concat_axis=0, tiled=True)  23.6 us
    all_to_all x1, blocking collectives, shards(): lax.all_to_all(weights, 'comp', split_axis=0, concat_axis=0, tiled=True)  18.4 us
    ppermute x2, starting transfers between devices, shards(): got_hi = lax.ppermute(lo, 'blk', backward)  11 us
    ppermute x2, waiting for transfers between devices, shards(): got_lo = lax.ppermute(hi, 'blk', forward)  5.91 us
    ppermute x2, waiting for transfers between devices, shards(): got_hi = lax.ppermute(lo, 'blk', backward)  4.45 us
    ppermute x2, starting transfers between devices, shards(): got_lo = lax.ppermute(hi, 'blk', forward)  3.84 us
  transfers between devices with their start and end apart: 4, of which 2 were waited for; matrix products, arithmetic and copies ran while one was open for 0% of the time, Pallas kernels for 13%

profile of v4, /device:TPU:7, one launch (start us, length us, event | category | flops | bytes accessed | tf_op | source)
XLA Modules:
  0.0 134.0 jit_solution(11138085242029528147)
XLA Ops:
  0.0 0.7 multiply_reduce_fusion
  0.7 0.1 mul.12.jh
  0.8 0.0 copy-start
  0.8 4.0 %edge.1 = (f32[19,32,256]{2,1,0:T(8,128)S(1)}, f32[19,32,256]{2,1,0:T(8,128)S(1)}, f32[6,2,32,256]{3,2,1,0:T(8,128)S(1)}) custom-call(f32[6,8,32,256]{3,2,1,0:T(8,128)} %bitcast.12, f32[6,8,32,256]{3,2,1,0:T(8,128)} %bitcast.18, f32[8,32,256]{2,1,0:T(8,128)} %bitcast.22, f32[108]{0:T(128)S(1)} %mul.12.jh), custom_call_target="tpu_custom_call" | custom-call | bytes 9000000 | tf_op jit(solution)/shard_map/edge/pallas_call | solution.py:60
  4.8 4.9 %collective-permute-start.1 = (f32[19,32,256]{2,1,0:T(8,128)S(1)}, f32[19,32,256]{2,1,0:T(8,128)S(1)}, u32[]{:S(2)}, u32[]{:S(2)}) collective-permute-start(f32[19,32,256]{2,1,0:T(8,128)S(1)} %get-tuple-element.38.lo.own_lo), channel_id=1, source_target_pairs={{1,0},{2,1},{3,2},{4,3},{5,4},{6,5},{7,6},{8,7},{9,8},{10,9},{11,1... | collective-permute-start | bytes 1867784 | tf_op jit(solution)/shard_map/ppermute | solution.py:656
  9.8 1.9 %collective-permute-start = (f32[19,32,256]{2,1,0:T(8,128)S(1)}, f32[19,32,256]{2,1,0:T(8,128)S(1)}, u32[]{:S(2)}, u32[]{:S(2)}) collective-permute-start(f32[19,32,256]{2,1,0:T(8,128)S(1)} %get-tuple-element.39.hi.own_hi), channel_id=1, source_target_pairs={{0,1},{1,2},{2,3},{3,4},{4,5},{5,6},{6,7},{7,8},{8,9},{9,10},{10,1... | collective-permute-start | bytes 1867784 | tf_op jit(solution)/shard_map/ppermute | solution.py:655
  11.7 0.1 pad_add_fusion.who
  11.8 0.0 copy-done
  11.8 18.4 %all_to_all.15.held_in = f32[16,2,8,128]{3,2,1,0:T(8,128)S(1)} all-to-all(f32[16,2,8,128]{3,2,1,0:T(8,128)S(1)} %bitcast.28), channel_id=1, replica_groups=mesh['comp'=16,'blk'=16] {'comp'}, dimensions={0} | all-to-all | bytes 262144 | tf_op jit(solution)/shard_map/all_to_all | solution.py:660
  30.2 6.4 %inner.2 = (f32[6,2,32,256]{3,2,1,0:T(8,128)S(1)}, f32[6,2,32,256]{3,2,1,0:T(8,128)S(1)}, f32[6,4,32,256]{3,2,1,0:T(8,128)S(1)}, f32[6,2,32,256]{3,2,1,0:T(8,128)S(1)}) custom-call(f32[6,8,32,256]{3,2,1,0:T(8,128)} %bitcast.13, f32[6,8,32,256]{3,2,1,0:T(8,128)} %bitcast.14, f32[6,8,32,256]{3,2,1,0:T(8,128)} %bitcast.19, f32[8,32,256]{2,1,0:T(8,128)} %bitcast.23, ...), custom_call_target="tpu_custom_call" | custom-call | bytes 12000000 | tf_op jit(solution)/shard_map/inner/pallas_call | solution.py:60
  36.5 4.3 %setup.1 = (s32[32,128]{1,0:T(8,128)}, s32[32,128]{1,0:T(8,128)}, f32[2,4096,128]{2,1,0:T(8,128)}) custom-call(s32[16,2,8,128]{3,2,1,0:T(8,128)} %bitcast.29, s32[16,2,128]{2,1,0:T(2,128)} %bitcast.37, s32[16,16]{1,0:T(8,128)} %bitcast.30, s32[3]{0:T(128)S(1)} %pad_add_fusion.who, f32[16,2,8,128]{3,2,1,0:T(8,128)S(1)} %all_to_all.15.held_in), custom_call_target="tpu_custom_call" | custom-call | bytes 12000000 | tf_op jit(solution)/shard_map/setup/pallas_call | solution.py:60
  40.8 0.0 collective-permute-done.1.got_hi.khi
  40.8 0.0 collective-permute-done.got_lo.klo
  40.8 13.3 %finish.2 = (f32[6,8,32,256]{3,2,1,0:T(8,128)S(1)}, f32[16,2,8,128]{3,2,1,0:T(8,128)S(1)}) custom-call(f32[6,8,32,256]{3,2,1,0:T(8,128)} %bitcast.15, f32[8,32,256]{2,1,0:T(8,128)} %bitcast.24, f32[108]{0:T(128)S(1)} %mul.12.jh, s32[3]{0:T(128)S(1)} %pad_add_fusion.who, s32[4096]{0:T(1024)} %bitcast.35, s32[16,16]{1,0:T(8,128)} %bitcast.31, ...), custom_call_target="tpu_custom_call" | custom-call | bytes 42000000 | tf_op jit(solution)/shard_map/finish/pallas_call | solution.py:60
  54.1 11.2 %all_to_all.16.vals = f32[16,2,8,128]{3,2,1,0:T(8,128)S(1)} all-to-all(f32[16,2,8,128]{3,2,1,0:T(8,128)S(1)} %get-tuple-element.47), channel_id=1, replica_groups=mesh['comp'=16,'blk'=16] {'comp'}, dimensions={0} | all-to-all | bytes 262144 | tf_op jit(solution)/shard_map/all_to_all | solution.py:681
  65.3 10.0 %scatter_edge.1 = (f32[6,8,32,256]{3,2,1,0:T(8,128)S(1)}, f32[18,32,256]{2,1,0:T(8,128)S(1)}, f32[18,32,256]{2,1,0:T(8,128)S(1)}, f32[6,2,32,256]{3,2,1,0:T(8,128)S(1)}) custom-call(f32[6,8,32,256]{3,2,1,0:T(8,128)S(1)} %get-tuple-element.46.q, f32[16,2,8,128]{3,2,1,0:T(8,128)S(1)} %all_to_all.16.vals, s32[4096]{0:T(1024)} %bitcast.33, ...), custom_call_target="tpu_custom_call" | custom-call | bytes 36000000 | tf_op jit(solution)/shard_map/scatter_edge/pallas_call | solution.py:60
  75.4 6.1 %collective-permute-start.3 = (f32[18,32,256]{2,1,0:T(8,128)S(1)}, f32[18,32,256]{2,1,0:T(8,128)S(1)}, u32[]{:S(2)}, u32[]{:S(2)}) collective-permute-start(f32[18,32,256]{2,1,0:T(8,128)S(1)} %get-tuple-element.50.lo.own_lo), channel_id=1, source_target_pairs={{1,0},{2,1},{3,2},{4,3},{5,4},{6,5},{7,6},{8,7},{9,8},{10,9},{11,1... | collective-permute-start | bytes 1769480 | tf_op jit(solution)/shard_map/ppermute | solution.py:656
  81.5 1.9 %collective-permute-start.2 = (f32[18,32,256]{2,1,0:T(8,128)S(1)}, f32[18,32,256]{2,1,0:T(8,128)S(1)}, u32[]{:S(2)}, u32[]{:S(2)}) collective-permute-start(f32[18,32,256]{2,1,0:T(8,128)S(1)} %get-tuple-element.51.hi.own_hi), channel_id=1, source_target_pairs={{0,1},{1,2},{2,3},{3,4},{4,5},{5,6},{6,7},{7,8},{8,9},{9,10},{10,1... | collective-permute-start | bytes 1769480 | tf_op jit(solution)/shard_map/ppermute | solution.py:655
  83.4 6.4 %inner.3 = (f32[6,2,32,256]{3,2,1,0:T(8,128)S(1)}, f32[6,2,32,256]{3,2,1,0:T(8,128)S(1)}, f32[6,4,32,256]{3,2,1,0:T(8,128)S(1)}, f32[6,2,32,256]{3,2,1,0:T(8,128)S(1)}) custom-call(f32[6,8,32,256]{3,2,1,0:T(8,128)S(1)} %get-tuple-element.49.q, f32[6,8,32,256]{3,2,1,0:T(8,128)} %bitcast.17, f32[6,8,32,256]{3,2,1,0:T(8,128)} %bitcast.21, ...), custom_call_target="tpu_custom_call" | custom-call | bytes 12000000 | tf_op jit(solution)/shard_map/inner/pallas_call | solution.py:60
  89.8 4.4 %collective-permute-done.3.got_hi = f32[18,32,256]{2,1,0:T(8,128)S(1)} collective-permute-done((f32[18,32,256]{2,1,0:T(8,128)S(1)}, f32[18,32,256]{2,1,0:T(8,128)S(1)}, u32[]{:S(2)}, u32[]{:S(2)}) %collective-permute-start.3) | collective-permute-done | bytes 589856 | tf_op jit(solution)/shard_map/ppermute | solution.py:656
  94.2 5.9 %collective-permute-done.2.got_lo = f32[18,32,256]{2,1,0:T(8,128)S(1)} collective-permute-done((f32[18,32,256]{2,1,0:T(8,128)S(1)}, f32[18,32,256]{2,1,0:T(8,128)S(1)}, u32[]{:S(2)}, u32[]{:S(2)}) %collective-permute-start.2) | collective-permute-done | bytes 589856 | tf_op jit(solution)/shard_map/ppermute | solution.py:655
  100.1 13.3 %finish.3 = (f32[6,8,32,256]{3,2,1,0:T(8,128)S(1)}, f32[16,2,8,128]{3,2,1,0:T(8,128)S(1)}) custom-call(f32[6,8,32,256]{3,2,1,0:T(8,128)S(1)} %get-tuple-element.49.q, f32[8,32,256]{2,1,0:T(8,128)} %bitcast.27, f32[108]{0:T(128)S(1)} %mul.12.jh, s32[3]{0:T(128)S(1)} %pad_add_fusion.who, s32[4096]{0:T(1024)} %bitcast.36, s32[16,16]{1,0:T(8,128)} %bitcast.32, ...), custom_call_target="tpu_custom_call" | custom-call | bytes 42000000 | tf_op jit(solution)/shard_map/finish/pallas_call | solution.py:60
  113.5 12.5 %all_to_all.17.vals = f32[16,2,8,128]{3,2,1,0:T(8,128)S(1)} all-to-all(f32[16,2,8,128]{3,2,1,0:T(8,128)S(1)} %get-tuple-element.58), channel_id=1, replica_groups=mesh['comp'=16,'blk'=16] {'comp'}, dimensions={0} | all-to-all | bytes 262144 | tf_op jit(solution)/shard_map/all_to_all | solution.py:681
  125.9 8.1 %scatter.1 = f32[6,8,32,256]{3,2,1,0:T(8,128)} custom-call(f32[6,8,32,256]{3,2,1,0:T(8,128)S(1)} %get-tuple-element.57.q, f32[16,2,8,128]{3,2,1,0:T(8,128)S(1)} %all_to_all.17.vals, s32[4096]{0:T(1024)} %bitcast.34), custom_call_target="tpu_custom_call" | custom-call | bytes 30000000 | tf_op jit(solution)/shard_map/scatter/pallas_call | solution.py:60
Async XLA Ops:
  0.8 10.9 %copy-start = (f32[1,1,16,2,8,128]{5,4,3,2,1,0:T(8,128)S(1)}, f32[1,1,16,2,8,128]{5,4,3,2,1,0:T(8,128)}, u32[]{:S(2)}) copy-start(f32[1,1,16,2,8,128]{5,4,3,2,1,0:T(8,128)} %param.13) | copy-start | bytes 393220
  4.8 36.0 %collective-permute-start.1 = (f32[19,32,256]{2,1,0:T(8,128)S(1)}, f32[19,32,256]{2,1,0:T(8,128)S(1)}, u32[]{:S(2)}, u32[]{:S(2)}) collective-permute-start(f32[19,32,256]{2,1,0:T(8,128)S(1)} %get-tuple-element.38.lo.own_lo), channel_id=1, source_target_pairs={{1,0},{2,1},{3,2},{4,3},{5,4},{6,5},{7,6},{8,7},{9,8},{10,9},{11,1... | collective-permute-start | bytes 1867784 | tf_op jit(solution)/shard_map/ppermute | solution.py:656
  9.8 31.1 %collective-permute-start = (f32[19,32,256]{2,1,0:T(8,128)S(1)}, f32[19,32,256]{2,1,0:T(8,128)S(1)}, u32[]{:S(2)}, u32[]{:S(2)}) collective-permute-start(f32[19,32,256]{2,1,0:T(8,128)S(1)} %get-tuple-element.39.hi.own_hi), channel_id=1, source_target_pairs={{0,1},{1,2},{2,3},{3,4},{4,5},{5,6},{6,7},{7,8},{8,9},{9,10},{10,1... | collective-permute-start | bytes 1867784 | tf_op jit(solution)/shard_map/ppermute | solution.py:655
  75.4 18.9 %collective-permute-start.3 = (f32[18,32,256]{2,1,0:T(8,128)S(1)}, f32[18,32,256]{2,1,0:T(8,128)S(1)}, u32[]{:S(2)}, u32[]{:S(2)}) collective-permute-start(f32[18,32,256]{2,1,0:T(8,128)S(1)} %get-tuple-element.50.lo.own_lo), channel_id=1, source_target_pairs={{1,0},{2,1},{3,2},{4,3},{5,4},{6,5},{7,6},{8,7},{9,8},{10,9},{11,1... | collective-permute-start | bytes 1769480 | tf_op jit(solution)/shard_map/ppermute | solution.py:656
  81.5 18.7 %collective-permute-start.2 = (f32[18,32,256]{2,1,0:T(8,128)S(1)}, f32[18,32,256]{2,1,0:T(8,128)S(1)}, u32[]{:S(2)}, u32[]{:S(2)}) collective-permute-start(f32[18,32,256]{2,1,0:T(8,128)S(1)} %get-tuple-element.51.hi.own_hi), channel_id=1, source_target_pairs={{0,1},{1,2},{2,3},{3,4},{4,5},{5,6},{6,7},{7,8},{8,9},{9,10},{10,1... | collective-permute-start | bytes 1769480 | tf_op jit(solution)/shard_map/ppermute | solution.py:655

commit v5 on v4

--- a/solution.py
+++ b/solution.py
@@ -647,24 +647,24 @@
     sems = pltpu.SemaphoreType.DMA((3,))
 
     lo, hi, er = call(
-        edge_body, "edge", messages(3 * NV + 1), [HBM] * 3 + [SMEM], [ANY] * 3,
+        edge_body, "edge", messages(3 * NV + 1), [HBM] * 3 + [SMEM], [HBM] * 3,
         scratch=(field(CX + 2),) + EDGE_SCRATCH + (sems,), cost_us=3.0,
     )(now, prev, kap, jh)
     state = now
     for sub in range(2):
+        kept = HBM if sub == 0 else ANY
         got_lo = lax.ppermute(hi, "blk", forward)
         got_hi = lax.ppermute(lo, "blk", backward)
         if sub == 0:
             klo, khi = got_lo, got_hi
-            weights, lo, who = lax.optimization_barrier((interp_weight[0, 0], lo, who))
-            held = lax.all_to_all(weights, "comp", split_axis=0, concat_axis=0, tiled=True)
-            jh, held = lax.optimization_barrier((jh, held))
         inner = call(
             functools.partial(inner_body, later=sub > 0), "inner", [rows_of(n) for n in (2, 2, 4, 2)],
-            [HBM if sub == 0 else ANY, HBM, HBM, HBM, SMEM, ANY, ANY], [ANY] * 4,
+            [kept, HBM, HBM, HBM, SMEM, kept, kept], [kept] * 4,
             scratch=INNER_SCRATCH, vmem_mb=14, cost_us=4.0,
         )(state, now, prev, kap, jh, lo, hi)
         if sub == 0:
+            weights, _ = lax.optimization_barrier((interp_weight[0, 0], lo))
+            held = lax.all_to_all(weights, "comp", split_axis=0, concat_axis=0, tiled=True)
             didx, ridx, wide = call(
                 setup_body, "setup", [idx_shape] * 2 + [sds((2, POINTS, LANES))],
                 [HBM] * 3 + [SMEM, ANY], [HBM] * 3, scratch=SETUP_SCRATCH, cost_us=4.0,
@@ -672,7 +672,7 @@
             didx, ridx = didx.reshape(-1), ridx.reshape(-1)
         relaxed, send = call(
             finish_body, "finish", [sds(STATE), sds((16, 2, 8, LANES))],
-            [HBM if sub == 0 else ANY, HBM, SMEM, SMEM, HBM, HBM] + [ANY] * 6 + [HBM] + [ANY] * 5,
+            [kept, HBM, SMEM, SMEM, HBM, HBM, kept, kept, ANY, ANY, ANY, ANY, HBM] + [kept] * 5,
             [ANY, VMEM], scratch=FINISH_SCRATCH, vmem_mb=30, cost_us=14.0,
         )(
             state, kap, jh, who, didx, pairs, lo, hi, got_lo, got_hi, klo, khi, wide,

time: 135 us -> 129 us (0.956)
  blocking collectives: 42 us -> 26.2 us
  starting transfers between devices: 14.8 us -> 22.4 us
  waiting for transfers between devices: 10.4 us -> 12.9 us
    all_to_all x1 -> x0, blocking collectives: 18.4 us -> none  [shards(): lax.all_to_all(weights, 'comp', split_axis=0, concat_axis=0, tiled=True)]
    all_to_all x0 -> x1, starting transfers between devices: none -> 9.72 us  [shards(): lax.all_to_all(weights, 'comp', split_axis=0, concat_axis=0, tiled=True)]
    ppermute x2, starting transfers between devices: 11 us -> 7.39 us  [shards(): got_hi = lax.ppermute(lo, 'blk', backward)]
    all_to_all x2, blocking collectives: 23.6 us -> 26.2 us  [shards(): lax.all_to_all(send, 'comp', split_axis=0, concat_axis=0, tiled=True)]
    all_to_all x0 -> x1, waiting for transfers between devices: none -> 2.37 us  [shards(): lax.all_to_all(weights, 'comp', split_axis=0, concat_axis=0, tiled=True)]
    ppermute x2, starting transfers between devices: 3.84 us -> 5.29 us  [shards(): got_lo = lax.ppermute(hi, 'blk', forward)]
  transfers between devices with their start and end apart: 4 -> 5, of which waited for: 2 -> 3; matrix products, arithmetic and copies ran while one was open for 0% -> 0% of each run, Pallas kernels for 13% -> 14%
where the time goes in v5:
time: 129 us
  Pallas kernels  66.3 us (51%)
  blocking collectives  26.2 us (20%)
  starting transfers between devices  22.4 us (17%)
  waiting for transfers between devices  12.9 us (10%)
    pallas_call x8, Pallas kernels, run(): kernel(*[pltpu.with_memory_space_constraint(a, pltpu.HBM) if spec is HBM...  66.3 us
    all_to_all x2, blocking collectives, shards(): lax.all_to_all(send, 'comp', split_axis=0, concat_axis=0, tiled=True)  26.2 us
    all_to_all x1, starting transfers between devices, shards(): lax.all_to_all(weights, 'comp', split_axis=0, concat_axis=0, tiled=True)  9.72 us
    ppermute x2, starting transfers between devices, shards(): got_hi = lax.ppermute(lo, 'blk', backward)  7.39 us
    ppermute x2, waiting for transfers between devices, shards(): got_hi = lax.ppermute(lo, 'blk', backward)  5.41 us
    ppermute x2, starting transfers between devices, shards(): got_lo = lax.ppermute(hi, 'blk', forward)  5.29 us
    ppermute x2, waiting for transfers between devices, shards(): got_lo = lax.ppermute(hi, 'blk', forward)  5.12 us
  transfers between devices with their start and end apart: 5, of which 3 were waited for; matrix products, arithmetic and copies ran while one was open for 0% of the time, Pallas kernels for 14%

profile of v5, /device:TPU:7, one launch (start us, length us, event | category | flops | bytes accessed | tf_op | source)
XLA Modules:
  0.0 128.7 jit_solution(6067806663307818220)
XLA Ops:
  0.0 0.7 multiply_reduce_fusion
  0.7 0.1 mul.12.jh
  0.8 4.5 %edge.1 = (f32[19,32,256]{2,1,0:T(8,128)}, f32[19,32,256]{2,1,0:T(8,128)}, f32[6,2,32,256]{3,2,1,0:T(8,128)}) custom-call(f32[6,8,32,256]{3,2,1,0:T(8,128)} %bitcast.12, f32[6,8,32,256]{3,2,1,0:T(8,128)} %bitcast.18, f32[8,32,256]{2,1,0:T(8,128)} %bitcast.22, f32[108]{0:T(128)S(1)} %mul.12.jh), custom_call_target="tpu_custom_call" | custom-call | bytes 9000000 | tf_op jit(solution)/shard_map/edge/pallas_call | solution.py:60
  5.3 3.2 %collective-permute-start = (f32[19,32,256]{2,1,0:T(8,128)}, f32[19,32,256]{2,1,0:T(8,128)S(1)}, u32[]{:S(2)}, u32[]{:S(2)}) collective-permute-start(f32[19,32,256]{2,1,0:T(8,128)} %get-tuple-element.31.hi.own_hi), channel_id=1, source_target_pairs={{0,1},{1,2},{2,3},{3,4},{4,5},{5,6},{6,7},{7,8},{8,9},{9,10},{10,1... | collective-permute-start | bytes 1867784 | tf_op jit(solution)/shard_map/ppermute | solution.py:656
  8.5 4.2 %collective-permute-start.1 = (f32[19,32,256]{2,1,0:T(8,128)}, f32[19,32,256]{2,1,0:T(8,128)S(1)}, u32[]{:S(2)}, u32[]{:S(2)}) collective-permute-start(f32[19,32,256]{2,1,0:T(8,128)} %get-tuple-element.28.lo.own_lo), channel_id=1, source_target_pairs={{1,0},{2,1},{3,2},{4,3},{5,4},{6,5},{7,6},{8,7},{9,8},{10,9},{11,1... | collective-permute-start | bytes 1867784 | tf_op jit(solution)/shard_map/ppermute | solution.py:657
  12.7 9.7 %all-to-all-start = ((f32[16,2,8,128]{3,2,1,0:T(8,128)}), f32[16,2,8,128]{3,2,1,0:T(8,128)S(1)}, u32[]{:S(2)}, u32[]{:S(2)}) async-start(f32[16,2,8,128]{3,2,1,0:T(8,128)} %bitcast.7), calls=%async_computation | async-start | bytes 262144 | tf_op jit(solution)/shard_map/all_to_all | solution.py:667
  22.4 6.7 %inner.2 = (f32[6,2,32,256]{3,2,1,0:T(8,128)}, f32[6,2,32,256]{3,2,1,0:T(8,128)}, f32[6,4,32,256]{3,2,1,0:T(8,128)}, f32[6,2,32,256]{3,2,1,0:T(8,128)}) custom-call(f32[6,8,32,256]{3,2,1,0:T(8,128)} %bitcast.13, f32[6,8,32,256]{3,2,1,0:T(8,128)} %bitcast.14, f32[6,8,32,256]{3,2,1,0:T(8,128)} %bitcast.19, f32[8,32,256]{2,1,0:T(8,128)} %bitcast.23, ...), custom_call_target="tpu_custom_call" | custom-call | bytes 12000000 | tf_op jit(solution)/shard_map/inner/pallas_call | solution.py:60
  29.2 0.1 pad_add_fusion.who
  29.2 2.4 %all-to-all-done.held_in = f32[16,2,8,128]{3,2,1,0:T(8,128)S(1)} async-done(((f32[16,2,8,128]{3,2,1,0:T(8,128)}), f32[16,2,8,128]{3,2,1,0:T(8,128)S(1)}, u32[]{:S(2)}, u32[]{:S(2)}) %all-to-all-start) | async-done | bytes 131104 | tf_op jit(solution)/shard_map/all_to_all | solution.py:667
  31.6 4.3 %setup.1 = (s32[32,128]{1,0:T(8,128)}, s32[32,128]{1,0:T(8,128)}, f32[2,4096,128]{2,1,0:T(8,128)}) custom-call(s32[16,2,8,128]{3,2,1,0:T(8,128)} %bitcast.28, s32[16,2,128]{2,1,0:T(2,128)} %bitcast.36, s32[16,16]{1,0:T(8,128)} %bitcast.29, s32[3]{0:T(128)S(1)} %pad_add_fusion.who, f32[16,2,8,128]{3,2,1,0:T(8,128)S(1)} %all-to-all-done.held_in), custom_call_target="tpu_custom_call" | custom-call | bytes 12000000 | tf_op jit(solution)/shard_map/setup/pallas_call | solution.py:60
  35.9 0.0 collective-permute-done.got_lo.klo
  35.9 0.0 collective-permute-done.1.got_hi.khi
  35.9 13.2 %finish.2 = (f32[6,8,32,256]{3,2,1,0:T(8,128)S(1)}, f32[16,2,8,128]{3,2,1,0:T(8,128)S(1)}) custom-call(f32[6,8,32,256]{3,2,1,0:T(8,128)} %bitcast.15, f32[8,32,256]{2,1,0:T(8,128)} %bitcast.24, f32[108]{0:T(128)S(1)} %mul.12.jh, s32[3]{0:T(128)S(1)} %pad_add_fusion.who, s32[4096]{0:T(1024)} %bitcast.34, s32[16,16]{1,0:T(8,128)} %bitcast.30, ...), custom_call_target="tpu_custom_call" | custom-call | bytes 42000000 | tf_op jit(solution)/shard_map/finish/pallas_call | solution.py:60
  49.1 13.7 %all_to_all.15.vals = f32[16,2,8,128]{3,2,1,0:T(8,128)S(1)} all-to-all(f32[16,2,8,128]{3,2,1,0:T(8,128)S(1)} %get-tuple-element.39), channel_id=1, replica_groups=mesh['comp'=16,'blk'=16] {'comp'}, dimensions={0} | all-to-all | bytes 262144 | tf_op jit(solution)/shard_map/all_to_all | solution.py:681
  62.8 10.0 %scatter_edge.1 = (f32[6,8,32,256]{3,2,1,0:T(8,128)S(1)}, f32[18,32,256]{2,1,0:T(8,128)S(1)}, f32[18,32,256]{2,1,0:T(8,128)S(1)}, f32[6,2,32,256]{3,2,1,0:T(8,128)S(1)}) custom-call(f32[6,8,32,256]{3,2,1,0:T(8,128)S(1)} %get-tuple-element.38.q, f32[16,2,8,128]{3,2,1,0:T(8,128)S(1)} %all_to_all.15.vals, s32[4096]{0:T(1024)} %bitcast.32, ...), custom_call_target="tpu_custom_call" | custom-call | bytes 36000000 | tf_op jit(solution)/shard_map/scatter_edge/pallas_call | solution.py:60
  72.9 3.2 %collective-permute-start.3 = (f32[18,32,256]{2,1,0:T(8,128)S(1)}, f32[18,32,256]{2,1,0:T(8,128)S(1)}, u32[]{:S(2)}, u32[]{:S(2)}) collective-permute-start(f32[18,32,256]{2,1,0:T(8,128)S(1)} %get-tuple-element.42.lo.own_lo), channel_id=1, source_target_pairs={{1,0},{2,1},{3,2},{4,3},{5,4},{6,5},{7,6},{8,7},{9,8},{10,9},{11,1... | collective-permute-start | bytes 1769480 | tf_op jit(solution)/shard_map/ppermute | solution.py:657
  76.1 2.1 %collective-permute-start.2 = (f32[18,32,256]{2,1,0:T(8,128)S(1)}, f32[18,32,256]{2,1,0:T(8,128)S(1)}, u32[]{:S(2)}, u32[]{:S(2)}) collective-permute-start(f32[18,32,256]{2,1,0:T(8,128)S(1)} %get-tuple-element.43.hi.own_hi), channel_id=1, source_target_pairs={{0,1},{1,2},{2,3},{3,4},{4,5},{5,6},{6,7},{7,8},{8,9},{9,10},{10,1... | collective-permute-start | bytes 1769480 | tf_op jit(solution)/shard_map/ppermute | solution.py:656
  78.2 6.4 %inner.3 = (f32[6,2,32,256]{3,2,1,0:T(8,128)S(1)}, f32[6,2,32,256]{3,2,1,0:T(8,128)S(1)}, f32[6,4,32,256]{3,2,1,0:T(8,128)S(1)}, f32[6,2,32,256]{3,2,1,0:T(8,128)S(1)}) custom-call(f32[6,8,32,256]{3,2,1,0:T(8,128)S(1)} %get-tuple-element.41.q, f32[6,8,32,256]{3,2,1,0:T(8,128)} %bitcast.17, f32[6,8,32,256]{3,2,1,0:T(8,128)} %bitcast.21, ...), custom_call_target="tpu_custom_call" | custom-call | bytes 12000000 | tf_op jit(solution)/shard_map/inner/pallas_call | solution.py:60
  84.6 5.4 %collective-permute-done.3.got_hi = f32[18,32,256]{2,1,0:T(8,128)S(1)} collective-permute-done((f32[18,32,256]{2,1,0:T(8,128)S(1)}, f32[18,32,256]{2,1,0:T(8,128)S(1)}, u32[]{:S(2)}, u32[]{:S(2)}) %collective-permute-start.3) | collective-permute-done | bytes 589856 | tf_op jit(solution)/shard_map/ppermute | solution.py:657
  90.0 5.1 %collective-permute-done.2.got_lo = f32[18,32,256]{2,1,0:T(8,128)S(1)} collective-permute-done((f32[18,32,256]{2,1,0:T(8,128)S(1)}, f32[18,32,256]{2,1,0:T(8,128)S(1)}, u32[]{:S(2)}, u32[]{:S(2)}) %collective-permute-start.2) | collective-permute-done | bytes 589856 | tf_op jit(solution)/shard_map/ppermute | solution.py:656
  95.1 13.1 %finish.3 = (f32[6,8,32,256]{3,2,1,0:T(8,128)S(1)}, f32[16,2,8,128]{3,2,1,0:T(8,128)S(1)}) custom-call(f32[6,8,32,256]{3,2,1,0:T(8,128)S(1)} %get-tuple-element.41.q, f32[8,32,256]{2,1,0:T(8,128)} %bitcast.27, f32[108]{0:T(128)S(1)} %mul.12.jh, s32[3]{0:T(128)S(1)} %pad_add_fusion.who, s32[4096]{0:T(1024)} %bitcast.35, s32[16,16]{1,0:T(8,128)} %bitcast.31, ...), custom_call_target="tpu_custom_call" | custom-call | bytes 42000000 | tf_op jit(solution)/shard_map/finish/pallas_call | solution.py:60
  108.2 12.4 %all_to_all.16.vals = f32[16,2,8,128]{3,2,1,0:T(8,128)S(1)} all-to-all(f32[16,2,8,128]{3,2,1,0:T(8,128)S(1)} %get-tuple-element.50), channel_id=1, replica_groups=mesh['comp'=16,'blk'=16] {'comp'}, dimensions={0} | all-to-all | bytes 262144 | tf_op jit(solution)/shard_map/all_to_all | solution.py:681
  120.7 8.1 %scatter.1 = f32[6,8,32,256]{3,2,1,0:T(8,128)} custom-call(f32[6,8,32,256]{3,2,1,0:T(8,128)S(1)} %get-tuple-element.49.q, f32[16,2,8,128]{3,2,1,0:T(8,128)S(1)} %all_to_all.16.vals, s32[4096]{0:T(1024)} %bitcast.33), custom_call_target="tpu_custom_call" | custom-call | bytes 30000000 | tf_op jit(solution)/shard_map/scatter/pallas_call | solution.py:60
Async XLA Ops:
  5.3 30.6 %collective-permute-start = (f32[19,32,256]{2,1,0:T(8,128)}, f32[19,32,256]{2,1,0:T(8,128)S(1)}, u32[]{:S(2)}, u32[]{:S(2)}) collective-permute-start(f32[19,32,256]{2,1,0:T(8,128)} %get-tuple-element.31.hi.own_hi), channel_id=1, source_target_pairs={{0,1},{1,2},{2,3},{3,4},{4,5},{5,6},{6,7},{7,8},{8,9},{9,10},{10,1... | collective-permute-start | bytes 1867784 | tf_op jit(solution)/shard_map/ppermute | solution.py:656
  8.5 27.4 %collective-permute-start.1 = (f32[19,32,256]{2,1,0:T(8,128)}, f32[19,32,256]{2,1,0:T(8,128)S(1)}, u32[]{:S(2)}, u32[]{:S(2)}) collective-permute-start(f32[19,32,256]{2,1,0:T(8,128)} %get-tuple-element.28.lo.own_lo), channel_id=1, source_target_pairs={{1,0},{2,1},{3,2},{4,3},{5,4},{6,5},{7,6},{8,7},{9,8},{10,9},{11,1... | collective-permute-start | bytes 1867784 | tf_op jit(solution)/shard_map/ppermute | solution.py:657
  12.7 18.9 %all-to-all-start = ((f32[16,2,8,128]{3,2,1,0:T(8,128)}), f32[16,2,8,128]{3,2,1,0:T(8,128)S(1)}, u32[]{:S(2)}, u32[]{:S(2)}) async-start(f32[16,2,8,128]{3,2,1,0:T(8,128)} %bitcast.7), calls=%async_computation | async-start | bytes 262144 | tf_op jit(solution)/shard_map/all_to_all | solution.py:667
  72.9 17.1 %collective-permute-start.3 = (f32[18,32,256]{2,1,0:T(8,128)S(1)}, f32[18,32,256]{2,1,0:T(8,128)S(1)}, u32[]{:S(2)}, u32[]{:S(2)}) collective-permute-start(f32[18,32,256]{2,1,0:T(8,128)S(1)} %get-tuple-element.42.lo.own_lo), channel_id=1, source_target_pairs={{1,0},{2,1},{3,2},{4,3},{5,4},{6,5},{7,6},{8,7},{9,8},{10,9},{11,1... | collective-permute-start | bytes 1769480 | tf_op jit(solution)/shard_map/ppermute | solution.py:657
  76.1 19.0 %collective-permute-start.2 = (f32[18,32,256]{2,1,0:T(8,128)S(1)}, f32[18,32,256]{2,1,0:T(8,128)S(1)}, u32[]{:S(2)}, u32[]{:S(2)}) collective-permute-start(f32[18,32,256]{2,1,0:T(8,128)S(1)} %get-tuple-element.43.hi.own_hi), channel_id=1, source_target_pairs={{0,1},{1,2},{2,3},{3,4},{4,5},{5,6},{6,7},{7,8},{8,9},{9,10},{10,1... | collective-permute-start | bytes 1769480 | tf_op jit(solution)/shard_map/ppermute | solution.py:656

commit v6 on v5

--- a/solution.py
+++ b/solution.py
@@ -144,12 +144,11 @@
 
 
 def each_tile(count, row_of, body):
-    @pl.loop(0, count * (NT // 2))
-    def _(n):
-        i = n // (NT // 2)
+    @pl.loop(0, count)
+    def _(i):
         row = row_of(i)
-        for u in range(2):
-            body(i, row, 2 * (n % (NT // 2)) + u)
+        for t in range(NT):
+            body(i, row, t)
 
 
 def start_row(f, at, kap, k, now, prev, n, t, jh, emit):
@@ -529,10 +528,10 @@
 
     loads.wait()
 
-    @pl.loop(0, POINTS // 64)
+    @pl.loop(0, TILES)
     def _(b):
-        for j in range(64):
-            at = pl.multiple_of(b * 64, 64) + j
+        for j in range(LANES):
+            at = pl.multiple_of(b * LANES, LANES) + j
             word = ridx[at]
             mask = (jnp.full((1, LANES), word, I32) & 15) == lane
             pltpu.store(u.at[pl.ds(word >> 4, 1), :], vrep[pl.ds(at, 1), :], mask=mask)

time: 129 us -> 128 us (level)
  Pallas kernels: 66.3 us -> 62.5 us
  blocking collectives: 26.2 us -> 27.7 us
    pallas_call x8, Pallas kernels: 66.3 us -> 62.5 us  [run(): kernel(*[pltpu.with_memory_space_constraint(a, pltpu.HBM) if spec is HBM...]
    all_to_all x2, blocking collectives: 26.2 us -> 27.7 us  [shards(): lax.all_to_all(send, 'comp', split_axis=0, concat_axis=0, tiled=True)]
  transfers between devices with their start and end apart: 5 -> 5, of which waited for: 3 -> 3; matrix products, arithmetic and copies ran while one was open for 0% -> 0% of each run, Pallas kernels for 14% -> 13%
where the time goes in v6:
time: 128 us; the launch traced here: 127 us
  Pallas kernels  62.5 us (49%)
  blocking collectives  27.7 us (22%)
  starting transfers between devices  22.8 us (18%)
  waiting for transfers between devices  13.2 us (10%)
    pallas_call x8, Pallas kernels, run(): kernel(*[pltpu.with_memory_space_constraint(a, pltpu.HBM) if spec is HBM...  62.5 us
    all_to_all x2, blocking collectives, shards(): lax.all_to_all(send, 'comp', split_axis=0, concat_axis=0, tiled=True)  27.7 us
    all_to_all x1, starting transfers between devices, shards(): lax.all_to_all(weights, 'comp', split_axis=0, concat_axis=0, tiled=True)  9.72 us
    ppermute x2, starting transfers between devices, shards(): got_hi = lax.ppermute(lo, 'blk', backward)  7.75 us
    ppermute x2, waiting for transfers between devices, shards(): got_lo = lax.ppermute(hi, 'blk', forward)  5.48 us
    ppermute x2, starting transfers between devices, shards(): got_lo = lax.ppermute(hi, 'blk', forward)  5.31 us
    ppermute x2, waiting for transfers between devices, shards(): got_hi = lax.ppermute(lo, 'blk', backward)  5.22 us
  transfers between devices with their start and end apart: 5, of which 3 were waited for; matrix products, arithmetic and copies ran while one was open for 0% of the time, Pallas kernels for 13%

profile of v6, /device:TPU:7, one launch (start us, length us, event | category | flops | bytes accessed | tf_op | source)
XLA Modules:
  0.0 127.4 jit_solution(10696715521444425821)
XLA Ops:
  0.0 0.7 multiply_reduce_fusion
  0.7 0.1 mul.12.jh
  0.8 4.4 %edge.1 = (f32[19,32,256]{2,1,0:T(8,128)}, f32[19,32,256]{2,1,0:T(8,128)}, f32[6,2,32,256]{3,2,1,0:T(8,128)}) custom-call(f32[6,8,32,256]{3,2,1,0:T(8,128)} %bitcast.12, f32[6,8,32,256]{3,2,1,0:T(8,128)} %bitcast.18, f32[8,32,256]{2,1,0:T(8,128)} %bitcast.22, f32[108]{0:T(128)S(1)} %mul.12.jh), custom_call_target="tpu_custom_call" | custom-call | bytes 9000000 | tf_op jit(solution)/shard_map/edge/pallas_call | solution.py:60
  5.2 3.2 %collective-permute-start = (f32[19,32,256]{2,1,0:T(8,128)}, f32[19,32,256]{2,1,0:T(8,128)S(1)}, u32[]{:S(2)}, u32[]{:S(2)}) collective-permute-start(f32[19,32,256]{2,1,0:T(8,128)} %get-tuple-element.31.hi.own_hi), channel_id=1, source_target_pairs={{0,1},{1,2},{2,3},{3,4},{4,5},{5,6},{6,7},{7,8},{8,9},{9,10},{10,1... | collective-permute-start | bytes 1867784 | tf_op jit(solution)/shard_map/ppermute | solution.py:655
  8.4 4.2 %collective-permute-start.1 = (f32[19,32,256]{2,1,0:T(8,128)}, f32[19,32,256]{2,1,0:T(8,128)S(1)}, u32[]{:S(2)}, u32[]{:S(2)}) collective-permute-start(f32[19,32,256]{2,1,0:T(8,128)} %get-tuple-element.28.lo.own_lo), channel_id=1, source_target_pairs={{1,0},{2,1},{3,2},{4,3},{5,4},{6,5},{7,6},{8,7},{9,8},{10,9},{11,1... | collective-permute-start | bytes 1867784 | tf_op jit(solution)/shard_map/ppermute | solution.py:656
  12.6 9.7 %all-to-all-start = ((f32[16,2,8,128]{3,2,1,0:T(8,128)}), f32[16,2,8,128]{3,2,1,0:T(8,128)S(1)}, u32[]{:S(2)}, u32[]{:S(2)}) async-start(f32[16,2,8,128]{3,2,1,0:T(8,128)} %bitcast.7), calls=%async_computation | async-start | bytes 262144 | tf_op jit(solution)/shard_map/all_to_all | solution.py:666
  22.4 6.6 %inner.2 = (f32[6,2,32,256]{3,2,1,0:T(8,128)}, f32[6,2,32,256]{3,2,1,0:T(8,128)}, f32[6,4,32,256]{3,2,1,0:T(8,128)}, f32[6,2,32,256]{3,2,1,0:T(8,128)}) custom-call(f32[6,8,32,256]{3,2,1,0:T(8,128)} %bitcast.13, f32[6,8,32,256]{3,2,1,0:T(8,128)} %bitcast.14, f32[6,8,32,256]{3,2,1,0:T(8,128)} %bitcast.19, f32[8,32,256]{2,1,0:T(8,128)} %bitcast.23, ...), custom_call_target="tpu_custom_call" | custom-call | bytes 12000000 | tf_op jit(solution)/shard_map/inner/pallas_call | solution.py:60
  28.9 0.1 pad_add_fusion.who
  29.0 2.5 %all-to-all-done.held_in = f32[16,2,8,128]{3,2,1,0:T(8,128)S(1)} async-done(((f32[16,2,8,128]{3,2,1,0:T(8,128)}), f32[16,2,8,128]{3,2,1,0:T(8,128)S(1)}, u32[]{:S(2)}, u32[]{:S(2)}) %all-to-all-start) | async-done | bytes 131104 | tf_op jit(solution)/shard_map/all_to_all | solution.py:666
  31.5 4.3 %setup.1 = (s32[32,128]{1,0:T(8,128)}, s32[32,128]{1,0:T(8,128)}, f32[2,4096,128]{2,1,0:T(8,128)}) custom-call(s32[16,2,8,128]{3,2,1,0:T(8,128)} %bitcast.28, s32[16,2,128]{2,1,0:T(2,128)} %bitcast.36, s32[16,16]{1,0:T(8,128)} %bitcast.29, s32[3]{0:T(128)S(1)} %pad_add_fusion.who, f32[16,2,8,128]{3,2,1,0:T(8,128)S(1)} %all-to-all-done.held_in), custom_call_target="tpu_custom_call" | custom-call | bytes 12000000 | tf_op jit(solution)/shard_map/setup/pallas_call | solution.py:60
  35.8 0.0 collective-permute-done.got_lo.klo
  35.8 0.0 collective-permute-done.1.got_hi.khi
  35.9 11.7 %finish.2 = (f32[6,8,32,256]{3,2,1,0:T(8,128)S(1)}, f32[16,2,8,128]{3,2,1,0:T(8,128)S(1)}) custom-call(f32[6,8,32,256]{3,2,1,0:T(8,128)} %bitcast.15, f32[8,32,256]{2,1,0:T(8,128)} %bitcast.24, f32[108]{0:T(128)S(1)} %mul.12.jh, s32[3]{0:T(128)S(1)} %pad_add_fusion.who, s32[4096]{0:T(1024)} %bitcast.34, s32[16,16]{1,0:T(8,128)} %bitcast.30, ...), custom_call_target="tpu_custom_call" | custom-call | bytes 42000000 | tf_op jit(solution)/shard_map/finish/pallas_call | solution.py:60
  47.5 14.1 %all_to_all.15.vals = f32[16,2,8,128]{3,2,1,0:T(8,128)S(1)} all-to-all(f32[16,2,8,128]{3,2,1,0:T(8,128)S(1)} %get-tuple-element.39), channel_id=1, replica_groups=mesh['comp'=16,'blk'=16] {'comp'}, dimensions={0} | all-to-all | bytes 262144 | tf_op jit(solution)/shard_map/all_to_all | solution.py:680
  61.6 9.8 %scatter_edge.1 = (f32[6,8,32,256]{3,2,1,0:T(8,128)S(1)}, f32[18,32,256]{2,1,0:T(8,128)S(1)}, f32[18,32,256]{2,1,0:T(8,128)S(1)}, f32[6,2,32,256]{3,2,1,0:T(8,128)S(1)}) custom-call(f32[6,8,32,256]{3,2,1,0:T(8,128)S(1)} %get-tuple-element.38.q, f32[16,2,8,128]{3,2,1,0:T(8,128)S(1)} %all_to_all.15.vals, s32[4096]{0:T(1024)} %bitcast.32, ...), custom_call_target="tpu_custom_call" | custom-call | bytes 36000000 | tf_op jit(solution)/shard_map/scatter_edge/pallas_call | solution.py:60
  71.5 3.6 %collective-permute-start.3 = (f32[18,32,256]{2,1,0:T(8,128)S(1)}, f32[18,32,256]{2,1,0:T(8,128)S(1)}, u32[]{:S(2)}, u32[]{:S(2)}) collective-permute-start(f32[18,32,256]{2,1,0:T(8,128)S(1)} %get-tuple-element.42.lo.own_lo), channel_id=1, source_target_pairs={{1,0},{2,1},{3,2},{4,3},{5,4},{6,5},{7,6},{8,7},{9,8},{10,9},{11,1... | collective-permute-start | bytes 1769480 | tf_op jit(solution)/shard_map/ppermute | solution.py:656
  75.0 2.1 %collective-permute-start.2 = (f32[18,32,256]{2,1,0:T(8,128)S(1)}, f32[18,32,256]{2,1,0:T(8,128)S(1)}, u32[]{:S(2)}, u32[]{:S(2)}) collective-permute-start(f32[18,32,256]{2,1,0:T(8,128)S(1)} %get-tuple-element.43.hi.own_hi), channel_id=1, source_target_pairs={{0,1},{1,2},{2,3},{3,4},{4,5},{5,6},{6,7},{7,8},{8,9},{9,10},{10,1... | collective-permute-start | bytes 1769480 | tf_op jit(solution)/shard_map/ppermute | solution.py:655
  77.1 6.2 %inner.3 = (f32[6,2,32,256]{3,2,1,0:T(8,128)S(1)}, f32[6,2,32,256]{3,2,1,0:T(8,128)S(1)}, f32[6,4,32,256]{3,2,1,0:T(8,128)S(1)}, f32[6,2,32,256]{3,2,1,0:T(8,128)S(1)}) custom-call(f32[6,8,32,256]{3,2,1,0:T(8,128)S(1)} %get-tuple-element.41.q, f32[6,8,32,256]{3,2,1,0:T(8,128)} %bitcast.17, f32[6,8,32,256]{3,2,1,0:T(8,128)} %bitcast.21, ...), custom_call_target="tpu_custom_call" | custom-call | bytes 12000000 | tf_op jit(solution)/shard_map/inner/pallas_call | solution.py:60
  83.3 5.2 %collective-permute-done.3.got_hi = f32[18,32,256]{2,1,0:T(8,128)S(1)} collective-permute-done((f32[18,32,256]{2,1,0:T(8,128)S(1)}, f32[18,32,256]{2,1,0:T(8,128)S(1)}, u32[]{:S(2)}, u32[]{:S(2)}) %collective-permute-start.3) | collective-permute-done | bytes 589856 | tf_op jit(solution)/shard_map/ppermute | solution.py:656
  88.6 5.5 %collective-permute-done.2.got_lo = f32[18,32,256]{2,1,0:T(8,128)S(1)} collective-permute-done((f32[18,32,256]{2,1,0:T(8,128)S(1)}, f32[18,32,256]{2,1,0:T(8,128)S(1)}, u32[]{:S(2)}, u32[]{:S(2)}) %collective-permute-start.2) | collective-permute-done | bytes 589856 | tf_op jit(solution)/shard_map/ppermute | solution.py:655
  94.0 11.6 %finish.3 = (f32[6,8,32,256]{3,2,1,0:T(8,128)S(1)}, f32[16,2,8,128]{3,2,1,0:T(8,128)S(1)}) custom-call(f32[6,8,32,256]{3,2,1,0:T(8,128)S(1)} %get-tuple-element.41.q, f32[8,32,256]{2,1,0:T(8,128)} %bitcast.27, f32[108]{0:T(128)S(1)} %mul.12.jh, s32[3]{0:T(128)S(1)} %pad_add_fusion.who, s32[4096]{0:T(1024)} %bitcast.35, s32[16,16]{1,0:T(8,128)} %bitcast.31, ...), custom_call_target="tpu_custom_call" | custom-call | bytes 42000000 | tf_op jit(solution)/shard_map/finish/pallas_call | solution.py:60
  105.7 13.7 %all_to_all.16.vals = f32[16,2,8,128]{3,2,1,0:T(8,128)S(1)} all-to-all(f32[16,2,8,128]{3,2,1,0:T(8,128)S(1)} %get-tuple-element.50), channel_id=1, replica_groups=mesh['comp'=16,'blk'=16] {'comp'}, dimensions={0} | all-to-all | bytes 262144 | tf_op jit(solution)/shard_map/all_to_all | solution.py:680
  119.3 7.9 %scatter.1 = f32[6,8,32,256]{3,2,1,0:T(8,128)} custom-call(f32[6,8,32,256]{3,2,1,0:T(8,128)S(1)} %get-tuple-element.49.q, f32[16,2,8,128]{3,2,1,0:T(8,128)S(1)} %all_to_all.16.vals, s32[4096]{0:T(1024)} %bitcast.33), custom_call_target="tpu_custom_call" | custom-call | bytes 30000000 | tf_op jit(solution)/shard_map/scatter/pallas_call | solution.py:60
Async XLA Ops:
  5.2 30.6 %collective-permute-start = (f32[19,32,256]{2,1,0:T(8,128)}, f32[19,32,256]{2,1,0:T(8,128)S(1)}, u32[]{:S(2)}, u32[]{:S(2)}) collective-permute-start(f32[19,32,256]{2,1,0:T(8,128)} %get-tuple-element.31.hi.own_hi), channel_id=1, source_target_pairs={{0,1},{1,2},{2,3},{3,4},{4,5},{5,6},{6,7},{7,8},{8,9},{9,10},{10,1... | collective-permute-start | bytes 1867784 | tf_op jit(solution)/shard_map/ppermute | solution.py:655
  8.4 27.4 %collective-permute-start.1 = (f32[19,32,256]{2,1,0:T(8,128)}, f32[19,32,256]{2,1,0:T(8,128)S(1)}, u32[]{:S(2)}, u32[]{:S(2)}) collective-permute-start(f32[19,32,256]{2,1,0:T(8,128)} %get-tuple-element.28.lo.own_lo), channel_id=1, source_target_pairs={{1,0},{2,1},{3,2},{4,3},{5,4},{6,5},{7,6},{8,7},{9,8},{10,9},{11,1... | collective-permute-start | bytes 1867784 | tf_op jit(solution)/shard_map/ppermute | solution.py:656
  12.6 18.9 %all-to-all-start = ((f32[16,2,8,128]{3,2,1,0:T(8,128)}), f32[16,2,8,128]{3,2,1,0:T(8,128)S(1)}, u32[]{:S(2)}, u32[]{:S(2)}) async-start(f32[16,2,8,128]{3,2,1,0:T(8,128)} %bitcast.7), calls=%async_computation | async-start | bytes 262144 | tf_op jit(solution)/shard_map/all_to_all | solution.py:666
  71.5 17.1 %collective-permute-start.3 = (f32[18,32,256]{2,1,0:T(8,128)S(1)}, f32[18,32,256]{2,1,0:T(8,128)S(1)}, u32[]{:S(2)}, u32[]{:S(2)}) collective-permute-start(f32[18,32,256]{2,1,0:T(8,128)S(1)} %get-tuple-element.42.lo.own_lo), channel_id=1, source_target_pairs={{1,0},{2,1},{3,2},{4,3},{5,4},{6,5},{7,6},{8,7},{9,8},{10,9},{11,1... | collective-permute-start | bytes 1769480 | tf_op jit(solution)/shard_map/ppermute | solution.py:656
  75.0 19.0 %collective-permute-start.2 = (f32[18,32,256]{2,1,0:T(8,128)S(1)}, f32[18,32,256]{2,1,0:T(8,128)S(1)}, u32[]{:S(2)}, u32[]{:S(2)}) collective-permute-start(f32[18,32,256]{2,1,0:T(8,128)S(1)} %get-tuple-element.43.hi.own_hi), channel_id=1, source_target_pairs={{0,1},{1,2},{2,3},{3,4},{4,5},{5,6},{6,7},{7,8},{8,9},{9,10},{10,1... | collective-permute-start | bytes 1769480 | tf_op jit(solution)/shard_map/ppermute | solution.py:655
